TPU v7x, 32 devices: a whole 2x2x4 slice. The times are simulated.
32 devices in a mesh: seq: 16 (over z, y, x), head: 2 (over core).
Axes of the slice: x: 2, y: 2, z: 4, core: 2. Of those that a mesh axis runs over, the one named last changes fastest.
Arguments:
- queries: bfloat16 [2048, 2048], P('seq', 'head'), may hold values from -144 to 144
- keys: bfloat16 [2048, 2048], P('seq', 'head'), may hold values from -4 to 4
- values: bfloat16 [2048, 2048], P('seq', 'head'), may hold values from -6 to 6
- grad_out: bfloat16 [2048, 2048], P('seq', 'head'), may hold values from -6 to 6
- bias_table: float32 [32, 128], P('head'), may hold values from -5 to 5
- bucket_ids: int32 [16, 4, 256], P('seq'), may hold values from 0 to 127
- block_mask: int32 [16, 4], P('seq'), may hold values 0 or 1
Outputs:
- grad_queries: bfloat16 [2048, 2048], P('seq', 'head')
- grad_keys: bfloat16 [2048, 2048], P('seq', 'head')
- grad_values: bfloat16 [2048, 2048], P('seq', 'head')
- grad_bias: float32 [32, 128], replicated
All inputs are finite; a program needn't handle non-finite values. No bound on the sum of `block_mask` on one device may be relied on, other than what follows from the above.
Results may differ from a plain program's by a relative error of at most 0.005.
Values may be sent and summed in bfloat16 or wider, within the bound.
No kernel may reach another device: no remote copies, remote signals or barrier semaphores. Data moves between devices by JAX's collectives and lax.ppermute only.
A program may use at most 64 MiB of HBM per device.

v0:
```python
import math

import jax
import jax.numpy as jnp
from jax import lax
from jax.experimental import pallas as pl
from jax.experimental.pallas import tpu as pltpu
from jax.sharding import PartitionSpec as P


F32 = jnp.float32
BF16 = jnp.bfloat16
NEG = -1e30
NT = (((1,), (1,)), ((), ()))
NN = (((1,), (0,)), ((), ()))
CODE_ROWS = 16
VMEM_BYTES = 67043328


def dot(a, b, dims):
    return lax.dot_general(a, b, dims, preferred_element_type=F32)


def at(start, size):
    return pl.ds(pl.multiple_of(start, size), size)


def call(kernel, outs, args, scratch=(), spaces=None, out_space=pltpu.VMEM, flops=0, limit=16 << 20):
    spaces = spaces or [pltpu.VMEM] * len(args)
    moved = sum(a.size * a.dtype.itemsize for a in args)
    args = [
        pltpu.with_memory_space_constraint(a, s) if s == pltpu.VMEM else a for a, s in zip(args, spaces, strict=True)
    ]
    return pl.pallas_call(
        kernel,
        out_shape=tuple(out_space(s, d) for s, d in outs),
        in_specs=[pl.BlockSpec(memory_space=s) for s in spaces],
        out_specs=tuple(pl.BlockSpec(memory_space=out_space) for _ in outs),
        scratch_shapes=list(scratch),
        compiler_params=pltpu.CompilerParams(vmem_limit_bytes=limit),
        cost_estimate=pl.CostEstimate(flops=flops, bytes_accessed=moved, transcendentals=0),
    )(*args)


class Sizes:
    def __init__(self, tok, width, heads, span, buckets, group):
        self.tok, self.width, self.heads, self.span, self.buckets = tok, width, heads, span, buckets
        self.group = group
        self.hd = width // heads
        self.hg = heads // group
        self.cw = self.hg * self.hd
        self.pairs = self.hg // 2
        self.scale = self.hd ** (-0.5)
        self.halo = span - 1
        self.wide = 2 * tok
        self.rows = 2 * tok + CODE_ROWS
        self.near = [(i, s) for i in range(group) for s in range(span) if s <= i]
        self.far = [(i, s) for i in range(group) for s in range(span) if s > i]
        assert heads % group == 0 and self.hg % 2 == 0 and 2 * self.hd == 128
        assert tok == 128 and buckets == 128 and group >= self.halo and self.hg <= 8
        assert math.frexp(self.scale)[0] == 0.5

    def me(self):
        return lax.rem(lax.axis_index("seq"), self.group)


def pack_kernel(z, q, k, v, d, ids, mask, *refs):
    kv, qd = refs[: z.group], refs[z.group : 2 * z.group]
    slots, flags, sem = refs[2 * z.group :]
    index = lax.axis_index("seq")
    me = z.me()
    copies = [
        pltpu.make_async_copy(ids.at[0], slots, sem.at[0]),
        pltpu.make_async_copy(mask, flags, sem.at[1]),
    ]
    for sources, dst in (((k, v), kv), ((q, d), qd)):
        for g in range(z.group):
            cols = at((me ^ g) * z.cw, z.cw)
            for n, src in enumerate(sources):
                rows = pl.ds(n * z.tok, z.tok)
                copies.append(pltpu.make_async_copy(src.at[:, cols], dst[g].at[rows, :], sem.at[len(copies)]))
    for copy in copies:
        copy.start()
    for copy in copies[:2]:
        copy.wait()
    rows = []
    for s in range(z.span):
        valid = True if s == 0 else (flags[0, s] == 1) & (index >= s)
        rows.append(jnp.where(valid, slots[s : s + 1, :] + 1, 0))
    rows.append(jnp.zeros((CODE_ROWS - z.span, z.wide), jnp.int32))
    codes = jnp.concatenate(rows, axis=0).astype(F32).astype(BF16)
    for g in range(z.group):
        kv[g][2 * z.tok :, :] = codes
    for copy in copies[2:]:
        copy.wait()


def kv_halo_kernel(z, *refs):
    out = refs[-1]
    me = z.me()
    first = z.group - z.halo
    for k in range(z.group):
        j = me ^ k

        @pl.when(j >= first)
        def _():
            out[at((j - first) * 2 * z.tok, 2 * z.tok), :] = refs[k][0 : 2 * z.tok, :]


def qd_halo_kernel(z, *refs):
    qd, kv, out = refs[: z.group], refs[z.group : -1], refs[-1]
    me = z.me()
    for k in range(z.group):
        j = me ^ k

        @pl.when(j < z.halo)
        def _():
            top = pl.multiple_of(j * z.rows, 16)
            out[pl.ds(top, 2 * z.tok), :] = qd[k][...]
            out[pl.ds(top + 2 * z.tok, CODE_ROWS), :] = kv[k][2 * z.tok :, :]


def onehot_of(codes, z):
    slots = lax.broadcasted_iota(jnp.int32, (z.buckets, codes.shape[1]), 0) + 1
    return jnp.where(codes.astype(jnp.int32) == slots, 1.0, 0.0).astype(BF16)


def thirds(x):
    hi = x.astype(BF16)
    rest = x - hi.astype(F32)
    mid = rest.astype(BF16)
    low = (rest - mid.astype(F32)).astype(BF16)
    return jnp.concatenate([hi.astype(F32), mid.astype(F32), low.astype(F32)], axis=0).astype(BF16)


def by_offset(split, codes, z):
    got = dot(split, onehot_of(codes, z), NN)
    return got[0:8] + got[8:16] + got[16:24] + jnp.where(codes == 0.0, NEG, 0.0)


def masked_pair(x, z):
    lane = lax.broadcasted_iota(jnp.int32, x.shape, 1)
    zero = jnp.zeros_like(x)
    return jnp.concatenate([jnp.where(lane < z.hd, x, zero), jnp.where(lane < z.hd, zero, x)], axis=0)


def toeplitz(row, z):
    base = pltpu.roll(jnp.broadcast_to(row, (8, z.wide)), z.tok + 1, 1, stride=1, stride_axis=0)
    tiles = [pltpu.roll(base, 8 * g, 1)[:, : z.tok] if g else base[:, : z.tok] for g in range(z.tok // 8)]
    return jnp.concatenate(tiles, axis=0)


def diagonals(x, z):
    tok = z.tok
    lane = lax.broadcasted_iota(jnp.int32, (8, tok), 1)
    total = x[tok - 8 :]
    high = jnp.zeros((8, tok), F32)
    for g in range(tok // 8 - 1):
        by = tok - 8 - 8 * g
        part = pltpu.roll(x[8 * g : 8 * g + 8], by, 1)
        total = total + part
        high = high + jnp.where(lane < by, part, 0.0)
    return total - high, high


def aligned(both):
    left = 7 - (lax.broadcasted_iota(jnp.int32, both.shape, 0) & 7)
    for bit in (1, 2, 4):
        both = jnp.where((left & bit) != 0, pltpu.roll(both, bit, 1), both)
    return both


def causal(z):
    row = lax.broadcasted_iota(jnp.int32, (z.tok, z.wide), 0)
    col = lax.broadcasted_iota(jnp.int32, (z.tok, z.wide), 1) % z.tok
    return row <= col


def folded(x, how):
    return how(how(x.reshape(x.shape[0] // 8, 8, x.shape[1]), 0), 0, keepdims=True)


def bias_rows(z, boff, base, pair):
    rows = [toeplitz(boff[pl.ds(base + 2 * pair + e, 1), :], z) for e in range(2)]
    return jnp.concatenate(rows, axis=1)


def bias_kernel(z, *refs):
    kv, table = refs[: z.group], refs[z.group]
    keys, values, near, far, codes, boff = refs[z.group + 1 :]
    tok = z.tok
    me = z.me()
    for k in range(z.group):
        j = me ^ k
        keys[at(j * tok, tok), :] = kv[k][0:tok, :]
        values[at(j * tok, tok), :] = kv[k][tok : 2 * tok, :]
        codes[at(j * CODE_ROWS, CODE_ROWS), :] = kv[k][2 * tok :, :].astype(F32)
    split = thirds(table[...])
    for i in range(z.group):
        for s in range(z.span):
            row = codes[i * CODE_ROWS + s : i * CODE_ROWS + s + 1, :]
            boff[(i * z.span + s) * 8 : (i * z.span + s) * 8 + 8, :] = by_offset(split, row, z)

    def each(pair, _):
        for tiles, out in ((z.near, near), (z.far, far)):
            for t, (i, s) in enumerate(tiles):
                bias = bias_rows(z, boff, (i * z.span + s) * 8, pair)
                out[t * z.pairs + pair] = jnp.where(causal(z), bias, NEG) if s == 0 else bias
        return 0

    lax.fori_loop(0, z.pairs, each, 0)


def forward_tile(key, value, q, d, bias, row, outs):
    weights, dprobs, tops, totals, accums = outs
    scores = dot(key, q, NT) + bias[row]
    top = folded(scores, jnp.max)
    w = jnp.exp(scores - top)
    dprob = dot(value, d, NT)
    weights[row] = w
    dprobs[row] = dprob
    tops[pl.ds(row, 1), :] = top
    totals[pl.ds(row, 1), :] = folded(w, jnp.sum)
    accums[pl.ds(row, 1), :] = folded(w * dprob, jnp.sum)


def near_kernel(z, *refs):
    qd, keys, values, bias = refs[: z.group], *refs[z.group : z.group + 3]
    qm, dom, *outs = refs[z.group + 3 :]
    tok = z.tok
    me = z.me()
    for k in range(z.group):
        j = me ^ k
        for pair in range(z.pairs):
            lanes = slice(pair * 128, (pair + 1) * 128)
            rows = at(j * z.wide, z.wide)
            qm[pair, rows, :] = masked_pair(qd[k][0:tok, lanes] * jnp.asarray(z.scale, BF16), z)
            dom[pair, rows, :] = masked_pair(qd[k][tok : 2 * tok, lanes], z)

    def each(pair, _):
        lanes = at(pair * 128, 128)
        for t, (i, s) in enumerate(z.near):
            rows = slice((i - s) * tok, (i - s + 1) * tok)
            wide = slice(i * z.wide, (i + 1) * z.wide)
            forward_tile(
                keys[rows, lanes], values[rows, lanes], qm[pair, wide, :], dom[pair, wide, :],
                bias, t * z.pairs + pair, outs,
            )
        return 0

    lax.fori_loop(0, z.pairs, each, 0)


def far_kernel(z, halo, qm, dom, bias, tops, totals, accums, stats, fnear, ffar, *outs):
    tok = z.tok

    def each(pair, _):
        lanes = at(pair * 128, 128)
        for t, (i, s) in enumerate(z.far):
            b = z.halo + i - s
            wide = slice(i * z.wide, (i + 1) * z.wide)
            forward_tile(
                halo[2 * b * tok : (2 * b + 1) * tok, lanes], halo[(2 * b + 1) * tok : (2 * b + 2) * tok, lanes],
                qm[pair, wide, :], dom[pair, wide, :], bias, t * z.pairs + pair, outs,
            )
        for i in range(z.group):
            mine = [(tops, totals, accums, fnear, t) for t, (n, _) in enumerate(z.near) if n == i]
            mine += [(outs[2], outs[3], outs[4], ffar, t) for t, (n, _) in enumerate(z.far) if n == i]
            rows = [pl.ds(t * z.pairs + pair, 1) for *_, t in mine]
            peaks = [m[0][row, :] for m, row in zip(mine, rows, strict=True)]
            top = peaks[0]
            for peak in peaks[1:]:
                top = jnp.maximum(top, peak)
            total = jnp.zeros_like(top)
            accum = jnp.zeros_like(top)
            for m, row, peak in zip(mine, rows, peaks, strict=True):
                share = jnp.exp(peak - top)
                total = total + share * m[1][row, :]
                accum = accum + share * m[2][row, :]
            lse = top + jnp.log(total)
            for m, row, peak in zip(mine, rows, peaks, strict=True):
                m[3][row, :] = jnp.exp(peak - lse)
            stats[0, pl.ds(i * z.pairs + pair, 1), :] = lse
            stats[1, pl.ds(i * z.pairs + pair, 1), :] = accum / total
        return 0

    lax.fori_loop(0, z.pairs, each, 0)


def own_kernel(z, keys, halo, codes, stats, fnear, ffar, wnear, dnear, wfar, dfar, *refs):
    p16, s16, dq, gb, offs = refs
    tok, span = z.tok, z.span

    def each(pair, _):
        lanes = at(pair * 128, 128)
        blocks = [halo[2 * b * tok : (2 * b + 1) * tok, lanes] for b in range(z.halo)]
        blocks += [keys[j * tok : (j + 1) * tok, lanes] for j in range(z.group)]
        turned = jnp.concatenate([block.T for block in blocks], axis=1)
        for i in range(z.group):
            wide = slice(i * z.wide, (i + 1) * z.wide)
            delta = stats[1, pl.ds(i * z.pairs + pair, 1), :]
            parts = []
            for s in reversed(range(span)):
                close = s <= i
                t = (z.near if close else z.far).index((i, s)) * z.pairs + pair
                w, d, f = (wnear, dnear, fnear) if close else (wfar, dfar, ffar)
                prob = w[t] * f[pl.ds(t, 1), :]
                dscore = prob * (d[t] - delta)
                half = dscore.astype(BF16)
                parts.append(half)
                if close:
                    rows = slice((i - s) * tok, (i - s + 1) * tok)
                    p16[pair, rows, wide] = prob.astype(BF16)
                    s16[pair, rows, wide] = half
                for e in range(2):
                    low, high = diagonals(dscore[:, e * tok : (e + 1) * tok], z)
                    row = at(((i * span + s) * z.hg + 2 * pair + e) * 8, 8)
                    offs[row, 0:tok] = low
                    offs[row, tok:] = high
            cross = dot(turned[:, i * tok : (i + span) * tok], jnp.concatenate(parts, axis=0), NN)
            both = jnp.concatenate([cross[0 : z.hd, 0:tok], cross[z.hd :, tok:]], axis=0)
            dq[i * tok : (i + 1) * tok, lanes] = (z.scale * both.T).astype(BF16)
        return 0

    lax.fori_loop(0, z.pairs, each, 0)
    head = lax.broadcasted_iota(jnp.int32, (8, z.wide), 0)

    def bucket(n, total):
        i, s = n // span, n % span
        both = aligned(offs[at(n * z.hg * 8, z.hg * 8), :])
        sums = jnp.zeros((8, z.wide), F32)
        for h in range(z.hg):
            sums = sums + jnp.where(head == h, both[8 * h : 8 * h + 8].sum(axis=0, keepdims=True), 0.0)
        got = dot(thirds(sums), onehot_of(codes[pl.ds(i * CODE_ROWS + s, 1), :], z), NT)
        return total + (got[0:8] + got[8:16] + got[16:24])

    gb[...] = lax.fori_loop(0, z.group * span, bucket, jnp.zeros((8, z.buckets), F32))


def tail_kernel(z, keys, values, qm, dom, p16, s16, halo, stats, table, dk, dv, qh, dh, ph, sh, boff):
    tok, span = z.tok, z.span
    split = thirds(table[...])
    for b in range(z.halo):
        codes = halo[b * z.rows + 2 * tok : (b + 1) * z.rows, :].astype(F32)
        for s in range(b + 1, span):
            boff[(b * span + s) * 8 : (b * span + s) * 8 + 8, :] = by_offset(split, codes[s : s + 1, :], z)

    def each(pair, _):
        lanes = at(pair * 128, 128)
        for b in range(z.halo):
            top = b * z.rows
            wide = slice(b * z.wide, (b + 1) * z.wide)
            q = masked_pair(halo[top : top + tok, lanes] * jnp.asarray(z.scale, BF16), z)
            d = masked_pair(halo[top + tok : top + 2 * tok, lanes], z)
            qh[wide, :] = q
            dh[wide, :] = d
            u = b * z.pairs + pair
            lse, delta = stats[0, pl.ds(u, 1), :], stats[1, pl.ds(u, 1), :]
            for s in range(b + 1, span):
                j = z.group + b - s
                rows = slice(j * tok, (j + 1) * tok)
                scores = dot(keys[rows, lanes], q, NT) + bias_rows(z, boff, (b * span + s) * 8, pair)
                prob = jnp.exp(scores - lse)
                dscore = prob * (dot(values[rows, lanes], d, NT) - delta)
                ph[rows, wide] = prob.astype(BF16)
                sh[rows, wide] = dscore.astype(BF16)
        for j in range(z.group):
            rows = slice(j * tok, (j + 1) * tok)
            near = slice(j * z.wide, z.group * z.wide)
            gk = dot(s16[pair, rows, near], qm[pair, near, :], NN)
            gv = dot(p16[pair, rows, near], dom[pair, near, :], NN)
            count = min(z.halo, j + span - z.group)
            if count > 0:
                past = slice(0, count * z.wide)
                gk = gk + dot(sh[rows, past], qh[past, :], NN)
                gv = gv + dot(ph[rows, past], dh[past, :], NN)
            dk[rows, lanes] = gk.astype(BF16)
            dv[rows, lanes] = gv.astype(BF16)
        return 0

    lax.fori_loop(0, z.pairs, each, 0)


def seal_kernel(z, parts, dq, dk, dv, *refs):
    sums, sends = refs[:parts], refs[parts:]
    tok = z.tok
    total = sums[0][...]
    for ref in sums[1:]:
        total = total + ref[...]
    split = thirds(total).astype(F32)
    low = jnp.concatenate([split[16:24], jnp.zeros((8, z.buckets), F32)], axis=0)
    rows16 = jnp.concatenate([split[0:16], low], axis=1).astype(BF16)
    me = z.me()
    for k in range(z.group):
        rows = at((me ^ k) * tok, tok)
        for n, ref in enumerate((dq, dk, dv)):
            sends[k][n * tok : (n + 1) * tok, :] = ref[rows, :]
        sends[k][3 * tok :, :] = rows16


def add_kernel(*refs):
    total = refs[0][...]
    for ref in refs[1:-1]:
        total = total + ref[...]
    refs[-1][...] = total


def collect_kernel(z, *refs):
    got, out = refs[:-1], refs[-1]
    me = z.me()
    owner = lax.broadcasted_iota(jnp.int32, out.shape, 0) // z.hg
    total = jnp.zeros(out.shape, F32)
    for k in range(z.group):
        rows = got[k][3 * z.tok :, :].astype(F32)
        sums = rows[0:8, 0 : z.buckets] + rows[8:16, 0 : z.buckets] + rows[0:8, z.buckets :]
        wide = jnp.concatenate([sums[0 : z.hg]] * (out.shape[0] // z.hg), axis=0)
        total = total + jnp.where(owner == lax.axis_index("head") * z.group + (me ^ k), wide, 0.0)
    out[...] = total


def unpack_kernel(z, *refs):
    got, outs, sem = refs[: z.group], refs[z.group : -1], refs[-1]
    me = z.me()
    copies = []
    for k in range(z.group):
        cols = at((me ^ k) * z.cw, z.cw)
        for n, out in enumerate(outs):
            src = got[k].at[n * z.tok : (n + 1) * z.tok, :]
            copies.append(pltpu.make_async_copy(src, out.at[:, cols], sem.at[len(copies)]))
    for copy in copies:
        copy.start()
    for copy in copies:
        copy.wait()


def bind(kernel, *fixed):
    def bound(*refs):
        return kernel(*fixed, *refs)

    return bound


def body(queries, keys, values, grad_out, bias_table, bucket_ids, block_mask):
    tok, width = queries.shape
    heads, buckets = bias_table.shape
    span = block_mask.shape[1]
    group = span
    z = Sizes(tok, width, heads, span, buckets, group)
    blocks = lax.axis_size("seq")
    sides = lax.axis_size("head")
    assert blocks % group == 0 and (blocks & (blocks - 1)) == 0 and (sides & (sides - 1)) == 0

    def swap(value, by, axis="seq"):
        return lax.ppermute(value, axis, [(i, i ^ by) for i in range(lax.axis_size(axis))])

    def shifted(value, by):
        return lax.ppermute(value, "seq", [(i, i + by) for i in range(blocks) if 0 <= i + by < blocks])

    def added(*terms):
        (total,) = call(add_kernel, [(terms[0].shape, terms[0].dtype)], terms)
        return total

    tables = jnp.pad(bias_table.reshape(group, z.hg, buckets), ((0, 0), (0, 8 - z.hg), (0, 0)))
    table = lax.dynamic_index_in_dim(tables, lax.axis_index("seq") % group, 0, keepdims=False)

    hbm = pltpu.HBM
    pack_bytes = group * (z.rows + 2 * tok) * z.cw * 2
    packed = call(
        bind(pack_kernel, z),
        [((z.rows, z.cw), BF16)] * group + [((2 * tok, z.cw), BF16)] * group,
        (queries, keys, values, grad_out, bucket_ids, block_mask),
        spaces=[hbm] * 6,
        scratch=[
            pltpu.VMEM((span, z.wide), jnp.int32),
            pltpu.SMEM((1, span), jnp.int32),
            pltpu.SemaphoreType.DMA((4 * group + 2,)),
        ],
        limit=VMEM_BYTES - pack_bytes - (520 << 10),
    )
    kv, qd = packed[:group], packed[group:]
    kv_got = [kv[0]] + [swap(kv[k], k) for k in range(1, group)]
    qd_got = [qd[0]] + [swap(qd[k], k) for k in range(1, group)]
    (kv_out,) = call(bind(kv_halo_kernel, z), [((z.halo * 2 * tok, z.cw), BF16)], kv_got)
    kv_halo = shifted(kv_out, group)
    (qd_out,) = call(bind(qd_halo_kernel, z), [((z.halo * z.rows, z.cw), BF16)], (*qd_got, *kv_got))
    qd_halo = shifted(qd_out, -group)

    def tile_outs(count):
        tile = ((count * z.pairs, tok, z.wide), F32)
        row = ((count * z.pairs, z.wide), F32)
        return [tile, tile, row, row, row]

    near, far = len(z.near), len(z.far)
    unit = 2 * 128 * tok * z.wide
    own_k, own_v, bias_near, bias_far, codes = call(
        bind(bias_kernel, z),
        [((group * tok, z.cw), BF16)] * 2
        + [((near * z.pairs, tok, z.wide), F32), ((far * z.pairs, tok, z.wide), F32)]
        + [((group * CODE_ROWS, z.wide), F32)],
        (*kv_got, table),
        scratch=[pltpu.VMEM((group * span * 8, z.wide), F32)],
    )
    qm, dom, wnear, dnear, *sums = call(
        bind(near_kernel, z),
        [((z.pairs, group * z.wide, 128), BF16)] * 2 + tile_outs(near),
        (*qd_got, own_k, own_v, bias_near),
        flops=2 * near * z.pairs * unit,
    )
    stats, fnear, ffar, wfar, dfar, *_ = call(
        bind(far_kernel, z),
        [((2, group * z.pairs, z.wide), F32), ((near * z.pairs, z.wide), F32), ((far * z.pairs, z.wide), F32)]
        + tile_outs(far),
        (kv_halo, qm, dom, bias_far, *sums),
        flops=2 * far * z.pairs * unit,
    )
    stats_halo = lax.ppermute(stats, "seq", [(i, (i - group) % blocks) for i in range(blocks)])
    p16, s16, dq, gb = call(
        bind(own_kernel, z),
        [((z.pairs, group * tok, group * z.wide), BF16)] * 2
        + [((group * tok, z.cw), BF16), ((8, buckets), F32)],
        (own_k, kv_halo, codes, stats, fnear, ffar, wnear, dnear, wfar, dfar),
        scratch=[pltpu.VMEM((group * span * z.hg * 8, z.wide), F32)],
        flops=2 * (near + far) * z.pairs * unit,
    )
    terms = [gb]
    by = group
    while by < blocks:
        if len(terms) > 1:
            terms = [added(*terms)]
        ways = 4 if by * 2 < blocks else 2
        terms += [swap(terms[0], by * n) for n in range(1, ways)]
        by *= ways
    dk, dv = call(
        bind(tail_kernel, z),
        [((group * tok, z.cw), BF16)] * 2,
        (own_k, own_v, qm, dom, p16, s16, qd_halo, stats_halo, table),
        scratch=[
            pltpu.VMEM((z.halo * z.wide, 128), BF16),
            pltpu.VMEM((z.halo * z.wide, 128), BF16),
            pltpu.VMEM((group * tok, z.halo * z.wide), BF16),
            pltpu.VMEM((group * tok, z.halo * z.wide), BF16),
            pltpu.VMEM((z.halo * span * 8, z.wide), F32),
        ],
        flops=4 * far * z.pairs * unit,
    )
    ret = call(bind(seal_kernel, z, len(terms)), [((3 * tok + CODE_ROWS, z.cw), BF16)] * group, (dq, dk, dv, *terms))
    ret_got = [ret[0]] + [swap(ret[k], k) for k in range(1, group)]
    (side,) = call(bind(collect_kernel, z), [((heads * sides, buckets), F32)], ret_got)
    parts = [side] + [swap(side, k, "head") for k in range(1, sides)]
    grads = call(
        bind(unpack_kernel, z),
        [((tok, width), BF16)] * 3,
        ret_got,
        out_space=hbm,
        scratch=[pltpu.SemaphoreType.DMA((3 * group,))],
    )
    return (*grads, sum(parts[1:], parts[0]))


def solution(mesh):
    placed = (
        P("seq", "head"),
        P("seq", "head"),
        P("seq", "head"),
        P("seq", "head"),
        P("head", None),
        P("seq", None, None),
        P("seq", None),
    )

    return jax.shard_map(
        body,
        mesh=mesh,
        in_specs=placed,
        out_specs=(P("seq", "head"), P("seq", "head"), P("seq", "head"), P()),
        check_vma=False,
    )
```

profile of v0, /device:TPU:0, one launch (start us, length us, event | category | flops | bytes accessed | tf_op | source)
XLA Modules:
  0.0 61.7 jit_solution(11010907692946455143)
XLA Ops:
  0.6 0.0 copy-start
  0.6 2.1 %shard_map.102 = (bf16[272,256]{1,0:T(8,128)(2,1)S(1)}, bf16[272,256]{1,0:T(8,128)(2,1)S(1)}, bf16[272,256]{1,0:T(8,128)(2,1)S(1)}, bf16[272,256]{1,0:T(8,128)(2...) custom-call(bf16[128,1024]{1,0:T(8,128)(2,1)} %refs_0_.1, ...), custom_call_target="tpu_custom_call" | custom-call | bytes 1052688 | tf_op jit(solution)/shard_map/pallas_call | solution.py:34
  2.8 3.0 %collective-permute-start = (bf16[272,256]{1,0:T(8,128)(2,1)S(1)}, bf16[272,256]{1,0:T(8,128)(2,1)S(1)}, u32[]{:S(2)}, u32[]{:S(2)}) collective-permute-start(bf16[272,256]{1,0:T(8,128)(2,1)S(1)} %get-tuple-element.43), channel_id=1, source_target_pairs={{0,2},{2,0},{4,6},{6,4},{8,10},{10,8},{12,14},{14,12},{16,18},{18,... | collective-permute-start | bytes 417800 | tf_op jit(solution)/shard_map/ppermute | solution.py:454
  5.8 1.5 %collective-permute-start.1 = (bf16[272,256]{1,0:T(8,128)(2,1)S(1)}, bf16[272,256]{1,0:T(8,128)(2,1)S(1)}, u32[]{:S(2)}, u32[]{:S(2)}) collective-permute-start(bf16[272,256]{1,0:T(8,128)(2,1)S(1)} %get-tuple-element.44), channel_id=1, source_target_pairs={{0,4},{2,6},{4,0},{6,2},{8,12},{10,14},{12,8},{14,10},{16,20},{18,... | collective-permute-start | bytes 417800 | tf_op jit(solution)/shard_map/ppermute | solution.py:454
  7.3 0.0 collective-permute-start.2
  7.4 1.9 %collective-permute-start.4 = (bf16[256,256]{1,0:T(8,128)(2,1)}, bf16[256,256]{1,0:T(8,128)(2,1)S(1)}, u32[]{:S(2)}, u32[]{:S(2)}) collective-permute-start(bf16[256,256]{1,0:T(8,128)(2,1)} %get-tuple-element.49), channel_id=1, source_target_pairs={{0,2},{2,0},{4,6},{6,4},{8,10},{10,8},{12,14},{14,12},{16,18},{18,... | collective-permute-start | bytes 393224 | tf_op jit(solution)/shard_map/ppermute | solution.py:454
  9.3 1.5 %collective-permute-start.5 = (bf16[256,256]{1,0:T(8,128)(2,1)}, bf16[256,256]{1,0:T(8,128)(2,1)S(1)}, u32[]{:S(2)}, u32[]{:S(2)}) collective-permute-start(bf16[256,256]{1,0:T(8,128)(2,1)} %get-tuple-element.50), channel_id=1, source_target_pairs={{0,4},{2,6},{4,0},{6,2},{8,12},{10,14},{12,8},{14,10},{16,20},{18,... | collective-permute-start | bytes 393224 | tf_op jit(solution)/shard_map/ppermute | solution.py:454
  10.8 0.0 collective-permute-done.refs_1_.refs_5_
  10.8 2.5 %collective-permute-start.6 = (bf16[256,256]{1,0:T(8,128)(2,1)S(1)}, bf16[256,256]{1,0:T(8,128)(2,1)S(1)}, u32[]{:S(2)}, u32[]{:S(2)}) collective-permute-start(bf16[256,256]{1,0:T(8,128)(2,1)S(1)} %get-tuple-element.51), channel_id=1, source_target_pairs={{0,6},{2,4},{4,2},{6,0},{8,14},{10,12},{12,10},{14,8},{16,22},{18,... | collective-permute-start | bytes 393224 | tf_op jit(solution)/shard_map/ppermute | solution.py:454
  13.3 1.7 %collective-permute-done.1.refs_2_.refs_6_ = bf16[272,256]{1,0:T(8,128)(2,1)S(1)} collective-permute-done((bf16[272,256]{1,0:T(8,128)(2,1)S(1)}, bf16[272,256]{1,0:T(8,128)(2,1)S(1)}, u32[]{:S(2)}, u32[]{:S(2)}) %collective-permute-start.1) | collective-permute-done | bytes 139296 | tf_op jit(solution)/shard_map/ppermute | solution.py:454
  15.0 0.0 collective-permute-done.2.refs_3_.refs_7_
  15.0 3.3 %collective-permute-start.3 = (bf16[768,256]{1,0:T(8,128)(2,1)S(1)}, bf16[768,256]{1,0:T(8,128)(2,1)S(1)}, u32[]{:S(2)}, u32[]{:S(2)}) collective-permute-start(bf16[768,256]{1,0:T(8,128)(2,1)S(1)} %shard_map.104), channel_id=1, source_target_pairs={{0,8},{2,10},{4,12},{6,14},{8,16},{10,18},{12,20},{14,22},{16,24},... | collective-permute-start | bytes 1179656 | tf_op jit(solution)/shard_map/ppermute | solution.py:457
  18.4 0.0 collective-permute-done.4.refs_1_
  18.4 1.2 %collective-permute-done.5.refs_2_ = bf16[256,256]{1,0:T(8,128)(2,1)S(1)} collective-permute-done((bf16[256,256]{1,0:T(8,128)(2,1)}, bf16[256,256]{1,0:T(8,128)(2,1)S(1)}, u32[]{:S(2)}, u32[]{:S(2)}) %collective-permute-start.5) | collective-permute-done | bytes 131104 | tf_op jit(solution)/shard_map/ppermute | solution.py:454
  19.5 0.0 collective-permute-done.6.refs_3_
  19.6 1.3 %collective-permute-start.7 = (bf16[816,256]{1,0:T(8,128)(2,1)S(1)}, bf16[816,256]{1,0:T(8,128)(2,1)S(1)}, u32[]{:S(2)}, u32[]{:S(2)}) collective-permute-start(bf16[816,256]{1,0:T(8,128)(2,1)S(1)} %shard_map.108), channel_id=1, source_target_pairs={{8,0},{10,2},{12,4},{14,6},{16,8},{18,10},{20,12},{22,14},{24,16},... | collective-permute-start | bytes 1253384 | tf_op jit(solution)/shard_map/ppermute | solution.py:457
  20.9 0.0 copy-done
  20.9 6.4 %shard_map.103 = (bf16[512,256]{1,0:T(8,128)(2,1)S(1)}, bf16[512,256]{1,0:T(8,128)(2,1)S(1)}, f32[20,128,256]{2,1,0:T(8,128)S(1)}, f32[12,128,256]{2,1,0:T(8,128)S(1)}, f32[64,256]{1,0:T(8,128)S(1)}) custom-call(bf16[272,256]{1,0:T(8,128)(2,1)S(1)} %get-tuple-element.42.refs_0_.refs_4_, bf16[272,256]{1,0:T(8,128)(2,1)S(1)} %collective-permute-done.refs_1_.refs_5_, ...), custom_call_target="tpu_custom_call" | custom-call | bytes 561152 | tf_op jit(solution)/shard_map/pallas_call | solution.py:34
  27.4 1.6 %shard_map.105 = (bf16[2,1024,128]{2,1,0:T(8,128)(2,1)S(1)}, bf16[2,1024,128]{2,1,0:T(8,128)(2,1)S(1)}, f32[20,128,256]{2,1,0:T(8,128)S(1)}, f32[20,128,256]{2,1...) custom-call(bf16[256,256]{1,0:T(8,128)(2,1)S(1)} %get-tuple-element.48.refs_0_, ...), custom_call_target="tpu_custom_call" | custom-call | flops 335544320 | bytes 3670016 | tf_op jit(solution)/shard_map/pallas_call | solution.py:34
  29.0 0.0 collective-permute-done.3.refs_0_.refs_1_
  29.0 1.6 %shard_map.106 = (f32[2,8,256]{2,1,0:T(8,128)S(1)}, f32[20,256]{1,0:T(8,128)S(1)}, f32[12,256]{1,0:T(8,128)S(1)}, f32[12,128,256]{2,1,0:T(8,128)S(1)}, f32[12,12...) custom-call(bf16[768,256]{1,0:T(8,128)(2,1)S(1)} %collective-permute-done.3.refs_0_.refs_1_, ...), custom_call_target="tpu_custom_call" | custom-call | flops 201326592 | bytes 3076096 | tf_op jit(solution)/shard_map/pallas_call | solution.py:34
  30.6 4.7 %collective-permute-start.8 = (f32[2,8,256]{2,1,0:T(8,128)S(1)}, f32[2,8,256]{2,1,0:T(8,128)S(1)}, u32[]{:S(2)}, u32[]{:S(2)}) collective-permute-start(f32[2,8,256]{2,1,0:T(8,128)S(1)} %get-tuple-element.60.refs_3_), channel_id=1, source_target_pairs={{0,24},{2,26},{4,28},{6,30},{8,0},{10,2},{12,4},{14,6},{16,8},{18,... | collective-permute-start | bytes 49160 | tf_op jit(solution)/shard_map/ppermute | solution.py:516
  35.3 7.8 %shard_map.107 = (bf16[2,512,1024]{2,1,0:T(8,128)(2,1)S(1)}, bf16[2,512,1024]{2,1,0:T(8,128)(2,1)S(1)}, bf16[512,256]{1,0:T(8,128)(2,1)S(1)}, f32[8,128]{1,0:T(8,128)S(1)}) custom-call(bf16[512,256]{1,0:T(8,128)(2,1)S(1)} %get-tuple-element.46.refs_4_.refs_0_, bf16[768,256]{1,0:T(8,128)(2,1)S(1)} %collective-permute-done.3.refs_0_.refs_1_, ...), custom_call_target="tpu_custom_call" | custom-call | flops 536870912 | bytes 9158656 | tf_op jit(solution)/shard_map/pallas_call | solution.py:34
  43.1 0.4 collective-permute-start.11
  43.5 0.0 collective-permute-start.10
  43.5 4.0 %collective-permute-start.9 = (f32[8,128]{1,0:T(8,128)S(1)}, f32[8,128]{1,0:T(8,128)S(1)}, u32[]{:S(2)}, u32[]{:S(2)}) collective-permute-start(f32[8,128]{1,0:T(8,128)S(1)} %get-tuple-element.72.refs_3_), channel_id=1, source_target_pairs={{0,8},{2,10},{4,12},{6,14},{8,0},{10,2},{12,4},{14,6},{16,24},{18,... | collective-permute-start | bytes 12296 | tf_op jit(solution)/shard_map/ppermute | solution.py:454
  47.4 0.0 collective-permute-done.8.refs_7_
  47.5 0.0 collective-permute-done.7.refs_6_
  47.5 2.3 %shard_map.109 = (bf16[512,256]{1,0:T(8,128)(2,1)S(1)}, bf16[512,256]{1,0:T(8,128)(2,1)S(1)}) custom-call(bf16[512,256]{1,0:T(8,128)(2,1)S(1)} %get-tuple-element.46.refs_4_.refs_0_, bf16[512,256]{1,0:T(8,128)(2,1)S(1)} %get-tuple-element.52.refs_5_.refs_1_, bf16[2,1024,128]{2,1,0:T(8,128)(2,1)S(1)} %get-tuple-element.54.refs_1_.refs_2_, ...), custom_call_target="tpu_custom_call" | custom-call | flops 402653184 | bytes 6205440 | tf_op jit(solution)/shard_map/pallas_call | solution.py:34
  49.7 0.0 collective-permute-done.11.refs_6_
  49.7 0.0 collective-permute-done.10.refs_5_
  49.7 0.0 collective-permute-done.9.refs_4_
  49.8 0.1 shard_map.110
  49.8 1.3 %collective-permute-start.12 = (bf16[400,256]{1,0:T(8,128)(2,1)S(1)}, bf16[400,256]{1,0:T(8,128)(2,1)S(1)}, u32[]{:S(2)}, u32[]{:S(2)}) collective-permute-start(bf16[400,256]{1,0:T(8,128)(2,1)S(1)} %get-tuple-element.74), channel_id=1, source_target_pairs={{0,2},{2,0},{4,6},{6,4},{8,10},{10,8},{12,14},{14,12},{16,18},{18,... | collective-permute-start | bytes 614408 | tf_op jit(solution)/shard_map/ppermute | solution.py:454
  51.1 0.8 %collective-permute-start.13 = (bf16[400,256]{1,0:T(8,128)(2,1)S(1)}, bf16[400,256]{1,0:T(8,128)(2,1)S(1)}, u32[]{:S(2)}, u32[]{:S(2)}) collective-permute-start(bf16[400,256]{1,0:T(8,128)(2,1)S(1)} %get-tuple-element.75), channel_id=1, source_target_pairs={{0,4},{2,6},{4,0},{6,2},{8,12},{10,14},{12,8},{14,10},{16,20},{18,... | collective-permute-start | bytes 614408 | tf_op jit(solution)/shard_map/ppermute | solution.py:454
  52.0 1.4 %collective-permute-start.14 = (bf16[400,256]{1,0:T(8,128)(2,1)S(1)}, bf16[400,256]{1,0:T(8,128)(2,1)S(1)}, u32[]{:S(2)}, u32[]{:S(2)}) collective-permute-start(bf16[400,256]{1,0:T(8,128)(2,1)S(1)} %get-tuple-element.76), channel_id=1, source_target_pairs={{0,6},{2,4},{4,2},{6,0},{8,14},{10,12},{12,10},{14,8},{16,22},{18,... | collective-permute-start | bytes 614408 | tf_op jit(solution)/shard_map/ppermute | solution.py:454
  53.4 3.2 %collective-permute-done.12.refs_1_ = bf16[400,256]{1,0:T(8,128)(2,1)S(1)} collective-permute-done((bf16[400,256]{1,0:T(8,128)(2,1)S(1)}, bf16[400,256]{1,0:T(8,128)(2,1)S(1)}, u32[]{:S(2)}, u32[]{:S(2)}) %collective-permute-start.12) | collective-permute-done | bytes 204832 | tf_op jit(solution)/shard_map/ppermute | solution.py:454
  56.6 3.2 %collective-permute-done.13.refs_2_ = bf16[400,256]{1,0:T(8,128)(2,1)S(1)} collective-permute-done((bf16[400,256]{1,0:T(8,128)(2,1)S(1)}, bf16[400,256]{1,0:T(8,128)(2,1)S(1)}, u32[]{:S(2)}, u32[]{:S(2)}) %collective-permute-start.13) | collective-permute-done | bytes 204832 | tf_op jit(solution)/shard_map/ppermute | solution.py:454
  59.8 0.0 collective-permute-done.14.refs_3_
  59.8 0.1 collective-permute-start.15
  59.9 1.0 %shard_map.111 = (bf16[128,1024]{1,0:T(8,128)(2,1)}, bf16[128,1024]{1,0:T(8,128)(2,1)}, bf16[128,1024]{1,0:T(8,128)(2,1)}) custom-call(bf16[400,256]{1,0:T(8,128)(2,1)S(1)} %get-tuple-element.73.refs_0_, bf16[400,256]{1,0:T(8,128)(2,1)S(1)} %collective-permute-done.12.refs_1_, bf16[400,256]{1,0:T(8,128)(2,1)S(1)} %collective-permute-done.13.refs_2_, ...), custom_call_target="tpu_custom_call" | custom-call | bytes 819200 | tf_op jit(solution)/shard_map/pallas_call | solution.py:34
  60.9 0.2 collective-permute-done.15
  61.1 0.6 add.15
  (4 shorter events, 0.1 us)
Async XLA Ops:
  0.6 20.3 %copy-start = (f32[16,128]{1,0:T(8,128)S(1)}, f32[16,128]{1,0:T(8,128)}, u32[]{:S(2)}) copy-start(f32[16,128]{1,0:T(8,128)} %param.11) | copy-start | bytes 24580
  2.8 8.0 %collective-permute-start = (bf16[272,256]{1,0:T(8,128)(2,1)S(1)}, bf16[272,256]{1,0:T(8,128)(2,1)S(1)}, u32[]{:S(2)}, u32[]{:S(2)}) collective-permute-start(bf16[272,256]{1,0:T(8,128)(2,1)S(1)} %get-tuple-element.43), channel_id=1, source_target_pairs={{0,2},{2,0},{4,6},{6,4},{8,10},{10,8},{12,14},{14,12},{16,18},{18,... | collective-permute-start | bytes 417800 | tf_op jit(solution)/shard_map/ppermute | solution.py:454
  5.8 9.2 %collective-permute-start.1 = (bf16[272,256]{1,0:T(8,128)(2,1)S(1)}, bf16[272,256]{1,0:T(8,128)(2,1)S(1)}, u32[]{:S(2)}, u32[]{:S(2)}) collective-permute-start(bf16[272,256]{1,0:T(8,128)(2,1)S(1)} %get-tuple-element.44), channel_id=1, source_target_pairs={{0,4},{2,6},{4,0},{6,2},{8,12},{10,14},{12,8},{14,10},{16,20},{18,... | collective-permute-start | bytes 417800 | tf_op jit(solution)/shard_map/ppermute | solution.py:454
  7.3 7.6 %collective-permute-start.2 = (bf16[272,256]{1,0:T(8,128)(2,1)S(1)}, bf16[272,256]{1,0:T(8,128)(2,1)S(1)}, u32[]{:S(2)}, u32[]{:S(2)}) collective-permute-start(bf16[272,256]{1,0:T(8,128)(2,1)S(1)} %get-tuple-element.45), channel_id=1, source_target_pairs={{0,6},{2,4},{4,2},{6,0},{8,14},{10,12},{12,10},{14,8},{16,22},{18,... | collective-permute-start | bytes 417800 | tf_op jit(solution)/shard_map/ppermute | solution.py:454
  7.4 11.0 %collective-permute-start.4 = (bf16[256,256]{1,0:T(8,128)(2,1)}, bf16[256,256]{1,0:T(8,128)(2,1)S(1)}, u32[]{:S(2)}, u32[]{:S(2)}) collective-permute-start(bf16[256,256]{1,0:T(8,128)(2,1)} %get-tuple-element.49), channel_id=1, source_target_pairs={{0,2},{2,0},{4,6},{6,4},{8,10},{10,8},{12,14},{14,12},{16,18},{18,... | collective-permute-start | bytes 393224 | tf_op jit(solution)/shard_map/ppermute | solution.py:454
  9.3 10.2 %collective-permute-start.5 = (bf16[256,256]{1,0:T(8,128)(2,1)}, bf16[256,256]{1,0:T(8,128)(2,1)S(1)}, u32[]{:S(2)}, u32[]{:S(2)}) collective-permute-start(bf16[256,256]{1,0:T(8,128)(2,1)} %get-tuple-element.50), channel_id=1, source_target_pairs={{0,4},{2,6},{4,0},{6,2},{8,12},{10,14},{12,8},{14,10},{16,20},{18,... | collective-permute-start | bytes 393224 | tf_op jit(solution)/shard_map/ppermute | solution.py:454
  10.8 8.7 %collective-permute-start.6 = (bf16[256,256]{1,0:T(8,128)(2,1)S(1)}, bf16[256,256]{1,0:T(8,128)(2,1)S(1)}, u32[]{:S(2)}, u32[]{:S(2)}) collective-permute-start(bf16[256,256]{1,0:T(8,128)(2,1)S(1)} %get-tuple-element.51), channel_id=1, source_target_pairs={{0,6},{2,4},{4,2},{6,0},{8,14},{10,12},{12,10},{14,8},{16,22},{18,... | collective-permute-start | bytes 393224 | tf_op jit(solution)/shard_map/ppermute | solution.py:454
  15.0 13.9 %collective-permute-start.3 = (bf16[768,256]{1,0:T(8,128)(2,1)S(1)}, bf16[768,256]{1,0:T(8,128)(2,1)S(1)}, u32[]{:S(2)}, u32[]{:S(2)}) collective-permute-start(bf16[768,256]{1,0:T(8,128)(2,1)S(1)} %shard_map.104), channel_id=1, source_target_pairs={{0,8},{2,10},{4,12},{6,14},{8,16},{10,18},{12,20},{14,22},{16,24},... | collective-permute-start | bytes 1179656 | tf_op jit(solution)/shard_map/ppermute | solution.py:457
  19.6 27.9 %collective-permute-start.7 = (bf16[816,256]{1,0:T(8,128)(2,1)S(1)}, bf16[816,256]{1,0:T(8,128)(2,1)S(1)}, u32[]{:S(2)}, u32[]{:S(2)}) collective-permute-start(bf16[816,256]{1,0:T(8,128)(2,1)S(1)} %shard_map.108), channel_id=1, source_target_pairs={{8,0},{10,2},{12,4},{14,6},{16,8},{18,10},{20,12},{22,14},{24,16},... | collective-permute-start | bytes 1253384 | tf_op jit(solution)/shard_map/ppermute | solution.py:457
  30.6 16.9 %collective-permute-start.8 = (f32[2,8,256]{2,1,0:T(8,128)S(1)}, f32[2,8,256]{2,1,0:T(8,128)S(1)}, u32[]{:S(2)}, u32[]{:S(2)}) collective-permute-start(f32[2,8,256]{2,1,0:T(8,128)S(1)} %get-tuple-element.60.refs_3_), channel_id=1, source_target_pairs={{0,24},{2,26},{4,28},{6,30},{8,0},{10,2},{12,4},{14,6},{16,8},{18,... | collective-permute-start | bytes 49160 | tf_op jit(solution)/shard_map/ppermute | solution.py:516
  43.1 6.7 %collective-permute-start.11 = (f32[8,128]{1,0:T(8,128)S(1)}, f32[8,128]{1,0:T(8,128)S(1)}, u32[]{:S(2)}, u32[]{:S(2)}) collective-permute-start(f32[8,128]{1,0:T(8,128)S(1)} %get-tuple-element.72.refs_3_), channel_id=1, source_target_pairs={{0,24},{2,26},{4,28},{6,30},{8,16},{10,18},{12,20},{14,22},{16,8},... | collective-permute-start | bytes 12296 | tf_op jit(solution)/shard_map/ppermute | solution.py:454
  43.5 6.2 %collective-permute-start.10 = (f32[8,128]{1,0:T(8,128)S(1)}, f32[8,128]{1,0:T(8,128)S(1)}, u32[]{:S(2)}, u32[]{:S(2)}) collective-permute-start(f32[8,128]{1,0:T(8,128)S(1)} %get-tuple-element.72.refs_3_), channel_id=1, source_target_pairs={{0,16},{2,18},{4,20},{6,22},{8,24},{10,26},{12,28},{14,30},{16,0},... | collective-permute-start | bytes 12296 | tf_op jit(solution)/shard_map/ppermute | solution.py:454
  43.5 6.3 %collective-permute-start.9 = (f32[8,128]{1,0:T(8,128)S(1)}, f32[8,128]{1,0:T(8,128)S(1)}, u32[]{:S(2)}, u32[]{:S(2)}) collective-permute-start(f32[8,128]{1,0:T(8,128)S(1)} %get-tuple-element.72.refs_3_), channel_id=1, source_target_pairs={{0,8},{2,10},{4,12},{6,14},{8,0},{10,2},{12,4},{14,6},{16,24},{18,... | collective-permute-start | bytes 12296 | tf_op jit(solution)/shard_map/ppermute | solution.py:454
  49.8 6.8 %collective-permute-start.12 = (bf16[400,256]{1,0:T(8,128)(2,1)S(1)}, bf16[400,256]{1,0:T(8,128)(2,1)S(1)}, u32[]{:S(2)}, u32[]{:S(2)}) collective-permute-start(bf16[400,256]{1,0:T(8,128)(2,1)S(1)} %get-tuple-element.74), channel_id=1, source_target_pairs={{0,2},{2,0},{4,6},{6,4},{8,10},{10,8},{12,14},{14,12},{16,18},{18,... | collective-permute-start | bytes 614408 | tf_op jit(solution)/shard_map/ppermute | solution.py:454
  51.1 8.7 %collective-permute-start.13 = (bf16[400,256]{1,0:T(8,128)(2,1)S(1)}, bf16[400,256]{1,0:T(8,128)(2,1)S(1)}, u32[]{:S(2)}, u32[]{:S(2)}) collective-permute-start(bf16[400,256]{1,0:T(8,128)(2,1)S(1)} %get-tuple-element.75), channel_id=1, source_target_pairs={{0,4},{2,6},{4,0},{6,2},{8,12},{10,14},{12,8},{14,10},{16,20},{18,... | collective-permute-start | bytes 614408 | tf_op jit(solution)/shard_map/ppermute | solution.py:454
  52.0 7.8 %collective-permute-start.14 = (bf16[400,256]{1,0:T(8,128)(2,1)S(1)}, bf16[400,256]{1,0:T(8,128)(2,1)S(1)}, u32[]{:S(2)}, u32[]{:S(2)}) collective-permute-start(bf16[400,256]{1,0:T(8,128)(2,1)S(1)} %get-tuple-element.76), channel_id=1, source_target_pairs={{0,6},{2,4},{4,2},{6,0},{8,14},{10,12},{12,10},{14,8},{16,22},{18,... | collective-permute-start | bytes 614408 | tf_op jit(solution)/shard_map/ppermute | solution.py:454
  59.8 1.2 %collective-permute-start.15 = (f32[32,128]{1,0:T(8,128)S(1)}, f32[32,128]{1,0:T(8,128)S(1)}, u32[]{:S(2)}, u32[]{:S(2)}) collective-permute-start(f32[32,128]{1,0:T(8,128)S(1)} %shard_map.112), channel_id=1, source_target_pairs={{0,1},{1,0},{2,3},{3,2},{4,5},{5,4},{6,7},{7,6},{8,9},{9,8},{10,11... | collective-permute-start | bytes 49160 | tf_op jit(solution)/shard_map/ppermute | solution.py:454
where the time goes:
time: 61.9 us; the launch traced here: 61.7 us
  starting transfers between devices  27.9 us (45%)
  Pallas kernels  22.9 us (37%)
  waiting for transfers between devices  9.44 us (15%)
  between operations  0.82 us (1%)
    pallas_call x11, Pallas kernels, call(): pl.pallas_call(kernel, out_shape=tuple((out_space(s, d) for s, d in outs)...  22.9 us
    ppermute x13, starting transfers between devices, swap(): lax.ppermute(value, axis, [(i, i ^ by) for i in range(lax.axis_size(axis))])  18.5 us
    ppermute x13, waiting for transfers between devices, swap(): lax.ppermute(value, axis, [(i, i ^ by) for i in range(lax.axis_size(axis))])  9.43 us
    ppermute x1, starting transfers between devices, body(): lax.ppermute(stats, 'seq', [(i, (i - group) % blocks) for i in range(bloc...  4.69 us
    ppermute x2, starting transfers between devices, shifted(): lax.ppermute(value, 'seq', [(i, i + by) for i in range(blocks) if 0 <= i...  4.64 us
  transfers between devices with their start and end apart: 16, of which 5 were waited for; matrix products, arithmetic and copies ran while one was open for 0% of the time, Pallas kernels for 34%

commit v1 on v0

--- a/solution.py
+++ b/solution.py
@@ -52,6 +52,7 @@
         self.pairs = self.hg // 2
         self.scale = self.hd ** (-0.5)
         self.halo = span - 1
+        self.ext = group + self.halo
         self.wide = 2 * tok
         self.rows = 2 * tok + CODE_ROWS
         self.near = [(i, s) for i in range(group) for s in range(span) if s <= i]
@@ -144,10 +145,35 @@
     return jnp.concatenate([jnp.where(lane < z.hd, x, zero), jnp.where(lane < z.hd, zero, x)], axis=0)
 
 
-def toeplitz(row, z):
-    base = pltpu.roll(jnp.broadcast_to(row, (8, z.wide)), z.tok + 1, 1, stride=1, stride_axis=0)
-    tiles = [pltpu.roll(base, 8 * g, 1)[:, : z.tok] if g else base[:, : z.tok] for g in range(z.tok // 8)]
+def slanted(row, z):
+    return pltpu.roll(jnp.broadcast_to(row, (8, z.wide)), z.tok + 1, 1, stride=1, stride_axis=0)
+
+
+def toeplitz(base, z):
+    tok = z.tok
+    lane = lax.broadcasted_iota(jnp.int32, (8, tok), 1)
+    low, high = base[:, 0:tok], base[:, tok:]
+    tiles = [low]
+    for g in range(1, tok // 8):
+        tiles.append(pltpu.roll(jnp.where(lane >= tok - 8 * g, high, low), 8 * g, 1))
     return jnp.concatenate(tiles, axis=0)
+
+
+def my_table(table, z):
+    head = lax.broadcasted_iota(jnp.int32, (8, z.buckets), 0)
+    rows = jnp.zeros((8, z.buckets), F32)
+    for h in range(z.hg):
+        rows = jnp.where(head == h, table[pl.ds(z.me() * z.hg + h, 1), :], rows)
+    return rows
+
+
+def slant_tables(z, table, code_rows, bases):
+    split = thirds(my_table(table, z))
+    for n, codes in enumerate(code_rows):
+        rows = by_offset(split, codes, z)
+        for h in range(z.hg):
+            at_row = (n * z.hg + h) * 8
+            bases[at_row : at_row + 8, :] = slanted(rows[h : h + 1, :], z)
 
 
 def diagonals(x, z):
@@ -180,14 +206,14 @@
     return how(how(x.reshape(x.shape[0] // 8, 8, x.shape[1]), 0), 0, keepdims=True)
 
 
-def bias_rows(z, boff, base, pair):
-    rows = [toeplitz(boff[pl.ds(base + 2 * pair + e, 1), :], z) for e in range(2)]
+def bias_rows(z, bases, n, pair):
+    rows = [toeplitz(bases[(n * z.hg + 2 * pair + e) * 8 : (n * z.hg + 2 * pair + e + 1) * 8, :], z) for e in range(2)]
     return jnp.concatenate(rows, axis=1)
 
 
 def bias_kernel(z, *refs):
     kv, table = refs[: z.group], refs[z.group]
-    keys, values, near, far, codes, boff = refs[z.group + 1 :]
+    keys, values, near, far, codes, bases = refs[z.group + 1 :]
     tok = z.tok
     me = z.me()
     for k in range(z.group):
@@ -195,20 +221,13 @@
         keys[at(j * tok, tok), :] = kv[k][0:tok, :]
         values[at(j * tok, tok), :] = kv[k][tok : 2 * tok, :]
         codes[at(j * CODE_ROWS, CODE_ROWS), :] = kv[k][2 * tok :, :].astype(F32)
-    split = thirds(table[...])
-    for i in range(z.group):
-        for s in range(z.span):
-            row = codes[i * CODE_ROWS + s : i * CODE_ROWS + s + 1, :]
-            boff[(i * z.span + s) * 8 : (i * z.span + s) * 8 + 8, :] = by_offset(split, row, z)
-
-    def each(pair, _):
-        for tiles, out in ((z.near, near), (z.far, far)):
-            for t, (i, s) in enumerate(tiles):
-                bias = bias_rows(z, boff, (i * z.span + s) * 8, pair)
+    tables = [(i, s) for i in range(z.group) for s in range(z.span)]
+    slant_tables(z, table, [codes[i * CODE_ROWS + s : i * CODE_ROWS + s + 1, :] for i, s in tables], bases)
+    for tiles, out in ((z.near, near), (z.far, far)):
+        for t, (i, s) in enumerate(tiles):
+            for pair in range(z.pairs):
+                bias = bias_rows(z, bases, i * z.span + s, pair)
                 out[t * z.pairs + pair] = jnp.where(causal(z), bias, NEG) if s == 0 else bias
-        return 0
-
-    lax.fori_loop(0, z.pairs, each, 0)
 
 
 def forward_tile(key, value, q, d, bias, row, outs):
@@ -287,8 +306,45 @@
     lax.fori_loop(0, z.pairs, each, 0)
 
 
-def own_kernel(z, keys, halo, codes, stats, fnear, ffar, wnear, dnear, wfar, dfar, *refs):
-    p16, s16, dq, gb, offs = refs
+def own_kernel(z, codes, stats, fnear, ffar, wnear, dnear, wfar, dfar, p16, s16, gb, offs):
+    tok, span = z.tok, z.span
+
+    def each(pair, _):
+        for i in range(z.group):
+            wide = slice(i * z.wide, (i + 1) * z.wide)
+            delta = stats[1, pl.ds(i * z.pairs + pair, 1), :]
+            for s in range(span):
+                close = s <= i
+                t = (z.near if close else z.far).index((i, s)) * z.pairs + pair
+                w, d, f = (wnear, dnear, fnear) if close else (wfar, dfar, ffar)
+                prob = w[t] * f[pl.ds(t, 1), :]
+                dscore = prob * (d[t] - delta)
+                rows = slice((z.halo + i - s) * tok, (z.halo + i - s + 1) * tok)
+                s16[pair, rows, wide] = dscore.astype(BF16)
+                if close:
+                    p16[pair, (i - s) * tok : (i - s + 1) * tok, wide] = prob.astype(BF16)
+                for e in range(2):
+                    low, high = diagonals(dscore[:, e * tok : (e + 1) * tok], z)
+                    row = at(((i * span + s) * z.hg + 2 * pair + e) * 8, 8)
+                    offs[row, 0:tok] = low
+                    offs[row, tok:] = high
+        return 0
+
+    lax.fori_loop(0, z.pairs, each, 0)
+    head = lax.broadcasted_iota(jnp.int32, (8, z.wide), 0)
+    total = jnp.zeros((8, z.buckets), F32)
+    for n in range(z.group * span):
+        both = aligned(offs[n * z.hg * 8 : (n + 1) * z.hg * 8, :])
+        sums = jnp.zeros((8, z.wide), F32)
+        for h in range(z.hg):
+            sums = sums + jnp.where(head == h, both[8 * h : 8 * h + 8].sum(axis=0, keepdims=True), 0.0)
+        row = n // span * CODE_ROWS + n % span
+        got = dot(thirds(sums), onehot_of(codes[row : row + 1, :], z), NT)
+        total = total + (got[0:8] + got[8:16] + got[16:24])
+    gb[...] = total
+
+
+def grad_q_kernel(z, keys, halo, s16, dq):
     tok, span = z.tok, z.span
 
     def each(pair, _):
@@ -297,83 +353,60 @@
         blocks += [keys[j * tok : (j + 1) * tok, lanes] for j in range(z.group)]
         turned = jnp.concatenate([block.T for block in blocks], axis=1)
         for i in range(z.group):
-            wide = slice(i * z.wide, (i + 1) * z.wide)
-            delta = stats[1, pl.ds(i * z.pairs + pair, 1), :]
-            parts = []
-            for s in reversed(range(span)):
-                close = s <= i
-                t = (z.near if close else z.far).index((i, s)) * z.pairs + pair
-                w, d, f = (wnear, dnear, fnear) if close else (wfar, dfar, ffar)
-                prob = w[t] * f[pl.ds(t, 1), :]
-                dscore = prob * (d[t] - delta)
-                half = dscore.astype(BF16)
-                parts.append(half)
-                if close:
-                    rows = slice((i - s) * tok, (i - s + 1) * tok)
-                    p16[pair, rows, wide] = prob.astype(BF16)
-                    s16[pair, rows, wide] = half
-                for e in range(2):
-                    low, high = diagonals(dscore[:, e * tok : (e + 1) * tok], z)
-                    row = at(((i * span + s) * z.hg + 2 * pair + e) * 8, 8)
-                    offs[row, 0:tok] = low
-                    offs[row, tok:] = high
-            cross = dot(turned[:, i * tok : (i + span) * tok], jnp.concatenate(parts, axis=0), NN)
+            window = slice(i * tok, (i + span) * tok)
+            cross = dot(turned[:, window], s16[pair, window, i * z.wide : (i + 1) * z.wide], NN)
             both = jnp.concatenate([cross[0 : z.hd, 0:tok], cross[z.hd :, tok:]], axis=0)
             dq[i * tok : (i + 1) * tok, lanes] = (z.scale * both.T).astype(BF16)
         return 0
 
     lax.fori_loop(0, z.pairs, each, 0)
-    head = lax.broadcasted_iota(jnp.int32, (8, z.wide), 0)
-
-    def bucket(n, total):
-        i, s = n // span, n % span
-        both = aligned(offs[at(n * z.hg * 8, z.hg * 8), :])
-        sums = jnp.zeros((8, z.wide), F32)
-        for h in range(z.hg):
-            sums = sums + jnp.where(head == h, both[8 * h : 8 * h + 8].sum(axis=0, keepdims=True), 0.0)
-        got = dot(thirds(sums), onehot_of(codes[pl.ds(i * CODE_ROWS + s, 1), :], z), NT)
-        return total + (got[0:8] + got[8:16] + got[16:24])
-
-    gb[...] = lax.fori_loop(0, z.group * span, bucket, jnp.zeros((8, z.buckets), F32))
-
-
-def tail_kernel(z, keys, values, qm, dom, p16, s16, halo, stats, table, dk, dv, qh, dh, ph, sh, boff):
+
+
+def tail_kernel(z, keys, values, halo, stats, table, qh, dh, ph, sh, bases):
     tok, span = z.tok, z.span
-    split = thirds(table[...])
+    tables = [(b, s) for b in range(z.halo) for s in range(b + 1, span)]
+    rows = []
     for b in range(z.halo):
         codes = halo[b * z.rows + 2 * tok : (b + 1) * z.rows, :].astype(F32)
-        for s in range(b + 1, span):
-            boff[(b * span + s) * 8 : (b * span + s) * 8 + 8, :] = by_offset(split, codes[s : s + 1, :], z)
-
-    def each(pair, _):
-        lanes = at(pair * 128, 128)
+        rows += [codes[s : s + 1, :] for s in range(b + 1, span)]
+    slant_tables(z, table, rows, bases)
+    for pair in range(z.pairs):
+        lanes = slice(pair * 128, (pair + 1) * 128)
         for b in range(z.halo):
             top = b * z.rows
             wide = slice(b * z.wide, (b + 1) * z.wide)
             q = masked_pair(halo[top : top + tok, lanes] * jnp.asarray(z.scale, BF16), z)
             d = masked_pair(halo[top + tok : top + 2 * tok, lanes], z)
-            qh[wide, :] = q
-            dh[wide, :] = d
+            qh[pair, wide, :] = q
+            dh[pair, wide, :] = d
             u = b * z.pairs + pair
-            lse, delta = stats[0, pl.ds(u, 1), :], stats[1, pl.ds(u, 1), :]
+            lse, delta = stats[0, u : u + 1, :], stats[1, u : u + 1, :]
             for s in range(b + 1, span):
                 j = z.group + b - s
-                rows = slice(j * tok, (j + 1) * tok)
-                scores = dot(keys[rows, lanes], q, NT) + bias_rows(z, boff, (b * span + s) * 8, pair)
-                prob = jnp.exp(scores - lse)
-                dscore = prob * (dot(values[rows, lanes], d, NT) - delta)
-                ph[rows, wide] = prob.astype(BF16)
-                sh[rows, wide] = dscore.astype(BF16)
+                block = slice(j * tok, (j + 1) * tok)
+                bias = bias_rows(z, bases, tables.index((b, s)), pair)
+                prob = jnp.exp(dot(keys[block, lanes], q, NT) + bias - lse)
+                dscore = prob * (dot(values[block, lanes], d, NT) - delta)
+                ph[pair, block, wide] = prob.astype(BF16)
+                sh[pair, block, wide] = dscore.astype(BF16)
+
+
+def grad_kv_kernel(z, qm, dom, p16, s16, qh, dh, ph, sh, dk, dv):
+    tok = z.tok
+
+    def each(pair, _):
+        lanes = at(pair * 128, 128)
         for j in range(z.group):
             rows = slice(j * tok, (j + 1) * tok)
+            ext = slice((z.halo + j) * tok, (z.halo + j + 1) * tok)
             near = slice(j * z.wide, z.group * z.wide)
-            gk = dot(s16[pair, rows, near], qm[pair, near, :], NN)
+            gk = dot(s16[pair, ext, near], qm[pair, near, :], NN)
             gv = dot(p16[pair, rows, near], dom[pair, near, :], NN)
-            count = min(z.halo, j + span - z.group)
+            count = min(z.halo, j + z.span - z.group)
             if count > 0:
                 past = slice(0, count * z.wide)
-                gk = gk + dot(sh[rows, past], qh[past, :], NN)
-                gv = gv + dot(ph[rows, past], dh[past, :], NN)
+                gk = gk + dot(sh[pair, rows, past], qh[pair, past, :], NN)
+                gv = gv + dot(ph[pair, rows, past], dh[pair, past, :], NN)
             dk[rows, lanes] = gk.astype(BF16)
             dv[rows, lanes] = gv.astype(BF16)
         return 0
@@ -381,21 +414,21 @@
     lax.fori_loop(0, z.pairs, each, 0)
 
 
-def seal_kernel(z, parts, dq, dk, dv, *refs):
-    sums, sends = refs[:parts], refs[parts:]
+def seal_kernel(z, sides, dq, dk, dv, *refs):
+    sums, sends = refs[:sides], refs[sides:]
     tok = z.tok
-    total = sums[0][...]
-    for ref in sums[1:]:
-        total = total + ref[...]
-    split = thirds(total).astype(F32)
-    low = jnp.concatenate([split[16:24], jnp.zeros((8, z.buckets), F32)], axis=0)
-    rows16 = jnp.concatenate([split[0:16], low], axis=1).astype(BF16)
+    packs = []
+    for ref in sums:
+        split = thirds(ref[...]).astype(F32)
+        low = jnp.concatenate([split[16:24], jnp.zeros((8, z.buckets), F32)], axis=0)
+        packs.append(jnp.concatenate([split[0:16], low], axis=1).astype(BF16))
     me = z.me()
     for k in range(z.group):
         rows = at((me ^ k) * tok, tok)
         for n, ref in enumerate((dq, dk, dv)):
             sends[k][n * tok : (n + 1) * tok, :] = ref[rows, :]
-        sends[k][3 * tok :, :] = rows16
+        for n, pack in enumerate(packs):
+            sends[k][3 * tok + n * CODE_ROWS : 3 * tok + (n + 1) * CODE_ROWS, :] = pack
 
 
 def add_kernel(*refs):
@@ -405,21 +438,8 @@
     refs[-1][...] = total
 
 
-def collect_kernel(z, *refs):
-    got, out = refs[:-1], refs[-1]
-    me = z.me()
-    owner = lax.broadcasted_iota(jnp.int32, out.shape, 0) // z.hg
-    total = jnp.zeros(out.shape, F32)
-    for k in range(z.group):
-        rows = got[k][3 * z.tok :, :].astype(F32)
-        sums = rows[0:8, 0 : z.buckets] + rows[8:16, 0 : z.buckets] + rows[0:8, z.buckets :]
-        wide = jnp.concatenate([sums[0 : z.hg]] * (out.shape[0] // z.hg), axis=0)
-        total = total + jnp.where(owner == lax.axis_index("head") * z.group + (me ^ k), wide, 0.0)
-    out[...] = total
-
-
-def unpack_kernel(z, *refs):
-    got, outs, sem = refs[: z.group], refs[z.group : -1], refs[-1]
+def unpack_kernel(z, sides, *refs):
+    got, outs, gb, held, sem = refs[: z.group], refs[z.group : -3], refs[-3], refs[-2], refs[-1]
     me = z.me()
     copies = []
     for k in range(z.group):
@@ -429,7 +449,20 @@
             copies.append(pltpu.make_async_copy(src, out.at[:, cols], sem.at[len(copies)]))
     for copy in copies:
         copy.start()
-    for copy in copies:
+    owner = lax.broadcasted_iota(jnp.int32, held.shape, 0) // z.hg
+    total = jnp.zeros(held.shape, F32)
+    for k in range(z.group):
+        for n in range(sides):
+            top = 3 * z.tok + n * CODE_ROWS
+            rows = got[k][top : top + CODE_ROWS, :].astype(F32)
+            sums = rows[0:8, 0 : z.buckets] + rows[8:16, 0 : z.buckets] + rows[0:8, z.buckets :]
+            wide = jnp.concatenate([sums[0 : z.hg]] * (held.shape[0] // z.hg), axis=0)
+            side = lax.axis_index("head") ^ n
+            total = total + jnp.where(owner == side * z.group + (me ^ k), wide, 0.0)
+    held[...] = total
+    last = pltpu.make_async_copy(held, gb, sem.at[len(copies)])
+    last.start()
+    for copy in copies + [last]:
         copy.wait()
 
 
@@ -459,9 +492,6 @@
     def added(*terms):
         (total,) = call(add_kernel, [(terms[0].shape, terms[0].dtype)], terms)
         return total
-
-    tables = jnp.pad(bias_table.reshape(group, z.hg, buckets), ((0, 0), (0, 8 - z.hg), (0, 0)))
-    table = lax.dynamic_index_in_dim(tables, lax.axis_index("seq") % group, 0, keepdims=False)
 
     hbm = pltpu.HBM
     pack_bytes = group * (z.rows + 2 * tok) * z.cw * 2
@@ -497,8 +527,8 @@
         [((group * tok, z.cw), BF16)] * 2
         + [((near * z.pairs, tok, z.wide), F32), ((far * z.pairs, tok, z.wide), F32)]
         + [((group * CODE_ROWS, z.wide), F32)],
-        (*kv_got, table),
-        scratch=[pltpu.VMEM((group * span * 8, z.wide), F32)],
+        (*kv_got, bias_table),
+        scratch=[pltpu.VMEM((group * span * z.hg * 8, z.wide), F32)],
     )
     qm, dom, wnear, dnear, *sums = call(
         bind(near_kernel, z),
@@ -514,47 +544,54 @@
         flops=2 * far * z.pairs * unit,
     )
     stats_halo = lax.ppermute(stats, "seq", [(i, (i - group) % blocks) for i in range(blocks)])
-    p16, s16, dq, gb = call(
+    p16, s16, gb = call(
         bind(own_kernel, z),
-        [((z.pairs, group * tok, group * z.wide), BF16)] * 2
-        + [((group * tok, z.cw), BF16), ((8, buckets), F32)],
-        (own_k, kv_halo, codes, stats, fnear, ffar, wnear, dnear, wfar, dfar),
+        [
+            ((z.pairs, group * tok, group * z.wide), BF16),
+            ((z.pairs, z.ext * tok, group * z.wide), BF16),
+            ((8, buckets), F32),
+        ],
+        (codes, stats, fnear, ffar, wnear, dnear, wfar, dfar),
         scratch=[pltpu.VMEM((group * span * z.hg * 8, z.wide), F32)],
-        flops=2 * (near + far) * z.pairs * unit,
-    )
-    terms = [gb]
+    )
     by = group
     while by < blocks:
-        if len(terms) > 1:
-            terms = [added(*terms)]
-        ways = 4 if by * 2 < blocks else 2
-        terms += [swap(terms[0], by * n) for n in range(1, ways)]
-        by *= ways
+        other = swap(gb, by)
+        gb = added(gb, other)
+        by = by * 2
+    sums_of = [gb] + [swap(gb, k, "head") for k in range(1, sides)]
+    (dq,) = call(
+        bind(grad_q_kernel, z),
+        [((group * tok, z.cw), BF16)],
+        (own_k, kv_halo, s16),
+        flops=(near + far) * z.pairs * unit,
+    )
+    lanes_of = ((z.pairs, group * tok, z.halo * z.wide), BF16)
+    rows_of = ((z.pairs, z.halo * z.wide, 128), BF16)
+    halo_terms = call(
+        bind(tail_kernel, z),
+        [rows_of, rows_of, lanes_of, lanes_of],
+        (own_k, own_v, qd_halo, stats_halo, bias_table),
+        scratch=[pltpu.VMEM((far * z.hg * 8, z.wide), F32)],
+        flops=2 * far * z.pairs * unit,
+    )
     dk, dv = call(
-        bind(tail_kernel, z),
+        bind(grad_kv_kernel, z),
         [((group * tok, z.cw), BF16)] * 2,
-        (own_k, own_v, qm, dom, p16, s16, qd_halo, stats_halo, table),
-        scratch=[
-            pltpu.VMEM((z.halo * z.wide, 128), BF16),
-            pltpu.VMEM((z.halo * z.wide, 128), BF16),
-            pltpu.VMEM((group * tok, z.halo * z.wide), BF16),
-            pltpu.VMEM((group * tok, z.halo * z.wide), BF16),
-            pltpu.VMEM((z.halo * span * 8, z.wide), F32),
-        ],
-        flops=4 * far * z.pairs * unit,
-    )
-    ret = call(bind(seal_kernel, z, len(terms)), [((3 * tok + CODE_ROWS, z.cw), BF16)] * group, (dq, dk, dv, *terms))
+        (qm, dom, p16, s16, *halo_terms),
+        flops=2 * (near + far) * z.pairs * unit,
+    )
+    ret = call(
+        bind(seal_kernel, z, sides), [((3 * tok + sides * CODE_ROWS, z.cw), BF16)] * group, (dq, dk, dv, *sums_of)
+    )
     ret_got = [ret[0]] + [swap(ret[k], k) for k in range(1, group)]
-    (side,) = call(bind(collect_kernel, z), [((heads * sides, buckets), F32)], ret_got)
-    parts = [side] + [swap(side, k, "head") for k in range(1, sides)]
-    grads = call(
-        bind(unpack_kernel, z),
-        [((tok, width), BF16)] * 3,
+    return call(
+        bind(unpack_kernel, z, sides),
+        [((tok, width), BF16)] * 3 + [((heads * sides, buckets), F32)],
         ret_got,
         out_space=hbm,
-        scratch=[pltpu.SemaphoreType.DMA((3 * group,))],
-    )
-    return (*grads, sum(parts[1:], parts[0]))
+        scratch=[pltpu.VMEM((heads * sides, buckets), F32), pltpu.SemaphoreType.DMA((3 * group + 1,))],
+    )
 
 
 def solution(mesh):

time: 61.9 us -> 54.5 us (0.88)
  Pallas kernels: 22.9 us -> 12.5 us
  waiting for transfers between devices: 9.44 us -> 15.1 us
  starting transfers between devices: 27.9 us -> 25.9 us
    pallas_call x11 -> x14, Pallas kernels: 22.9 us -> 12.5 us  [call(): pl.pallas_call(kernel, out_shape=tuple((out_space(s, d) for s, d in outs)...]
    ppermute x13 -> x12, waiting for transfers between devices: 9.43 us -> 14.2 us  [swap(): lax.ppermute(value, axis, [(i, i ^ by) for i in range(lax.axis_size(axis))])]
    ppermute x1, starting transfers between devices: 4.69 us -> 2.47 us  [body(): lax.ppermute(stats, 'seq', [(i, (i - group) % blocks) for i in range(bloc...]
    ppermute x2, waiting for transfers between devices: 0.01 us -> 0.88 us  [shifted(): lax.ppermute(value, 'seq', [(i, i + by) for i in range(blocks) if 0 <= i...]
    ppermute x13 -> x12, starting transfers between devices: 18.5 us -> 18.8 us  [swap(): lax.ppermute(value, axis, [(i, i ^ by) for i in range(lax.axis_size(axis))])]
  transfers between devices with their start and end apart: 16 -> 15, of which waited for: 5 -> 6; matrix products, arithmetic and copies ran while one was open for 0% -> 0% of each run, Pallas kernels for 34% -> 19%
where the time goes in v1:
time: 54.5 us; the launch traced here: 54.3 us
  starting transfers between devices  25.9 us (48%)
  waiting for transfers between devices  15.1 us (28%)
  Pallas kernels  12.5 us (23%)
  between operations  0.77 us (1%)
    ppermute x12, starting transfers between devices, swap(): lax.ppermute(value, axis, [(i, i ^ by) for i in range(lax.axis_size(axis))])  18.8 us
    ppermute x12, waiting for transfers between devices, swap(): lax.ppermute(value, axis, [(i, i ^ by) for i in range(lax.axis_size(axis))])  14.2 us
    pallas_call x14, Pallas kernels, call(): pl.pallas_call(kernel, out_shape=tuple((out_space(s, d) for s, d in outs)...  12.5 us
    ppermute x2, starting transfers between devices, shifted(): lax.ppermute(value, 'seq', [(i, i + by) for i in range(blocks) if 0 <= i...  4.64 us
    ppermute x1, starting transfers between devices, body(): lax.ppermute(stats, 'seq', [(i, (i - group) % blocks) for i in range(bloc...  2.47 us
  transfers between devices with their start and end apart: 15, of which 6 were waited for; matrix products, arithmetic and copies ran while one was open for 0% of the time, Pallas kernels for 19%

profile of v1, /device:TPU:0, one launch (start us, length us, event | category | flops | bytes accessed | tf_op | source)
XLA Modules:
  0.0 54.3 jit_solution(5427902445152192154)
XLA Ops:
  0.6 0.0 copy-start
  0.6 1.4 %shard_map.102 = (bf16[272,256]{1,0:T(8,128)(2,1)S(1)}, bf16[272,256]{1,0:T(8,128)(2,1)S(1)}, bf16[272,256]{1,0:T(8,128)(2,1)S(1)}, bf16[272,256]{1,0:T(8,128)(2...) custom-call(bf16[128,1024]{1,0:T(8,128)(2,1)} %refs_0_.1, ...), custom_call_target="tpu_custom_call" | custom-call | bytes 1052688 | tf_op jit(solution)/shard_map/pallas_call | solution.py:34
  2.1 3.0 %collective-permute-start = (bf16[272,256]{1,0:T(8,128)(2,1)S(1)}, bf16[272,256]{1,0:T(8,128)(2,1)S(1)}, u32[]{:S(2)}, u32[]{:S(2)}) collective-permute-start(bf16[272,256]{1,0:T(8,128)(2,1)S(1)} %get-tuple-element.43), channel_id=1, source_target_pairs={{0,2},{2,0},{4,6},{6,4},{8,10},{10,8},{12,14},{14,12},{16,18},{18,... | collective-permute-start | bytes 417800 | tf_op jit(solution)/shard_map/ppermute | solution.py:487
  5.1 1.5 %collective-permute-start.1 = (bf16[272,256]{1,0:T(8,128)(2,1)S(1)}, bf16[272,256]{1,0:T(8,128)(2,1)S(1)}, u32[]{:S(2)}, u32[]{:S(2)}) collective-permute-start(bf16[272,256]{1,0:T(8,128)(2,1)S(1)} %get-tuple-element.44), channel_id=1, source_target_pairs={{0,4},{2,6},{4,0},{6,2},{8,12},{10,14},{12,8},{14,10},{16,20},{18,... | collective-permute-start | bytes 417800 | tf_op jit(solution)/shard_map/ppermute | solution.py:487
  6.6 0.0 collective-permute-start.2
  6.7 1.9 %collective-permute-start.4 = (bf16[256,256]{1,0:T(8,128)(2,1)S(1)}, bf16[256,256]{1,0:T(8,128)(2,1)S(1)}, u32[]{:S(2)}, u32[]{:S(2)}) collective-permute-start(bf16[256,256]{1,0:T(8,128)(2,1)S(1)} %get-tuple-element.49), channel_id=1, source_target_pairs={{0,2},{2,0},{4,6},{6,4},{8,10},{10,8},{12,14},{14,12},{16,18},{18,... | collective-permute-start | bytes 393224 | tf_op jit(solution)/shard_map/ppermute | solution.py:487
  8.6 1.5 %collective-permute-start.5 = (bf16[256,256]{1,0:T(8,128)(2,1)S(1)}, bf16[256,256]{1,0:T(8,128)(2,1)S(1)}, u32[]{:S(2)}, u32[]{:S(2)}) collective-permute-start(bf16[256,256]{1,0:T(8,128)(2,1)S(1)} %get-tuple-element.50), channel_id=1, source_target_pairs={{0,4},{2,6},{4,0},{6,2},{8,12},{10,14},{12,8},{14,10},{16,20},{18,... | collective-permute-start | bytes 393224 | tf_op jit(solution)/shard_map/ppermute | solution.py:487
  10.1 0.0 collective-permute-done.refs_1_.refs_5_
  10.1 2.5 %collective-permute-start.6 = (bf16[256,256]{1,0:T(8,128)(2,1)S(1)}, bf16[256,256]{1,0:T(8,128)(2,1)S(1)}, u32[]{:S(2)}, u32[]{:S(2)}) collective-permute-start(bf16[256,256]{1,0:T(8,128)(2,1)S(1)} %get-tuple-element.51), channel_id=1, source_target_pairs={{0,6},{2,4},{4,2},{6,0},{8,14},{10,12},{12,10},{14,8},{16,22},{18,... | collective-permute-start | bytes 393224 | tf_op jit(solution)/shard_map/ppermute | solution.py:487
  12.6 1.7 %collective-permute-done.1.refs_2_.refs_6_ = bf16[272,256]{1,0:T(8,128)(2,1)S(1)} collective-permute-done((bf16[272,256]{1,0:T(8,128)(2,1)S(1)}, bf16[272,256]{1,0:T(8,128)(2,1)S(1)}, u32[]{:S(2)}, u32[]{:S(2)}) %collective-permute-start.1) | collective-permute-done | bytes 139296 | tf_op jit(solution)/shard_map/ppermute | solution.py:487
  14.3 0.0 collective-permute-done.2.refs_3_.refs_7_
  14.3 3.3 %collective-permute-start.3 = (bf16[768,256]{1,0:T(8,128)(2,1)S(1)}, bf16[768,256]{1,0:T(8,128)(2,1)S(1)}, u32[]{:S(2)}, u32[]{:S(2)}) collective-permute-start(bf16[768,256]{1,0:T(8,128)(2,1)S(1)} %shard_map.104), channel_id=1, source_target_pairs={{0,8},{2,10},{4,12},{6,14},{8,16},{10,18},{12,20},{14,22},{16,24},... | collective-permute-start | bytes 1179656 | tf_op jit(solution)/shard_map/ppermute | solution.py:490
  17.7 0.0 collective-permute-done.4.refs_1_
  17.7 1.2 %collective-permute-done.5.refs_2_ = bf16[256,256]{1,0:T(8,128)(2,1)S(1)} collective-permute-done((bf16[256,256]{1,0:T(8,128)(2,1)S(1)}, bf16[256,256]{1,0:T(8,128)(2,1)S(1)}, u32[]{:S(2)}, u32[]{:S(2)}) %collective-permute-start.5) | collective-permute-done | bytes 131104 | tf_op jit(solution)/shard_map/ppermute | solution.py:487
  18.8 0.0 collective-permute-done.6.refs_3_
  18.9 1.3 %collective-permute-start.7 = (bf16[816,256]{1,0:T(8,128)(2,1)S(1)}, bf16[816,256]{1,0:T(8,128)(2,1)S(1)}, u32[]{:S(2)}, u32[]{:S(2)}) collective-permute-start(bf16[816,256]{1,0:T(8,128)(2,1)S(1)} %shard_map.109), channel_id=1, source_target_pairs={{8,0},{10,2},{12,4},{14,6},{16,8},{18,10},{20,12},{22,14},{24,16},... | collective-permute-start | bytes 1253384 | tf_op jit(solution)/shard_map/ppermute | solution.py:490
  20.2 0.0 copy-done
  20.2 1.4 %shard_map.103 = (bf16[512,256]{1,0:T(8,128)(2,1)S(1)}, bf16[512,256]{1,0:T(8,128)(2,1)S(1)}, f32[20,128,256]{2,1,0:T(8,128)S(1)}, f32[12,128,256]{2,1,0:T(8,128)S(1)}, f32[64,256]{1,0:T(8,128)S(1)}) custom-call(bf16[272,256]{1,0:T(8,128)(2,1)S(1)} %get-tuple-element.42.refs_0_.refs_4_, bf16[272,256]{1,0:T(8,128)(2,1)S(1)} %collective-permute-done.refs_1_.refs_5_, ...), custom_call_target="tpu_custom_call" | custom-call | bytes 565248 | tf_op jit(solution)/shard_map/pallas_call | solution.py:34
  21.6 1.6 %shard_map.105 = (bf16[2,1024,128]{2,1,0:T(8,128)(2,1)S(1)}, bf16[2,1024,128]{2,1,0:T(8,128)(2,1)S(1)}, f32[20,128,256]{2,1,0:T(8,128)S(1)}, f32[20,128,256]{2,1...) custom-call(bf16[256,256]{1,0:T(8,128)(2,1)S(1)} %get-tuple-element.48.refs_0_, ...), custom_call_target="tpu_custom_call" | custom-call | flops 335544320 | bytes 3670016 | tf_op jit(solution)/shard_map/pallas_call | solution.py:34
  23.2 0.9 %collective-permute-done.3.refs_0_.refs_1_ = bf16[768,256]{1,0:T(8,128)(2,1)S(1)} collective-permute-done((bf16[768,256]{1,0:T(8,128)(2,1)S(1)}, bf16[768,256]{1,0:T(8,128)(2,1)S(1)}, u32[]{:S(2)}, u32[]{:S(2)}) %collective-permute-start.3) | collective-permute-done | bytes 393248 | tf_op jit(solution)/shard_map/ppermute | solution.py:490
  24.1 1.6 %shard_map.106 = (f32[2,8,256]{2,1,0:T(8,128)S(1)}, f32[20,256]{1,0:T(8,128)S(1)}, f32[12,256]{1,0:T(8,128)S(1)}, f32[12,128,256]{2,1,0:T(8,128)S(1)}, f32[12,12...) custom-call(bf16[768,256]{1,0:T(8,128)(2,1)S(1)} %collective-permute-done.3.refs_0_.refs_1_, ...), custom_call_target="tpu_custom_call" | custom-call | flops 201326592 | bytes 3076096 | tf_op jit(solution)/shard_map/pallas_call | solution.py:34
  25.7 2.2 %shard_map.107 = (bf16[2,512,1024]{2,1,0:T(8,128)(2,1)S(1)}, bf16[2,896,1024]{2,1,0:T(8,128)(2,1)S(1)}, f32[8,128]{1,0:T(8,128)S(1)}) custom-call(f32[64,256]{1,0:T(8,128)S(1)} %get-tuple-element.47.refs_0_, f32[2,8,256]{2,1,0:T(8,128)S(1)} %get-tuple-element.60.refs_1_, f32[20,256]{1,0:T(8,128)S(1)} %get-tuple-element.61.refs_2_, ...), custom_call_target="tpu_custom_call" | custom-call | bytes 8503296 | tf_op jit(solution)/shard_map/pallas_call | solution.py:34
  27.8 2.5 %collective-permute-start.9 = (f32[8,128]{1,0:T(8,128)S(1)}, f32[8,128]{1,0:T(8,128)S(1)}, u32[]{:S(2)}, u32[]{:S(2)}) collective-permute-start(f32[8,128]{1,0:T(8,128)S(1)} %get-tuple-element.75.refs_0_), channel_id=1, source_target_pairs={{0,8},{2,10},{4,12},{6,14},{8,0},{10,2},{12,4},{14,6},{16,24},{18,... | collective-permute-start | bytes 12296 | tf_op jit(solution)/shard_map/ppermute | solution.py:487
  30.4 2.5 %collective-permute-start.8 = (f32[2,8,256]{2,1,0:T(8,128)S(1)}, f32[2,8,256]{2,1,0:T(8,128)S(1)}, u32[]{:S(2)}, u32[]{:S(2)}) collective-permute-start(f32[2,8,256]{2,1,0:T(8,128)S(1)} %get-tuple-element.60.refs_1_), channel_id=1, source_target_pairs={{0,24},{2,26},{4,28},{6,30},{8,0},{10,2},{12,4},{14,6},{16,8},{18,... | collective-permute-start | bytes 49160 | tf_op jit(solution)/shard_map/ppermute | solution.py:546
  32.8 0.0 collective-permute-done.9.refs_1_
  32.8 2.1 %collective-permute-start.10 = (f32[8,128]{1,0:T(8,128)S(1)}, f32[8,128]{1,0:T(8,128)S(1)}, u32[]{:S(2)}, u32[]{:S(2)}) collective-permute-start(f32[8,128]{1,0:T(8,128)S(1)} %shard_map.112.refs_0_), channel_id=1, source_target_pairs={{0,16},{2,18},{4,20},{6,22},{8,24},{10,26},{12,28},{14,30},{16,0},... | collective-permute-start | bytes 12296 | tf_op jit(solution)/shard_map/ppermute | solution.py:487
  35.0 0.8 %shard_map.108.refs_0_ = bf16[512,256]{1,0:T(8,128)(2,1)S(1)} custom-call(bf16[512,256]{1,0:T(8,128)(2,1)S(1)} %get-tuple-element.46.refs_4_.refs_0_, bf16[768,256]{1,0:T(8,128)(2,1)S(1)} %collective-permute-done.3.refs_0_.refs_1_, bf16[2,896,1024]{2,1,0:T(8,128)(2,1)S(1)} %get-tuple-element.67.refs_2_.refs_3_), custom_call_target="tpu_custom_call" | custom-call | flops 268435456 | bytes 4325376 | tf_op jit(solution)/shard_map/pallas_call | solution.py:34
  35.8 1.5 %collective-permute-done.10.refs_1_ = f32[8,128]{1,0:T(8,128)S(1)} collective-permute-done((f32[8,128]{1,0:T(8,128)S(1)}, f32[8,128]{1,0:T(8,128)S(1)}, u32[]{:S(2)}, u32[]{:S(2)}) %collective-permute-start.10) | collective-permute-done | bytes 4128 | tf_op jit(solution)/shard_map/ppermute | solution.py:487
  37.4 0.0 collective-permute-start.11
  37.4 0.0 collective-permute-done.8.refs_3_
  37.4 0.0 collective-permute-done.7.refs_2_
  37.4 1.0 %shard_map.110 = (bf16[2,768,128]{2,1,0:T(8,128)(2,1)S(1)}, bf16[2,768,128]{2,1,0:T(8,128)(2,1)S(1)}, bf16[2,512,768]{2,1,0:T(8,128)(2,1)S(1)}, bf16[2,512,768]{2,1,0:T(8,128)(2,1)S(1)}) custom-call(bf16[512,256]{1,0:T(8,128)(2,1)S(1)} %get-tuple-element.46.refs_4_.refs_0_, bf16[512,256]{1,0:T(8,128)(2,1)S(1)} %get-tuple-element.52.refs_5_.refs_1_, ...), custom_call_target="tpu_custom_call" | custom-call | flops 201326592 | bytes 966656 | tf_op jit(solution)/shard_map/pallas_call | solution.py:34
  38.4 1.5 %shard_map.111 = (bf16[512,256]{1,0:T(8,128)(2,1)S(1)}, bf16[512,256]{1,0:T(8,128)(2,1)S(1)}) custom-call(bf16[2,1024,128]{2,1,0:T(8,128)(2,1)S(1)} %get-tuple-element.54.refs_1_.refs_0_, bf16[2,1024,128]{2,1,0:T(8,128)(2,1)S(1)} %get-tuple-element.55.refs_2_.refs_1_, bf16[2,512,1024]{2,1,0:T(8,128)(2,1)S(1)} %get-tuple-element.68.refs_2_, ...), custom_call_target="tpu_custom_call" | custom-call | flops 536870912 | bytes 10747904 | tf_op jit(solution)/shard_map/pallas_call | solution.py:34
  39.8 0.0 collective-permute-done.11.refs_4_
  39.8 0.1 shard_map.114
  39.9 1.5 %collective-permute-start.12 = (bf16[416,256]{1,0:T(8,128)(2,1)S(1)}, bf16[416,256]{1,0:T(8,128)(2,1)S(1)}, u32[]{:S(2)}, u32[]{:S(2)}) collective-permute-start(bf16[416,256]{1,0:T(8,128)(2,1)S(1)} %get-tuple-element.77), channel_id=1, source_target_pairs={{0,2},{2,0},{4,6},{6,4},{8,10},{10,8},{12,14},{14,12},{16,18},{18,... | collective-permute-start | bytes 638984 | tf_op jit(solution)/shard_map/ppermute | solution.py:487
  41.4 0.5 collective-permute-start.13
  41.9 1.6 %collective-permute-start.14 = (bf16[416,256]{1,0:T(8,128)(2,1)S(1)}, bf16[416,256]{1,0:T(8,128)(2,1)S(1)}, u32[]{:S(2)}, u32[]{:S(2)}) collective-permute-start(bf16[416,256]{1,0:T(8,128)(2,1)S(1)} %get-tuple-element.79), channel_id=1, source_target_pairs={{0,6},{2,4},{4,2},{6,0},{8,14},{10,12},{12,10},{14,8},{16,22},{18,... | collective-permute-start | bytes 638984 | tf_op jit(solution)/shard_map/ppermute | solution.py:487
  43.5 4.6 %collective-permute-done.12.refs_1_ = bf16[416,256]{1,0:T(8,128)(2,1)S(1)} collective-permute-done((bf16[416,256]{1,0:T(8,128)(2,1)S(1)}, bf16[416,256]{1,0:T(8,128)(2,1)S(1)}, u32[]{:S(2)}, u32[]{:S(2)}) %collective-permute-start.12) | collective-permute-done | bytes 213024 | tf_op jit(solution)/shard_map/ppermute | solution.py:487
  48.1 5.2 %collective-permute-done.13.refs_2_ = bf16[416,256]{1,0:T(8,128)(2,1)S(1)} collective-permute-done((bf16[416,256]{1,0:T(8,128)(2,1)S(1)}, bf16[416,256]{1,0:T(8,128)(2,1)S(1)}, u32[]{:S(2)}, u32[]{:S(2)}) %collective-permute-start.13) | collective-permute-done | bytes 213024 | tf_op jit(solution)/shard_map/ppermute | solution.py:487
  53.3 0.0 collective-permute-done.14.refs_3_
  53.3 1.0 %shard_map.115 = (bf16[128,1024]{1,0:T(8,128)(2,1)}, bf16[128,1024]{1,0:T(8,128)(2,1)}, bf16[128,1024]{1,0:T(8,128)(2,1)}, f32[32,128]{1,0:T(8,128)}) custom-call(bf16[416,256]{1,0:T(8,128)(2,1)S(1)} %get-tuple-element.76.refs_0_, bf16[416,256]{1,0:T(8,128)(2,1)S(1)} %collective-permute-done.12.refs_1_, ...), custom_call_target="tpu_custom_call" | custom-call | bytes 851968 | tf_op jit(solution)/shard_map/pallas_call | solution.py:34
  (4 shorter events, 0.1 us)
Async XLA Ops:
  0.6 19.6 %copy-start = (f32[16,128]{1,0:T(8,128)S(1)}, f32[16,128]{1,0:T(8,128)}, u32[]{:S(2)}) copy-start(f32[16,128]{1,0:T(8,128)} %refs_4_.5) | copy-start | bytes 24580
  2.1 8.0 %collective-permute-start = (bf16[272,256]{1,0:T(8,128)(2,1)S(1)}, bf16[272,256]{1,0:T(8,128)(2,1)S(1)}, u32[]{:S(2)}, u32[]{:S(2)}) collective-permute-start(bf16[272,256]{1,0:T(8,128)(2,1)S(1)} %get-tuple-element.43), channel_id=1, source_target_pairs={{0,2},{2,0},{4,6},{6,4},{8,10},{10,8},{12,14},{14,12},{16,18},{18,... | collective-permute-start | bytes 417800 | tf_op jit(solution)/shard_map/ppermute | solution.py:487
  5.1 9.2 %collective-permute-start.1 = (bf16[272,256]{1,0:T(8,128)(2,1)S(1)}, bf16[272,256]{1,0:T(8,128)(2,1)S(1)}, u32[]{:S(2)}, u32[]{:S(2)}) collective-permute-start(bf16[272,256]{1,0:T(8,128)(2,1)S(1)} %get-tuple-element.44), channel_id=1, source_target_pairs={{0,4},{2,6},{4,0},{6,2},{8,12},{10,14},{12,8},{14,10},{16,20},{18,... | collective-permute-start | bytes 417800 | tf_op jit(solution)/shard_map/ppermute | solution.py:487
  6.6 7.6 %collective-permute-start.2 = (bf16[272,256]{1,0:T(8,128)(2,1)S(1)}, bf16[272,256]{1,0:T(8,128)(2,1)S(1)}, u32[]{:S(2)}, u32[]{:S(2)}) collective-permute-start(bf16[272,256]{1,0:T(8,128)(2,1)S(1)} %get-tuple-element.45), channel_id=1, source_target_pairs={{0,6},{2,4},{4,2},{6,0},{8,14},{10,12},{12,10},{14,8},{16,22},{18,... | collective-permute-start | bytes 417800 | tf_op jit(solution)/shard_map/ppermute | solution.py:487
  6.7 11.0 %collective-permute-start.4 = (bf16[256,256]{1,0:T(8,128)(2,1)S(1)}, bf16[256,256]{1,0:T(8,128)(2,1)S(1)}, u32[]{:S(2)}, u32[]{:S(2)}) collective-permute-start(bf16[256,256]{1,0:T(8,128)(2,1)S(1)} %get-tuple-element.49), channel_id=1, source_target_pairs={{0,2},{2,0},{4,6},{6,4},{8,10},{10,8},{12,14},{14,12},{16,18},{18,... | collective-permute-start | bytes 393224 | tf_op jit(solution)/shard_map/ppermute | solution.py:487
  8.6 10.2 %collective-permute-start.5 = (bf16[256,256]{1,0:T(8,128)(2,1)S(1)}, bf16[256,256]{1,0:T(8,128)(2,1)S(1)}, u32[]{:S(2)}, u32[]{:S(2)}) collective-permute-start(bf16[256,256]{1,0:T(8,128)(2,1)S(1)} %get-tuple-element.50), channel_id=1, source_target_pairs={{0,4},{2,6},{4,0},{6,2},{8,12},{10,14},{12,8},{14,10},{16,20},{18,... | collective-permute-start | bytes 393224 | tf_op jit(solution)/shard_map/ppermute | solution.py:487
  10.1 8.7 %collective-permute-start.6 = (bf16[256,256]{1,0:T(8,128)(2,1)S(1)}, bf16[256,256]{1,0:T(8,128)(2,1)S(1)}, u32[]{:S(2)}, u32[]{:S(2)}) collective-permute-start(bf16[256,256]{1,0:T(8,128)(2,1)S(1)} %get-tuple-element.51), channel_id=1, source_target_pairs={{0,6},{2,4},{4,2},{6,0},{8,14},{10,12},{12,10},{14,8},{16,22},{18,... | collective-permute-start | bytes 393224 | tf_op jit(solution)/shard_map/ppermute | solution.py:487
  14.3 9.8 %collective-permute-start.3 = (bf16[768,256]{1,0:T(8,128)(2,1)S(1)}, bf16[768,256]{1,0:T(8,128)(2,1)S(1)}, u32[]{:S(2)}, u32[]{:S(2)}) collective-permute-start(bf16[768,256]{1,0:T(8,128)(2,1)S(1)} %shard_map.104), channel_id=1, source_target_pairs={{0,8},{2,10},{4,12},{6,14},{8,16},{10,18},{12,20},{14,22},{16,24},... | collective-permute-start | bytes 1179656 | tf_op jit(solution)/shard_map/ppermute | solution.py:490
  18.9 18.5 %collective-permute-start.7 = (bf16[816,256]{1,0:T(8,128)(2,1)S(1)}, bf16[816,256]{1,0:T(8,128)(2,1)S(1)}, u32[]{:S(2)}, u32[]{:S(2)}) collective-permute-start(bf16[816,256]{1,0:T(8,128)(2,1)S(1)} %shard_map.109), channel_id=1, source_target_pairs={{8,0},{10,2},{12,4},{14,6},{16,8},{18,10},{20,12},{22,14},{24,16},... | collective-permute-start | bytes 1253384 | tf_op jit(solution)/shard_map/ppermute | solution.py:490
  27.8 5.0 %collective-permute-start.9 = (f32[8,128]{1,0:T(8,128)S(1)}, f32[8,128]{1,0:T(8,128)S(1)}, u32[]{:S(2)}, u32[]{:S(2)}) collective-permute-start(f32[8,128]{1,0:T(8,128)S(1)} %get-tuple-element.75.refs_0_), channel_id=1, source_target_pairs={{0,8},{2,10},{4,12},{6,14},{8,0},{10,2},{12,4},{14,6},{16,24},{18,... | collective-permute-start | bytes 12296 | tf_op jit(solution)/shard_map/ppermute | solution.py:487
  30.4 7.0 %collective-permute-start.8 = (f32[2,8,256]{2,1,0:T(8,128)S(1)}, f32[2,8,256]{2,1,0:T(8,128)S(1)}, u32[]{:S(2)}, u32[]{:S(2)}) collective-permute-start(f32[2,8,256]{2,1,0:T(8,128)S(1)} %get-tuple-element.60.refs_1_), channel_id=1, source_target_pairs={{0,24},{2,26},{4,28},{6,30},{8,0},{10,2},{12,4},{14,6},{16,8},{18,... | collective-permute-start | bytes 49160 | tf_op jit(solution)/shard_map/ppermute | solution.py:546
  32.8 4.5 %collective-permute-start.10 = (f32[8,128]{1,0:T(8,128)S(1)}, f32[8,128]{1,0:T(8,128)S(1)}, u32[]{:S(2)}, u32[]{:S(2)}) collective-permute-start(f32[8,128]{1,0:T(8,128)S(1)} %shard_map.112.refs_0_), channel_id=1, source_target_pairs={{0,16},{2,18},{4,20},{6,22},{8,24},{10,26},{12,28},{14,30},{16,0},... | collective-permute-start | bytes 12296 | tf_op jit(solution)/shard_map/ppermute | solution.py:487
  37.4 2.5 %collective-permute-start.11 = (f32[8,128]{1,0:T(8,128)S(1)}, f32[8,128]{1,0:T(8,128)S(1)}, u32[]{:S(2)}, u32[]{:S(2)}) collective-permute-start(f32[8,128]{1,0:T(8,128)S(1)} %shard_map.113.refs_3_), channel_id=1, source_target_pairs={{0,1},{1,0},{2,3},{3,2},{4,5},{5,4},{6,7},{7,6},{8,9},{9,8},{10,11... | collective-permute-start | bytes 12296 | tf_op jit(solution)/shard_map/ppermute | solution.py:487
  39.9 8.2 %collective-permute-start.12 = (bf16[416,256]{1,0:T(8,128)(2,1)S(1)}, bf16[416,256]{1,0:T(8,128)(2,1)S(1)}, u32[]{:S(2)}, u32[]{:S(2)}) collective-permute-start(bf16[416,256]{1,0:T(8,128)(2,1)S(1)} %get-tuple-element.77), channel_id=1, source_target_pairs={{0,2},{2,0},{4,6},{6,4},{8,10},{10,8},{12,14},{14,12},{16,18},{18,... | collective-permute-start | bytes 638984 | tf_op jit(solution)/shard_map/ppermute | solution.py:487
  41.4 11.9 %collective-permute-start.13 = (bf16[416,256]{1,0:T(8,128)(2,1)S(1)}, bf16[416,256]{1,0:T(8,128)(2,1)S(1)}, u32[]{:S(2)}, u32[]{:S(2)}) collective-permute-start(bf16[416,256]{1,0:T(8,128)(2,1)S(1)} %get-tuple-element.78), channel_id=1, source_target_pairs={{0,4},{2,6},{4,0},{6,2},{8,12},{10,14},{12,8},{14,10},{16,20},{18,... | collective-permute-start | bytes 638984 | tf_op jit(solution)/shard_map/ppermute | solution.py:487
  41.9 11.4 %collective-permute-start.14 = (bf16[416,256]{1,0:T(8,128)(2,1)S(1)}, bf16[416,256]{1,0:T(8,128)(2,1)S(1)}, u32[]{:S(2)}, u32[]{:S(2)}) collective-permute-start(bf16[416,256]{1,0:T(8,128)(2,1)S(1)} %get-tuple-element.79), channel_id=1, source_target_pairs={{0,6},{2,4},{4,2},{6,0},{8,14},{10,12},{12,10},{14,8},{16,22},{18,... | collective-permute-start | bytes 638984 | tf_op jit(solution)/shard_map/ppermute | solution.py:487

commit v2 on v1

--- a/solution.py
+++ b/solution.py
@@ -362,7 +362,7 @@
     lax.fori_loop(0, z.pairs, each, 0)
 
 
-def tail_kernel(z, keys, values, halo, stats, table, qh, dh, ph, sh, bases):
+def tail_kernel(z, keys, values, halo, even, odd, table, qh, dh, ph, sh, bases):
     tok, span = z.tok, z.span
     tables = [(b, s) for b in range(z.halo) for s in range(b + 1, span)]
     rows = []
@@ -370,6 +370,7 @@
         codes = halo[b * z.rows + 2 * tok : (b + 1) * z.rows, :].astype(F32)
         rows += [codes[s : s + 1, :] for s in range(b + 1, span)]
     slant_tables(z, table, rows, bases)
+    second = lax.rem(lax.div(lax.axis_index("seq"), z.group), 2) == 1
     for pair in range(z.pairs):
         lanes = slice(pair * 128, (pair + 1) * 128)
         for b in range(z.halo):
@@ -380,7 +381,7 @@
             qh[pair, wide, :] = q
             dh[pair, wide, :] = d
             u = b * z.pairs + pair
-            lse, delta = stats[0, u : u + 1, :], stats[1, u : u + 1, :]
+            lse, delta = (jnp.where(second, odd[n, u : u + 1, :], even[n, u : u + 1, :]) for n in range(2))
             for s in range(b + 1, span):
                 j = z.group + b - s
                 block = slice(j * tok, (j + 1) * tok)
@@ -489,6 +490,14 @@
     def shifted(value, by):
         return lax.ppermute(value, "seq", [(i, i + by) for i in range(blocks) if 0 <= i + by < blocks])
 
+    def neighbours(first):
+        pairs = []
+        for i in range(blocks):
+            g = (i // group - first) ^ 1
+            g = g + first if i // group >= first else i // group
+            pairs.append((i, i if g * group >= blocks else g * group + i % group))
+        return pairs
+
     def added(*terms):
         (total,) = call(add_kernel, [(terms[0].shape, terms[0].dtype)], terms)
         return total
@@ -543,7 +552,7 @@
         (kv_halo, qm, dom, bias_far, *sums),
         flops=2 * far * z.pairs * unit,
     )
-    stats_halo = lax.ppermute(stats, "seq", [(i, (i - group) % blocks) for i in range(blocks)])
+    stats_halo = [lax.ppermute(stats, "seq", neighbours(n)) for n in range(2)]
     p16, s16, gb = call(
         bind(own_kernel, z),
         [
@@ -571,7 +580,7 @@
     halo_terms = call(
         bind(tail_kernel, z),
         [rows_of, rows_of, lanes_of, lanes_of],
-        (own_k, own_v, qd_halo, stats_halo, bias_table),
+        (own_k, own_v, qd_halo, *stats_halo, bias_table),
         scratch=[pltpu.VMEM((far * z.hg * 8, z.wide), F32)],
         flops=2 * far * z.pairs * unit,
     )

time: 54.5 us -> 57.2 us (1.050)
  waiting for transfers between devices: 15.1 us -> 17.3 us
    ppermute x1 -> x2, starting transfers between devices: 2.47 us -> 5.11 us  [body(): stats_halo = [lax.ppermute(stats, 'seq', neighbours(n)) for n in range(2)]]
    ppermute x12, starting transfers between devices: 18.8 us -> 16.6 us  [swap(): lax.ppermute(value, axis, [(i, i ^ by) for i in range(lax.axis_size(axis))])]
    ppermute x12, waiting for transfers between devices: 14.2 us -> 16.4 us  [swap(): lax.ppermute(value, axis, [(i, i ^ by) for i in range(lax.axis_size(axis))])]
  transfers between devices with their start and end apart: 15 -> 16, of which waited for: 6 -> 6; matrix products, arithmetic and copies ran while one was open for 0% -> 0% of each run, Pallas kernels for 19% -> 18%
where the time goes in v2:
time: 57.2 us; the launch traced here: 57 us
  starting transfers between devices  26.4 us (46%)
  waiting for transfers between devices  17.3 us (30%)
  Pallas kernels  12.5 us (22%)
  between operations  0.79 us (1%)
    ppermute x12, starting transfers between devices, swap(): lax.ppermute(value, axis, [(i, i ^ by) for i in range(lax.axis_size(axis))])  16.6 us
    ppermute x12, waiting for transfers between devices, swap(): lax.ppermute(value, axis, [(i, i ^ by) for i in range(lax.axis_size(axis))])  16.4 us
    pallas_call x14, Pallas kernels, call(): pl.pallas_call(kernel, out_shape=tuple((out_space(s, d) for s, d in outs)...  12.5 us
    ppermute x2, starting transfers between devices, body(): stats_halo = [lax.ppermute(stats, 'seq', neighbours(n)) for n in range(2)]  5.11 us
    ppermute x2, starting transfers between devices, shifted(): lax.ppermute(value, 'seq', [(i, i + by) for i in range(blocks) if 0 <= i...  4.64 us
  transfers between devices with their start and end apart: 16, of which 6 were waited for; matrix products, arithmetic and copies ran while one was open for 0% of the time, Pallas kernels for 18%

profile of v2, /device:TPU:0, one launch (start us, length us, event | category | flops | bytes accessed | tf_op | source)
XLA Modules:
  0.0 57.0 jit_solution(7271341978082192744)
XLA Ops:
  0.6 0.0 copy-start
  0.6 1.4 %shard_map.102 = (bf16[272,256]{1,0:T(8,128)(2,1)S(1)}, bf16[272,256]{1,0:T(8,128)(2,1)S(1)}, bf16[272,256]{1,0:T(8,128)(2,1)S(1)}, bf16[272,256]{1,0:T(8,128)(2...) custom-call(bf16[128,1024]{1,0:T(8,128)(2,1)} %refs_0_.1, ...), custom_call_target="tpu_custom_call" | custom-call | bytes 1052688 | tf_op jit(solution)/shard_map/pallas_call | solution.py:34
  2.1 3.0 %collective-permute-start = (bf16[272,256]{1,0:T(8,128)(2,1)S(1)}, bf16[272,256]{1,0:T(8,128)(2,1)S(1)}, u32[]{:S(2)}, u32[]{:S(2)}) collective-permute-start(bf16[272,256]{1,0:T(8,128)(2,1)S(1)} %get-tuple-element.43), channel_id=1, source_target_pairs={{0,2},{2,0},{4,6},{6,4},{8,10},{10,8},{12,14},{14,12},{16,18},{18,... | collective-permute-start | bytes 417800 | tf_op jit(solution)/shard_map/ppermute | solution.py:488
  5.1 1.5 %collective-permute-start.1 = (bf16[272,256]{1,0:T(8,128)(2,1)S(1)}, bf16[272,256]{1,0:T(8,128)(2,1)S(1)}, u32[]{:S(2)}, u32[]{:S(2)}) collective-permute-start(bf16[272,256]{1,0:T(8,128)(2,1)S(1)} %get-tuple-element.44), channel_id=1, source_target_pairs={{0,4},{2,6},{4,0},{6,2},{8,12},{10,14},{12,8},{14,10},{16,20},{18,... | collective-permute-start | bytes 417800 | tf_op jit(solution)/shard_map/ppermute | solution.py:488
  6.6 0.0 collective-permute-start.2
  6.7 1.9 %collective-permute-start.4 = (bf16[256,256]{1,0:T(8,128)(2,1)S(1)}, bf16[256,256]{1,0:T(8,128)(2,1)S(1)}, u32[]{:S(2)}, u32[]{:S(2)}) collective-permute-start(bf16[256,256]{1,0:T(8,128)(2,1)S(1)} %get-tuple-element.49), channel_id=1, source_target_pairs={{0,2},{2,0},{4,6},{6,4},{8,10},{10,8},{12,14},{14,12},{16,18},{18,... | collective-permute-start | bytes 393224 | tf_op jit(solution)/shard_map/ppermute | solution.py:488
  8.6 1.5 %collective-permute-start.5 = (bf16[256,256]{1,0:T(8,128)(2,1)S(1)}, bf16[256,256]{1,0:T(8,128)(2,1)S(1)}, u32[]{:S(2)}, u32[]{:S(2)}) collective-permute-start(bf16[256,256]{1,0:T(8,128)(2,1)S(1)} %get-tuple-element.50), channel_id=1, source_target_pairs={{0,4},{2,6},{4,0},{6,2},{8,12},{10,14},{12,8},{14,10},{16,20},{18,... | collective-permute-start | bytes 393224 | tf_op jit(solution)/shard_map/ppermute | solution.py:488
  10.1 0.0 collective-permute-done.refs_1_.refs_5_
  10.1 2.5 %collective-permute-start.6 = (bf16[256,256]{1,0:T(8,128)(2,1)S(1)}, bf16[256,256]{1,0:T(8,128)(2,1)S(1)}, u32[]{:S(2)}, u32[]{:S(2)}) collective-permute-start(bf16[256,256]{1,0:T(8,128)(2,1)S(1)} %get-tuple-element.51), channel_id=1, source_target_pairs={{0,6},{2,4},{4,2},{6,0},{8,14},{10,12},{12,10},{14,8},{16,22},{18,... | collective-permute-start | bytes 393224 | tf_op jit(solution)/shard_map/ppermute | solution.py:488
  12.6 1.7 %collective-permute-done.1.refs_2_.refs_6_ = bf16[272,256]{1,0:T(8,128)(2,1)S(1)} collective-permute-done((bf16[272,256]{1,0:T(8,128)(2,1)S(1)}, bf16[272,256]{1,0:T(8,128)(2,1)S(1)}, u32[]{:S(2)}, u32[]{:S(2)}) %collective-permute-start.1) | collective-permute-done | bytes 139296 | tf_op jit(solution)/shard_map/ppermute | solution.py:488
  14.3 0.0 collective-permute-done.2.refs_3_.refs_7_
  14.3 3.3 %collective-permute-start.3 = (bf16[768,256]{1,0:T(8,128)(2,1)S(1)}, bf16[768,256]{1,0:T(8,128)(2,1)S(1)}, u32[]{:S(2)}, u32[]{:S(2)}) collective-permute-start(bf16[768,256]{1,0:T(8,128)(2,1)S(1)} %shard_map.104), channel_id=1, source_target_pairs={{0,8},{2,10},{4,12},{6,14},{8,16},{10,18},{12,20},{14,22},{16,24},... | collective-permute-start | bytes 1179656 | tf_op jit(solution)/shard_map/ppermute | solution.py:491
  17.7 0.0 collective-permute-done.4.refs_1_
  17.7 1.2 %collective-permute-done.5.refs_2_ = bf16[256,256]{1,0:T(8,128)(2,1)S(1)} collective-permute-done((bf16[256,256]{1,0:T(8,128)(2,1)S(1)}, bf16[256,256]{1,0:T(8,128)(2,1)S(1)}, u32[]{:S(2)}, u32[]{:S(2)}) %collective-permute-start.5) | collective-permute-done | bytes 131104 | tf_op jit(solution)/shard_map/ppermute | solution.py:488
  18.8 0.0 collective-permute-done.6.refs_3_
  18.9 1.3 %collective-permute-start.7 = (bf16[816,256]{1,0:T(8,128)(2,1)S(1)}, bf16[816,256]{1,0:T(8,128)(2,1)S(1)}, u32[]{:S(2)}, u32[]{:S(2)}) collective-permute-start(bf16[816,256]{1,0:T(8,128)(2,1)S(1)} %shard_map.109), channel_id=1, source_target_pairs={{8,0},{10,2},{12,4},{14,6},{16,8},{18,10},{20,12},{22,14},{24,16},... | collective-permute-start | bytes 1253384 | tf_op jit(solution)/shard_map/ppermute | solution.py:491
  20.2 0.0 copy-done
  20.2 1.4 %shard_map.103 = (bf16[512,256]{1,0:T(8,128)(2,1)S(1)}, bf16[512,256]{1,0:T(8,128)(2,1)S(1)}, f32[20,128,256]{2,1,0:T(8,128)S(1)}, f32[12,128,256]{2,1,0:T(8,128)S(1)}, f32[64,256]{1,0:T(8,128)S(1)}) custom-call(bf16[272,256]{1,0:T(8,128)(2,1)S(1)} %get-tuple-element.42.refs_0_.refs_4_, bf16[272,256]{1,0:T(8,128)(2,1)S(1)} %collective-permute-done.refs_1_.refs_5_, ...), custom_call_target="tpu_custom_call" | custom-call | bytes 565248 | tf_op jit(solution)/shard_map/pallas_call | solution.py:34
  21.6 1.6 %shard_map.105 = (bf16[2,1024,128]{2,1,0:T(8,128)(2,1)S(1)}, bf16[2,1024,128]{2,1,0:T(8,128)(2,1)S(1)}, f32[20,128,256]{2,1,0:T(8,128)S(1)}, f32[20,128,256]{2,1...) custom-call(bf16[256,256]{1,0:T(8,128)(2,1)S(1)} %get-tuple-element.48.refs_0_, ...), custom_call_target="tpu_custom_call" | custom-call | flops 335544320 | bytes 3670016 | tf_op jit(solution)/shard_map/pallas_call | solution.py:34
  23.2 0.9 %collective-permute-done.3.refs_0_.refs_1_ = bf16[768,256]{1,0:T(8,128)(2,1)S(1)} collective-permute-done((bf16[768,256]{1,0:T(8,128)(2,1)S(1)}, bf16[768,256]{1,0:T(8,128)(2,1)S(1)}, u32[]{:S(2)}, u32[]{:S(2)}) %collective-permute-start.3) | collective-permute-done | bytes 393248 | tf_op jit(solution)/shard_map/ppermute | solution.py:491
  24.1 1.6 %shard_map.106 = (f32[2,8,256]{2,1,0:T(8,128)S(1)}, f32[20,256]{1,0:T(8,128)S(1)}, f32[12,256]{1,0:T(8,128)S(1)}, f32[12,128,256]{2,1,0:T(8,128)S(1)}, f32[12,12...) custom-call(bf16[768,256]{1,0:T(8,128)(2,1)S(1)} %collective-permute-done.3.refs_0_.refs_1_, ...), custom_call_target="tpu_custom_call" | custom-call | flops 201326592 | bytes 3076096 | tf_op jit(solution)/shard_map/pallas_call | solution.py:34
  25.7 2.2 %shard_map.107 = (bf16[2,512,1024]{2,1,0:T(8,128)(2,1)S(1)}, bf16[2,896,1024]{2,1,0:T(8,128)(2,1)S(1)}, f32[8,128]{1,0:T(8,128)S(1)}) custom-call(f32[64,256]{1,0:T(8,128)S(1)} %get-tuple-element.47.refs_0_, f32[2,8,256]{2,1,0:T(8,128)S(1)} %get-tuple-element.60.refs_1_, f32[20,256]{1,0:T(8,128)S(1)} %get-tuple-element.61.refs_2_, ...), custom_call_target="tpu_custom_call" | custom-call | bytes 8503296 | tf_op jit(solution)/shard_map/pallas_call | solution.py:34
  27.8 2.5 %collective-permute-start.10 = (f32[8,128]{1,0:T(8,128)S(1)}, f32[8,128]{1,0:T(8,128)S(1)}, u32[]{:S(2)}, u32[]{:S(2)}) collective-permute-start(f32[8,128]{1,0:T(8,128)S(1)} %get-tuple-element.75.refs_0_), channel_id=1, source_target_pairs={{0,8},{2,10},{4,12},{6,14},{8,0},{10,2},{12,4},{14,6},{16,24},{18,... | collective-permute-start | bytes 12296 | tf_op jit(solution)/shard_map/ppermute | solution.py:488
  30.4 0.7 %collective-permute-start.9 = (f32[2,8,256]{2,1,0:T(8,128)S(1)}, f32[2,8,256]{2,1,0:T(8,128)S(1)}, u32[]{:S(2)}, u32[]{:S(2)}) collective-permute-start(f32[2,8,256]{2,1,0:T(8,128)S(1)} %get-tuple-element.60.refs_1_), channel_id=1, source_target_pairs={{0,0},{2,2},{4,4},{6,6},{8,16},{10,18},{12,20},{14,22},{16,8},{18,... | collective-permute-start | bytes 49160 | tf_op jit(solution)/shard_map/ppermute | solution.py:555
  31.0 4.5 %collective-permute-start.8 = (f32[2,8,256]{2,1,0:T(8,128)S(1)}, f32[2,8,256]{2,1,0:T(8,128)S(1)}, u32[]{:S(2)}, u32[]{:S(2)}) collective-permute-start(f32[2,8,256]{2,1,0:T(8,128)S(1)} %get-tuple-element.60.refs_1_), channel_id=1, source_target_pairs={{0,8},{2,10},{4,12},{6,14},{8,0},{10,2},{12,4},{14,6},{16,24},{18,... | collective-permute-start | bytes 49160 | tf_op jit(solution)/shard_map/ppermute | solution.py:555
  35.5 0.0 collective-permute-done.10.refs_1_
  35.5 0.0 collective-permute-start.11
  35.5 0.8 %shard_map.108.refs_0_ = bf16[512,256]{1,0:T(8,128)(2,1)S(1)} custom-call(bf16[512,256]{1,0:T(8,128)(2,1)S(1)} %get-tuple-element.46.refs_4_.refs_0_, bf16[768,256]{1,0:T(8,128)(2,1)S(1)} %collective-permute-done.3.refs_0_.refs_1_, bf16[2,896,1024]{2,1,0:T(8,128)(2,1)S(1)} %get-tuple-element.67.refs_2_.refs_3_), custom_call_target="tpu_custom_call" | custom-call | flops 268435456 | bytes 4325376 | tf_op jit(solution)/shard_map/pallas_call | solution.py:34
  36.3 3.7 %collective-permute-done.11.refs_1_ = f32[8,128]{1,0:T(8,128)S(1)} collective-permute-done((f32[8,128]{1,0:T(8,128)S(1)}, f32[8,128]{1,0:T(8,128)S(1)}, u32[]{:S(2)}, u32[]{:S(2)}) %collective-permute-start.11) | collective-permute-done | bytes 4128 | tf_op jit(solution)/shard_map/ppermute | solution.py:488
  40.0 0.0 collective-permute-start.12
  40.0 0.0 collective-permute-done.9.refs_4_
  40.0 0.0 collective-permute-done.8.refs_3_
  40.0 0.0 collective-permute-done.7.refs_2_
  40.0 1.0 %shard_map.110 = (bf16[2,768,128]{2,1,0:T(8,128)(2,1)S(1)}, bf16[2,768,128]{2,1,0:T(8,128)(2,1)S(1)}, bf16[2,512,768]{2,1,0:T(8,128)(2,1)S(1)}, bf16[2,512,768]{2,1,0:T(8,128)(2,1)S(1)}) custom-call(bf16[512,256]{1,0:T(8,128)(2,1)S(1)} %get-tuple-element.46.refs_4_.refs_0_, bf16[512,256]{1,0:T(8,128)(2,1)S(1)} %get-tuple-element.52.refs_5_.refs_1_, ...), custom_call_target="tpu_custom_call" | custom-call | flops 201326592 | bytes 983040 | tf_op jit(solution)/shard_map/pallas_call | solution.py:34
  41.0 1.4 %shard_map.111 = (bf16[512,256]{1,0:T(8,128)(2,1)S(1)}, bf16[512,256]{1,0:T(8,128)(2,1)S(1)}) custom-call(bf16[2,1024,128]{2,1,0:T(8,128)(2,1)S(1)} %get-tuple-element.54.refs_1_.refs_0_, bf16[2,1024,128]{2,1,0:T(8,128)(2,1)S(1)} %get-tuple-element.55.refs_2_.refs_1_, bf16[2,512,1024]{2,1,0:T(8,128)(2,1)S(1)} %get-tuple-element.68.refs_2_, ...), custom_call_target="tpu_custom_call" | custom-call | flops 536870912 | bytes 10747904 | tf_op jit(solution)/shard_map/pallas_call | solution.py:34
  42.5 0.0 collective-permute-done.12.refs_4_
  42.5 0.1 shard_map.114
  42.6 1.5 %collective-permute-start.13 = (bf16[416,256]{1,0:T(8,128)(2,1)S(1)}, bf16[416,256]{1,0:T(8,128)(2,1)S(1)}, u32[]{:S(2)}, u32[]{:S(2)}) collective-permute-start(bf16[416,256]{1,0:T(8,128)(2,1)S(1)} %get-tuple-element.77), channel_id=1, source_target_pairs={{0,2},{2,0},{4,6},{6,4},{8,10},{10,8},{12,14},{14,12},{16,18},{18,... | collective-permute-start | bytes 638984 | tf_op jit(solution)/shard_map/ppermute | solution.py:488
  44.0 0.5 collective-permute-start.14
  44.5 1.6 %collective-permute-start.15 = (bf16[416,256]{1,0:T(8,128)(2,1)S(1)}, bf16[416,256]{1,0:T(8,128)(2,1)S(1)}, u32[]{:S(2)}, u32[]{:S(2)}) collective-permute-start(bf16[416,256]{1,0:T(8,128)(2,1)S(1)} %get-tuple-element.79), channel_id=1, source_target_pairs={{0,6},{2,4},{4,2},{6,0},{8,14},{10,12},{12,10},{14,8},{16,22},{18,... | collective-permute-start | bytes 638984 | tf_op jit(solution)/shard_map/ppermute | solution.py:488
  46.1 4.6 %collective-permute-done.13.refs_1_ = bf16[416,256]{1,0:T(8,128)(2,1)S(1)} collective-permute-done((bf16[416,256]{1,0:T(8,128)(2,1)S(1)}, bf16[416,256]{1,0:T(8,128)(2,1)S(1)}, u32[]{:S(2)}, u32[]{:S(2)}) %collective-permute-start.13) | collective-permute-done | bytes 213024 | tf_op jit(solution)/shard_map/ppermute | solution.py:488
  50.7 5.2 %collective-permute-done.14.refs_2_ = bf16[416,256]{1,0:T(8,128)(2,1)S(1)} collective-permute-done((bf16[416,256]{1,0:T(8,128)(2,1)S(1)}, bf16[416,256]{1,0:T(8,128)(2,1)S(1)}, u32[]{:S(2)}, u32[]{:S(2)}) %collective-permute-start.14) | collective-permute-done | bytes 213024 | tf_op jit(solution)/shard_map/ppermute | solution.py:488
  56.0 0.0 collective-permute-done.15.refs_3_
  56.0 1.0 %shard_map.115 = (bf16[128,1024]{1,0:T(8,128)(2,1)}, bf16[128,1024]{1,0:T(8,128)(2,1)}, bf16[128,1024]{1,0:T(8,128)(2,1)}, f32[32,128]{1,0:T(8,128)}) custom-call(bf16[416,256]{1,0:T(8,128)(2,1)S(1)} %get-tuple-element.76.refs_0_, bf16[416,256]{1,0:T(8,128)(2,1)S(1)} %collective-permute-done.13.refs_1_, ...), custom_call_target="tpu_custom_call" | custom-call | bytes 851968 | tf_op jit(solution)/shard_map/pallas_call | solution.py:34
  (4 shorter events, 0.1 us)
Async XLA Ops:
  0.6 19.6 %copy-start = (f32[16,128]{1,0:T(8,128)S(1)}, f32[16,128]{1,0:T(8,128)}, u32[]{:S(2)}) copy-start(f32[16,128]{1,0:T(8,128)} %refs_5_.3) | copy-start | bytes 24580
  2.1 8.0 %collective-permute-start = (bf16[272,256]{1,0:T(8,128)(2,1)S(1)}, bf16[272,256]{1,0:T(8,128)(2,1)S(1)}, u32[]{:S(2)}, u32[]{:S(2)}) collective-permute-start(bf16[272,256]{1,0:T(8,128)(2,1)S(1)} %get-tuple-element.43), channel_id=1, source_target_pairs={{0,2},{2,0},{4,6},{6,4},{8,10},{10,8},{12,14},{14,12},{16,18},{18,... | collective-permute-start | bytes 417800 | tf_op jit(solution)/shard_map/ppermute | solution.py:488
  5.1 9.2 %collective-permute-start.1 = (bf16[272,256]{1,0:T(8,128)(2,1)S(1)}, bf16[272,256]{1,0:T(8,128)(2,1)S(1)}, u32[]{:S(2)}, u32[]{:S(2)}) collective-permute-start(bf16[272,256]{1,0:T(8,128)(2,1)S(1)} %get-tuple-element.44), channel_id=1, source_target_pairs={{0,4},{2,6},{4,0},{6,2},{8,12},{10,14},{12,8},{14,10},{16,20},{18,... | collective-permute-start | bytes 417800 | tf_op jit(solution)/shard_map/ppermute | solution.py:488
  6.6 7.6 %collective-permute-start.2 = (bf16[272,256]{1,0:T(8,128)(2,1)S(1)}, bf16[272,256]{1,0:T(8,128)(2,1)S(1)}, u32[]{:S(2)}, u32[]{:S(2)}) collective-permute-start(bf16[272,256]{1,0:T(8,128)(2,1)S(1)} %get-tuple-element.45), channel_id=1, source_target_pairs={{0,6},{2,4},{4,2},{6,0},{8,14},{10,12},{12,10},{14,8},{16,22},{18,... | collective-permute-start | bytes 417800 | tf_op jit(solution)/shard_map/ppermute | solution.py:488
  6.7 11.0 %collective-permute-start.4 = (bf16[256,256]{1,0:T(8,128)(2,1)S(1)}, bf16[256,256]{1,0:T(8,128)(2,1)S(1)}, u32[]{:S(2)}, u32[]{:S(2)}) collective-permute-start(bf16[256,256]{1,0:T(8,128)(2,1)S(1)} %get-tuple-element.49), channel_id=1, source_target_pairs={{0,2},{2,0},{4,6},{6,4},{8,10},{10,8},{12,14},{14,12},{16,18},{18,... | collective-permute-start | bytes 393224 | tf_op jit(solution)/shard_map/ppermute | solution.py:488
  8.6 10.2 %collective-permute-start.5 = (bf16[256,256]{1,0:T(8,128)(2,1)S(1)}, bf16[256,256]{1,0:T(8,128)(2,1)S(1)}, u32[]{:S(2)}, u32[]{:S(2)}) collective-permute-start(bf16[256,256]{1,0:T(8,128)(2,1)S(1)} %get-tuple-element.50), channel_id=1, source_target_pairs={{0,4},{2,6},{4,0},{6,2},{8,12},{10,14},{12,8},{14,10},{16,20},{18,... | collective-permute-start | bytes 393224 | tf_op jit(solution)/shard_map/ppermute | solution.py:488
  10.1 8.7 %collective-permute-start.6 = (bf16[256,256]{1,0:T(8,128)(2,1)S(1)}, bf16[256,256]{1,0:T(8,128)(2,1)S(1)}, u32[]{:S(2)}, u32[]{:S(2)}) collective-permute-start(bf16[256,256]{1,0:T(8,128)(2,1)S(1)} %get-tuple-element.51), channel_id=1, source_target_pairs={{0,6},{2,4},{4,2},{6,0},{8,14},{10,12},{12,10},{14,8},{16,22},{18,... | collective-permute-start | bytes 393224 | tf_op jit(solution)/shard_map/ppermute | solution.py:488
  14.3 9.8 %collective-permute-start.3 = (bf16[768,256]{1,0:T(8,128)(2,1)S(1)}, bf16[768,256]{1,0:T(8,128)(2,1)S(1)}, u32[]{:S(2)}, u32[]{:S(2)}) collective-permute-start(bf16[768,256]{1,0:T(8,128)(2,1)S(1)} %shard_map.104), channel_id=1, source_target_pairs={{0,8},{2,10},{4,12},{6,14},{8,16},{10,18},{12,20},{14,22},{16,24},... | collective-permute-start | bytes 1179656 | tf_op jit(solution)/shard_map/ppermute | solution.py:491
  18.9 21.1 %collective-permute-start.7 = (bf16[816,256]{1,0:T(8,128)(2,1)S(1)}, bf16[816,256]{1,0:T(8,128)(2,1)S(1)}, u32[]{:S(2)}, u32[]{:S(2)}) collective-permute-start(bf16[816,256]{1,0:T(8,128)(2,1)S(1)} %shard_map.109), channel_id=1, source_target_pairs={{8,0},{10,2},{12,4},{14,6},{16,8},{18,10},{20,12},{22,14},{24,16},... | collective-permute-start | bytes 1253384 | tf_op jit(solution)/shard_map/ppermute | solution.py:491
  27.8 7.7 %collective-permute-start.10 = (f32[8,128]{1,0:T(8,128)S(1)}, f32[8,128]{1,0:T(8,128)S(1)}, u32[]{:S(2)}, u32[]{:S(2)}) collective-permute-start(f32[8,128]{1,0:T(8,128)S(1)} %get-tuple-element.75.refs_0_), channel_id=1, source_target_pairs={{0,8},{2,10},{4,12},{6,14},{8,0},{10,2},{12,4},{14,6},{16,24},{18,... | collective-permute-start | bytes 12296 | tf_op jit(solution)/shard_map/ppermute | solution.py:488
  30.4 9.6 %collective-permute-start.9 = (f32[2,8,256]{2,1,0:T(8,128)S(1)}, f32[2,8,256]{2,1,0:T(8,128)S(1)}, u32[]{:S(2)}, u32[]{:S(2)}) collective-permute-start(f32[2,8,256]{2,1,0:T(8,128)S(1)} %get-tuple-element.60.refs_1_), channel_id=1, source_target_pairs={{0,0},{2,2},{4,4},{6,6},{8,16},{10,18},{12,20},{14,22},{16,8},{18,... | collective-permute-start | bytes 49160 | tf_op jit(solution)/shard_map/ppermute | solution.py:555
  31.0 9.0 %collective-permute-start.8 = (f32[2,8,256]{2,1,0:T(8,128)S(1)}, f32[2,8,256]{2,1,0:T(8,128)S(1)}, u32[]{:S(2)}, u32[]{:S(2)}) collective-permute-start(f32[2,8,256]{2,1,0:T(8,128)S(1)} %get-tuple-element.60.refs_1_), channel_id=1, source_target_pairs={{0,8},{2,10},{4,12},{6,14},{8,0},{10,2},{12,4},{14,6},{16,24},{18,... | collective-permute-start | bytes 49160 | tf_op jit(solution)/shard_map/ppermute | solution.py:555
  35.5 4.5 %collective-permute-start.11 = (f32[8,128]{1,0:T(8,128)S(1)}, f32[8,128]{1,0:T(8,128)S(1)}, u32[]{:S(2)}, u32[]{:S(2)}) collective-permute-start(f32[8,128]{1,0:T(8,128)S(1)} %shard_map.112.refs_0_), channel_id=1, source_target_pairs={{0,16},{2,18},{4,20},{6,22},{8,24},{10,26},{12,28},{14,30},{16,0},... | collective-permute-start | bytes 12296 | tf_op jit(solution)/shard_map/ppermute | solution.py:488
  40.0 2.5 %collective-permute-start.12 = (f32[8,128]{1,0:T(8,128)S(1)}, f32[8,128]{1,0:T(8,128)S(1)}, u32[]{:S(2)}, u32[]{:S(2)}) collective-permute-start(f32[8,128]{1,0:T(8,128)S(1)} %shard_map.113.refs_3_), channel_id=1, source_target_pairs={{0,1},{1,0},{2,3},{3,2},{4,5},{5,4},{6,7},{7,6},{8,9},{9,8},{10,11... | collective-permute-start | bytes 12296 | tf_op jit(solution)/shard_map/ppermute | solution.py:488
  42.6 8.2 %collective-permute-start.13 = (bf16[416,256]{1,0:T(8,128)(2,1)S(1)}, bf16[416,256]{1,0:T(8,128)(2,1)S(1)}, u32[]{:S(2)}, u32[]{:S(2)}) collective-permute-start(bf16[416,256]{1,0:T(8,128)(2,1)S(1)} %get-tuple-element.77), channel_id=1, source_target_pairs={{0,2},{2,0},{4,6},{6,4},{8,10},{10,8},{12,14},{14,12},{16,18},{18,... | collective-permute-start | bytes 638984 | tf_op jit(solution)/shard_map/ppermute | solution.py:488
  44.0 11.9 %collective-permute-start.14 = (bf16[416,256]{1,0:T(8,128)(2,1)S(1)}, bf16[416,256]{1,0:T(8,128)(2,1)S(1)}, u32[]{:S(2)}, u32[]{:S(2)}) collective-permute-start(bf16[416,256]{1,0:T(8,128)(2,1)S(1)} %get-tuple-element.78), channel_id=1, source_target_pairs={{0,4},{2,6},{4,0},{6,2},{8,12},{10,14},{12,8},{14,10},{16,20},{18,... | collective-permute-start | bytes 638984 | tf_op jit(solution)/shard_map/ppermute | solution.py:488
  44.5 11.4 %collective-permute-start.15 = (bf16[416,256]{1,0:T(8,128)(2,1)S(1)}, bf16[416,256]{1,0:T(8,128)(2,1)S(1)}, u32[]{:S(2)}, u32[]{:S(2)}) collective-permute-start(bf16[416,256]{1,0:T(8,128)(2,1)S(1)} %get-tuple-element.79), channel_id=1, source_target_pairs={{0,6},{2,4},{4,2},{6,0},{8,14},{10,12},{12,10},{14,8},{16,22},{18,... | collective-permute-start | bytes 638984 | tf_op jit(solution)/shard_map/ppermute | solution.py:488

commit v3 on v1

--- a/solution.py
+++ b/solution.py
@@ -65,14 +65,15 @@
         return lax.rem(lax.axis_index("seq"), self.group)
 
 
-def pack_kernel(z, q, k, v, d, ids, mask, *refs):
+def pack_kernel(z, q, k, v, d, bias, ids, mask, *refs):
     kv, qd = refs[: z.group], refs[z.group : 2 * z.group]
-    slots, flags, sem = refs[2 * z.group :]
+    table, slots, flags, sem = refs[2 * z.group :]
     index = lax.axis_index("seq")
     me = z.me()
     copies = [
         pltpu.make_async_copy(ids.at[0], slots, sem.at[0]),
         pltpu.make_async_copy(mask, flags, sem.at[1]),
+        pltpu.make_async_copy(bias, table, sem.at[2]),
     ]
     for sources, dst in (((k, v), kv), ((q, d), qd)):
         for g in range(z.group):
@@ -414,8 +415,8 @@
     lax.fori_loop(0, z.pairs, each, 0)
 
 
-def seal_kernel(z, sides, dq, dk, dv, *refs):
-    sums, sends = refs[:sides], refs[sides:]
+def seal_kernel(z, sides, grads, *refs):
+    sources, sums, sends = refs[:grads], refs[grads : grads + sides], refs[grads + sides :]
     tok = z.tok
     packs = []
     for ref in sums:
@@ -425,10 +426,11 @@
     me = z.me()
     for k in range(z.group):
         rows = at((me ^ k) * tok, tok)
-        for n, ref in enumerate((dq, dk, dv)):
+        for n, ref in enumerate(sources):
             sends[k][n * tok : (n + 1) * tok, :] = ref[rows, :]
         for n, pack in enumerate(packs):
-            sends[k][3 * tok + n * CODE_ROWS : 3 * tok + (n + 1) * CODE_ROWS, :] = pack
+            top = grads * tok + n * CODE_ROWS
+            sends[k][top : top + CODE_ROWS, :] = pack
 
 
 def add_kernel(*refs):
@@ -438,8 +440,8 @@
     refs[-1][...] = total
 
 
-def unpack_kernel(z, sides, *refs):
-    got, outs, gb, held, sem = refs[: z.group], refs[z.group : -3], refs[-3], refs[-2], refs[-1]
+def unpack_kernel(z, grads, *refs):
+    got, outs, sem = refs[: z.group], refs[z.group : z.group + grads], refs[-1]
     me = z.me()
     copies = []
     for k in range(z.group):
@@ -449,11 +451,23 @@
             copies.append(pltpu.make_async_copy(src, out.at[:, cols], sem.at[len(copies)]))
     for copy in copies:
         copy.start()
+    return copies
+
+
+def unpack_kv_kernel(z, *refs):
+    for copy in unpack_kernel(z, 2, *refs):
+        copy.wait()
+
+
+def unpack_q_kernel(z, sides, *refs):
+    got, (out, gb, held, sem) = refs[: z.group], refs[z.group :]
+    me = z.me()
+    copies = unpack_kernel(z, 1, *got, out, sem)
     owner = lax.broadcasted_iota(jnp.int32, held.shape, 0) // z.hg
     total = jnp.zeros(held.shape, F32)
     for k in range(z.group):
         for n in range(sides):
-            top = 3 * z.tok + n * CODE_ROWS
+            top = z.tok + n * CODE_ROWS
             rows = got[k][top : top + CODE_ROWS, :].astype(F32)
             sums = rows[0:8, 0 : z.buckets] + rows[8:16, 0 : z.buckets] + rows[0:8, z.buckets :]
             wide = jnp.concatenate([sums[0 : z.hg]] * (held.shape[0] // z.hg), axis=0)
@@ -487,7 +501,7 @@
         return lax.ppermute(value, axis, [(i, i ^ by) for i in range(lax.axis_size(axis))])
 
     def shifted(value, by):
-        return lax.ppermute(value, "seq", [(i, i + by) for i in range(blocks) if 0 <= i + by < blocks])
+        return lax.ppermute(value, "seq", [(i, (i + by) % blocks) for i in range(blocks)])
 
     def added(*terms):
         (total,) = call(add_kernel, [(terms[0].shape, terms[0].dtype)], terms)
@@ -497,17 +511,17 @@
     pack_bytes = group * (z.rows + 2 * tok) * z.cw * 2
     packed = call(
         bind(pack_kernel, z),
-        [((z.rows, z.cw), BF16)] * group + [((2 * tok, z.cw), BF16)] * group,
-        (queries, keys, values, grad_out, bucket_ids, block_mask),
-        spaces=[hbm] * 6,
+        [((z.rows, z.cw), BF16)] * group + [((2 * tok, z.cw), BF16)] * group + [((heads, buckets), F32)],
+        (queries, keys, values, grad_out, bias_table, bucket_ids, block_mask),
+        spaces=[hbm] * 7,
         scratch=[
             pltpu.VMEM((span, z.wide), jnp.int32),
             pltpu.SMEM((1, span), jnp.int32),
-            pltpu.SemaphoreType.DMA((4 * group + 2,)),
+            pltpu.SemaphoreType.DMA((4 * group + 3,)),
         ],
         limit=VMEM_BYTES - pack_bytes - (520 << 10),
     )
-    kv, qd = packed[:group], packed[group:]
+    kv, qd, table = packed[:group], packed[group : 2 * group], packed[2 * group]
     kv_got = [kv[0]] + [swap(kv[k], k) for k in range(1, group)]
     qd_got = [qd[0]] + [swap(qd[k], k) for k in range(1, group)]
     (kv_out,) = call(bind(kv_halo_kernel, z), [((z.halo * 2 * tok, z.cw), BF16)], kv_got)
@@ -527,7 +541,7 @@
         [((group * tok, z.cw), BF16)] * 2
         + [((near * z.pairs, tok, z.wide), F32), ((far * z.pairs, tok, z.wide), F32)]
         + [((group * CODE_ROWS, z.wide), F32)],
-        (*kv_got, bias_table),
+        (*kv_got, table),
         scratch=[pltpu.VMEM((group * span * z.hg * 8, z.wide), F32)],
     )
     qm, dom, wnear, dnear, *sums = call(
@@ -543,7 +557,7 @@
         (kv_halo, qm, dom, bias_far, *sums),
         flops=2 * far * z.pairs * unit,
     )
-    stats_halo = lax.ppermute(stats, "seq", [(i, (i - group) % blocks) for i in range(blocks)])
+    stats_halo = shifted(stats, -group)
     p16, s16, gb = call(
         bind(own_kernel, z),
         [
@@ -571,7 +585,7 @@
     halo_terms = call(
         bind(tail_kernel, z),
         [rows_of, rows_of, lanes_of, lanes_of],
-        (own_k, own_v, qd_halo, stats_halo, bias_table),
+        (own_k, own_v, qd_halo, stats_halo, table),
         scratch=[pltpu.VMEM((far * z.hg * 8, z.wide), F32)],
         flops=2 * far * z.pairs * unit,
     )
@@ -581,17 +595,25 @@
         (qm, dom, p16, s16, *halo_terms),
         flops=2 * (near + far) * z.pairs * unit,
     )
-    ret = call(
-        bind(seal_kernel, z, sides), [((3 * tok + sides * CODE_ROWS, z.cw), BF16)] * group, (dq, dk, dv, *sums_of)
-    )
-    ret_got = [ret[0]] + [swap(ret[k], k) for k in range(1, group)]
-    return call(
-        bind(unpack_kernel, z, sides),
-        [((tok, width), BF16)] * 3 + [((heads * sides, buckets), F32)],
-        ret_got,
+    ret = call(bind(seal_kernel, z, 0, 2), [((2 * tok, z.cw), BF16)] * group, (dk, dv))
+    kv_back = [ret[0]] + [swap(ret[k], k) for k in range(1, group)]
+    ret = call(bind(seal_kernel, z, sides, 1), [((tok + sides * CODE_ROWS, z.cw), BF16)] * group, (dq, *sums_of))
+    q_back = [ret[0]] + [swap(ret[k], k) for k in range(1, group)]
+    grad_k, grad_v = call(
+        bind(unpack_kv_kernel, z),
+        [((tok, width), BF16)] * 2,
+        kv_back,
         out_space=hbm,
-        scratch=[pltpu.VMEM((heads * sides, buckets), F32), pltpu.SemaphoreType.DMA((3 * group + 1,))],
-    )
+        scratch=[pltpu.SemaphoreType.DMA((2 * group,))],
+    )
+    grad_q, grad_bias = call(
+        bind(unpack_q_kernel, z, sides),
+        [((tok, width), BF16), ((heads * sides, buckets), F32)],
+        q_back,
+        out_space=hbm,
+        scratch=[pltpu.VMEM((heads * sides, buckets), F32), pltpu.SemaphoreType.DMA((group + 1,))],
+    )
+    return grad_q, grad_k, grad_v, grad_bias
 
 
 def solution(mesh):

time: 54.5 us -> 63 us (1.16)
  starting transfers between devices: 25.9 us -> 31.2 us
  waiting for transfers between devices: 15.1 us -> 17.6 us
  Pallas kernels: 12.5 us -> 13.2 us
    ppermute x12 -> x15, starting transfers between devices: 18.8 us -> 25 us  [swap(): lax.ppermute(value, axis, [(i, i ^ by) for i in range(lax.axis_size(axis))])]
    ppermute x12 -> x15, waiting for transfers between devices: 14.2 us -> 15.5 us  [swap(): lax.ppermute(value, axis, [(i, i ^ by) for i in range(lax.axis_size(axis))])]
    ppermute x3, waiting for transfers between devices: 0.89 us -> 2.11 us  [shifted(): lax.ppermute(value, 'seq', [(i, (i + by) % blocks) for i in range(blocks)])]
    ppermute x3, starting transfers between devices: 7.12 us -> 6.19 us  [shifted(): lax.ppermute(value, 'seq', [(i, (i + by) % blocks) for i in range(blocks)])]
    pallas_call x14 -> x16, Pallas kernels: 12.5 us -> 13.2 us  [call(): pl.pallas_call(kernel, out_shape=tuple((out_space(s, d) for s, d in outs)...]
  transfers between devices with their start and end apart: 15 -> 18, of which waited for: 6 -> 8; matrix products, arithmetic and copies ran while one was open for 0% -> 0% of each run, Pallas kernels for 19% -> 17%
where the time goes in v3:
time: 63 us; the launch traced here: 62.8 us
  starting transfers between devices  31.2 us (50%)
  waiting for transfers between devices  17.6 us (28%)
  Pallas kernels  13.2 us (21%)
  between operations  0.76 us (1%)
    ppermute x15, starting transfers between devices, swap(): lax.ppermute(value, axis, [(i, i ^ by) for i in range(lax.axis_size(axis))])  25 us
    ppermute x15, waiting for transfers between devices, swap(): lax.ppermute(value, axis, [(i, i ^ by) for i in range(lax.axis_size(axis))])  15.5 us
    pallas_call x16, Pallas kernels, call(): pl.pallas_call(kernel, out_shape=tuple((out_space(s, d) for s, d in outs)...  13.2 us
    ppermute x3, starting transfers between devices, shifted(): lax.ppermute(value, 'seq', [(i, (i + by) % blocks) for i in range(blocks)])  6.19 us
    ppermute x3, waiting for transfers between devices, shifted(): lax.ppermute(value, 'seq', [(i, (i + by) % blocks) for i in range(blocks)])  2.11 us
  transfers between devices with their start and end apart: 18, of which 8 were waited for; matrix products, arithmetic and copies ran while one was open for 0% of the time, Pallas kernels for 17%

profile of v3, /device:TPU:0, one launch (start us, length us, event | category | flops | bytes accessed | tf_op | source)
XLA Modules:
  0.0 62.8 jit_solution(2020425135719559407)
XLA Ops:
  0.6 1.5 %shard_map.102 = (bf16[272,256]{1,0:T(8,128)(2,1)S(1)}, bf16[272,256]{1,0:T(8,128)(2,1)S(1)}, bf16[272,256]{1,0:T(8,128)(2,1)S(1)}, bf16[272,256]{1,0:T(8,128)(2...) custom-call(bf16[128,1024]{1,0:T(8,128)(2,1)} %refs_0_.1, ...), custom_call_target="tpu_custom_call" | custom-call | bytes 1060880 | tf_op jit(solution)/shard_map/pallas_call | solution.py:34
  2.1 3.0 %collective-permute-start = (bf16[272,256]{1,0:T(8,128)(2,1)S(1)}, bf16[272,256]{1,0:T(8,128)(2,1)S(1)}, u32[]{:S(2)}, u32[]{:S(2)}) collective-permute-start(bf16[272,256]{1,0:T(8,128)(2,1)S(1)} %get-tuple-element.52), channel_id=1, source_target_pairs={{0,2},{2,0},{4,6},{6,4},{8,10},{10,8},{12,14},{14,12},{16,18},{18,... | collective-permute-start | bytes 417800 | tf_op jit(solution)/shard_map/ppermute | solution.py:501
  5.1 1.5 %collective-permute-start.1 = (bf16[272,256]{1,0:T(8,128)(2,1)S(1)}, bf16[272,256]{1,0:T(8,128)(2,1)S(1)}, u32[]{:S(2)}, u32[]{:S(2)}) collective-permute-start(bf16[272,256]{1,0:T(8,128)(2,1)S(1)} %get-tuple-element.53), channel_id=1, source_target_pairs={{0,4},{2,6},{4,0},{6,2},{8,12},{10,14},{12,8},{14,10},{16,20},{18,... | collective-permute-start | bytes 417800 | tf_op jit(solution)/shard_map/ppermute | solution.py:501
  6.6 0.0 collective-permute-start.2
  6.7 1.9 %collective-permute-start.4 = (bf16[256,256]{1,0:T(8,128)(2,1)S(1)}, bf16[256,256]{1,0:T(8,128)(2,1)S(1)}, u32[]{:S(2)}, u32[]{:S(2)}) collective-permute-start(bf16[256,256]{1,0:T(8,128)(2,1)S(1)} %get-tuple-element.59), channel_id=1, source_target_pairs={{0,2},{2,0},{4,6},{6,4},{8,10},{10,8},{12,14},{14,12},{16,18},{18,... | collective-permute-start | bytes 393224 | tf_op jit(solution)/shard_map/ppermute | solution.py:501
  8.6 1.5 %collective-permute-start.5 = (bf16[256,256]{1,0:T(8,128)(2,1)S(1)}, bf16[256,256]{1,0:T(8,128)(2,1)S(1)}, u32[]{:S(2)}, u32[]{:S(2)}) collective-permute-start(bf16[256,256]{1,0:T(8,128)(2,1)S(1)} %get-tuple-element.60), channel_id=1, source_target_pairs={{0,4},{2,6},{4,0},{6,2},{8,12},{10,14},{12,8},{14,10},{16,20},{18,... | collective-permute-start | bytes 393224 | tf_op jit(solution)/shard_map/ppermute | solution.py:501
  10.1 0.0 collective-permute-done.refs_1_.refs_5_
  10.1 2.5 %collective-permute-start.6 = (bf16[256,256]{1,0:T(8,128)(2,1)S(1)}, bf16[256,256]{1,0:T(8,128)(2,1)S(1)}, u32[]{:S(2)}, u32[]{:S(2)}) collective-permute-start(bf16[256,256]{1,0:T(8,128)(2,1)S(1)} %get-tuple-element.61), channel_id=1, source_target_pairs={{0,6},{2,4},{4,2},{6,0},{8,14},{10,12},{12,10},{14,8},{16,22},{18,... | collective-permute-start | bytes 393224 | tf_op jit(solution)/shard_map/ppermute | solution.py:501
  12.6 1.7 %collective-permute-done.1.refs_2_.refs_6_ = bf16[272,256]{1,0:T(8,128)(2,1)S(1)} collective-permute-done((bf16[272,256]{1,0:T(8,128)(2,1)S(1)}, bf16[272,256]{1,0:T(8,128)(2,1)S(1)}, u32[]{:S(2)}, u32[]{:S(2)}) %collective-permute-start.1) | collective-permute-done | bytes 139296 | tf_op jit(solution)/shard_map/ppermute | solution.py:501
  14.3 0.0 collective-permute-done.2.refs_3_.refs_7_
  14.3 1.5 %collective-permute-start.3 = (bf16[768,256]{1,0:T(8,128)(2,1)S(1)}, bf16[768,256]{1,0:T(8,128)(2,1)S(1)}, u32[]{:S(2)}, u32[]{:S(2)}) collective-permute-start(bf16[768,256]{1,0:T(8,128)(2,1)S(1)} %shard_map.104), channel_id=1, source_target_pairs={{0,8},{2,10},{4,12},{6,14},{8,16},{10,18},{12,20},{14,22},{16,24},... | collective-permute-start | bytes 1179656 | tf_op jit(solution)/shard_map/ppermute | solution.py:504
  15.8 0.1 collective-permute-done.4.refs_1_
  15.9 2.9 %collective-permute-done.5.refs_2_ = bf16[256,256]{1,0:T(8,128)(2,1)S(1)} collective-permute-done((bf16[256,256]{1,0:T(8,128)(2,1)S(1)}, bf16[256,256]{1,0:T(8,128)(2,1)S(1)}, u32[]{:S(2)}, u32[]{:S(2)}) %collective-permute-start.5) | collective-permute-done | bytes 131104 | tf_op jit(solution)/shard_map/ppermute | solution.py:501
  18.9 0.0 collective-permute-done.6.refs_3_
  18.9 3.7 %collective-permute-start.13 = (bf16[816,256]{1,0:T(8,128)(2,1)S(1)}, bf16[816,256]{1,0:T(8,128)(2,1)S(1)}, u32[]{:S(2)}, u32[]{:S(2)}) collective-permute-start(bf16[816,256]{1,0:T(8,128)(2,1)S(1)} %shard_map.113), channel_id=1, source_target_pairs={{0,24},{2,26},{4,28},{6,30},{8,0},{10,2},{12,4},{14,6},{16,8},{18,... | collective-permute-start | bytes 1253384 | tf_op jit(solution)/shard_map/ppermute | solution.py:504
  22.6 1.4 %shard_map.103 = (bf16[512,256]{1,0:T(8,128)(2,1)S(1)}, bf16[512,256]{1,0:T(8,128)(2,1)S(1)}, f32[20,128,256]{2,1,0:T(8,128)S(1)}, f32[12,128,256]{2,1,0:T(8,128)S(1)}, f32[64,256]{1,0:T(8,128)S(1)}) custom-call(bf16[272,256]{1,0:T(8,128)(2,1)S(1)} %get-tuple-element.51.refs_0_.refs_4_, bf16[272,256]{1,0:T(8,128)(2,1)S(1)} %collective-permute-done.refs_1_.refs_5_, ...), custom_call_target="tpu_custom_call" | custom-call | bytes 565248 | tf_op jit(solution)/shard_map/pallas_call | solution.py:34
  24.0 1.5 %shard_map.105 = (bf16[2,1024,128]{2,1,0:T(8,128)(2,1)S(1)}, bf16[2,1024,128]{2,1,0:T(8,128)(2,1)S(1)}, f32[20,128,256]{2,1,0:T(8,128)S(1)}, f32[20,128,256]{2,1...) custom-call(bf16[256,256]{1,0:T(8,128)(2,1)S(1)} %get-tuple-element.58.refs_0_, ...), custom_call_target="tpu_custom_call" | custom-call | flops 335544320 | bytes 3670016 | tf_op jit(solution)/shard_map/pallas_call | solution.py:34
  25.5 2.1 %collective-permute-done.3.refs_0_.refs_1_ = bf16[768,256]{1,0:T(8,128)(2,1)S(1)} collective-permute-done((bf16[768,256]{1,0:T(8,128)(2,1)S(1)}, bf16[768,256]{1,0:T(8,128)(2,1)S(1)}, u32[]{:S(2)}, u32[]{:S(2)}) %collective-permute-start.3) | collective-permute-done | bytes 393248 | tf_op jit(solution)/shard_map/ppermute | solution.py:504
  27.6 1.6 %shard_map.106 = (f32[2,8,256]{2,1,0:T(8,128)S(1)}, f32[20,256]{1,0:T(8,128)S(1)}, f32[12,256]{1,0:T(8,128)S(1)}, f32[12,128,256]{2,1,0:T(8,128)S(1)}, f32[12,12...) custom-call(bf16[768,256]{1,0:T(8,128)(2,1)S(1)} %collective-permute-done.3.refs_0_.refs_1_, ...), custom_call_target="tpu_custom_call" | custom-call | flops 201326592 | bytes 3076096 | tf_op jit(solution)/shard_map/pallas_call | solution.py:34
  29.2 2.2 %shard_map.107 = (bf16[2,512,1024]{2,1,0:T(8,128)(2,1)S(1)}, bf16[2,896,1024]{2,1,0:T(8,128)(2,1)S(1)}, f32[8,128]{1,0:T(8,128)S(1)}) custom-call(f32[64,256]{1,0:T(8,128)S(1)} %get-tuple-element.57.refs_0_, f32[2,8,256]{2,1,0:T(8,128)S(1)} %get-tuple-element.70.refs_1_, f32[20,256]{1,0:T(8,128)S(1)} %get-tuple-element.71.refs_2_, ...), custom_call_target="tpu_custom_call" | custom-call | bytes 8503296 | tf_op jit(solution)/shard_map/pallas_call | solution.py:34
  31.4 0.1 collective-permute-start.7
  31.5 3.6 %collective-permute-done.7.refs_1_ = f32[8,128]{1,0:T(8,128)S(1)} collective-permute-done((f32[8,128]{1,0:T(8,128)S(1)}, f32[8,128]{1,0:T(8,128)S(1)}, u32[]{:S(2)}, u32[]{:S(2)}) %collective-permute-start.7) | collective-permute-done | bytes 4128 | tf_op jit(solution)/shard_map/ppermute | solution.py:501
  35.1 7.0 %collective-permute-start.8 = (f32[8,128]{1,0:T(8,128)S(1)}, f32[8,128]{1,0:T(8,128)S(1)}, u32[]{:S(2)}, u32[]{:S(2)}) collective-permute-start(f32[8,128]{1,0:T(8,128)S(1)} %shard_map.109.refs_0_), channel_id=1, source_target_pairs={{0,16},{2,18},{4,20},{6,22},{8,24},{10,26},{12,28},{14,30},{16,0},... | collective-permute-start | bytes 12296 | tf_op jit(solution)/shard_map/ppermute | solution.py:501
  42.1 1.1 %collective-permute-start.14 = (f32[2,8,256]{2,1,0:T(8,128)S(1)}, f32[2,8,256]{2,1,0:T(8,128)S(1)}, u32[]{:S(2)}, u32[]{:S(2)}) collective-permute-start(f32[2,8,256]{2,1,0:T(8,128)S(1)} %get-tuple-element.70.refs_1_), channel_id=1, source_target_pairs={{0,24},{2,26},{4,28},{6,30},{8,0},{10,2},{12,4},{14,6},{16,8},{18,... | collective-permute-start | bytes 49160 | tf_op jit(solution)/shard_map/ppermute | solution.py:504
  43.2 0.5 collective-permute-done.8.refs_1_
  43.7 0.0 collective-permute-start.9
  43.7 0.8 %shard_map.108.refs_0_ = bf16[512,256]{1,0:T(8,128)(2,1)S(1)} custom-call(bf16[512,256]{1,0:T(8,128)(2,1)S(1)} %get-tuple-element.56.refs_4_.refs_0_, bf16[768,256]{1,0:T(8,128)(2,1)S(1)} %collective-permute-done.3.refs_0_.refs_1_, bf16[2,896,1024]{2,1,0:T(8,128)(2,1)S(1)} %get-tuple-element.77.refs_2_.refs_3_), custom_call_target="tpu_custom_call" | custom-call | flops 268435456 | bytes 4325376 | tf_op jit(solution)/shard_map/pallas_call | solution.py:34
  44.5 0.3 collective-permute-done.9.refs_2_
  44.9 1.5 %collective-permute-start.10 = (bf16[160,256]{1,0:T(8,128)(2,1)S(1)}, bf16[160,256]{1,0:T(8,128)(2,1)S(1)}, u32[]{:S(2)}, u32[]{:S(2)}) collective-permute-start(bf16[160,256]{1,0:T(8,128)(2,1)S(1)} %get-tuple-element.80), channel_id=1, source_target_pairs={{0,2},{2,0},{4,6},{6,4},{8,10},{10,8},{12,14},{14,12},{16,18},{18,... | collective-permute-start | bytes 245768 | tf_op jit(solution)/shard_map/ppermute | solution.py:501
  46.4 0.0 collective-permute-done.14.refs_3_
  46.4 0.0 collective-permute-done.13.refs_2_
  46.4 1.0 %shard_map.114 = (bf16[2,768,128]{2,1,0:T(8,128)(2,1)S(1)}, bf16[2,768,128]{2,1,0:T(8,128)(2,1)S(1)}, bf16[2,512,768]{2,1,0:T(8,128)(2,1)S(1)}, bf16[2,512,768]{2,1,0:T(8,128)(2,1)S(1)}) custom-call(bf16[512,256]{1,0:T(8,128)(2,1)S(1)} %get-tuple-element.56.refs_4_.refs_0_, bf16[512,256]{1,0:T(8,128)(2,1)S(1)} %get-tuple-element.62.refs_5_.refs_1_, ...), custom_call_target="tpu_custom_call" | custom-call | flops 201326592 | bytes 966656 | tf_op jit(solution)/shard_map/pallas_call | solution.py:34
  47.4 1.4 %shard_map.115 = (bf16[512,256]{1,0:T(8,128)(2,1)S(1)}, bf16[512,256]{1,0:T(8,128)(2,1)S(1)}) custom-call(bf16[2,1024,128]{2,1,0:T(8,128)(2,1)S(1)} %get-tuple-element.64.refs_1_.refs_0_, bf16[2,1024,128]{2,1,0:T(8,128)(2,1)S(1)} %get-tuple-element.65.refs_2_.refs_1_, bf16[2,512,1024]{2,1,0:T(8,128)(2,1)S(1)} %get-tuple-element.84.refs_2_, ...), custom_call_target="tpu_custom_call" | custom-call | flops 536870912 | bytes 10747904 | tf_op jit(solution)/shard_map/pallas_call | solution.py:34
  48.9 0.9 %collective-permute-start.15 = (bf16[256,256]{1,0:T(8,128)(2,1)S(1)}, bf16[256,256]{1,0:T(8,128)(2,1)S(1)}, u32[]{:S(2)}, u32[]{:S(2)}) collective-permute-start(bf16[256,256]{1,0:T(8,128)(2,1)S(1)} %get-tuple-element.92), channel_id=1, source_target_pairs={{0,2},{2,0},{4,6},{6,4},{8,10},{10,8},{12,14},{14,12},{16,18},{18,... | collective-permute-start | bytes 393224 | tf_op jit(solution)/shard_map/ppermute | solution.py:501
  49.8 1.1 %collective-permute-start.16 = (bf16[256,256]{1,0:T(8,128)(2,1)S(1)}, bf16[256,256]{1,0:T(8,128)(2,1)S(1)}, u32[]{:S(2)}, u32[]{:S(2)}) collective-permute-start(bf16[256,256]{1,0:T(8,128)(2,1)S(1)} %get-tuple-element.93), channel_id=1, source_target_pairs={{0,4},{2,6},{4,0},{6,2},{8,12},{10,14},{12,8},{14,10},{16,20},{18,... | collective-permute-start | bytes 393224 | tf_op jit(solution)/shard_map/ppermute | solution.py:501
  50.9 1.5 %collective-permute-start.17 = (bf16[256,256]{1,0:T(8,128)(2,1)S(1)}, bf16[256,256]{1,0:T(8,128)(2,1)S(1)}, u32[]{:S(2)}, u32[]{:S(2)}) collective-permute-start(bf16[256,256]{1,0:T(8,128)(2,1)S(1)} %get-tuple-element.94), channel_id=1, source_target_pairs={{0,6},{2,4},{4,2},{6,0},{8,14},{10,12},{12,10},{14,8},{16,22},{18,... | collective-permute-start | bytes 393224 | tf_op jit(solution)/shard_map/ppermute | solution.py:501
  52.4 0.8 %collective-permute-start.11 = (bf16[160,256]{1,0:T(8,128)(2,1)S(1)}, bf16[160,256]{1,0:T(8,128)(2,1)S(1)}, u32[]{:S(2)}, u32[]{:S(2)}) collective-permute-start(bf16[160,256]{1,0:T(8,128)(2,1)S(1)} %get-tuple-element.81), channel_id=1, source_target_pairs={{0,4},{2,6},{4,0},{6,2},{8,12},{10,14},{12,8},{14,10},{16,20},{18,... | collective-permute-start | bytes 245768 | tf_op jit(solution)/shard_map/ppermute | solution.py:501
  53.2 0.0 collective-permute-done.10.refs_1_
  53.2 1.5 %collective-permute-start.12 = (bf16[160,256]{1,0:T(8,128)(2,1)S(1)}, bf16[160,256]{1,0:T(8,128)(2,1)S(1)}, u32[]{:S(2)}, u32[]{:S(2)}) collective-permute-start(bf16[160,256]{1,0:T(8,128)(2,1)S(1)} %get-tuple-element.82), channel_id=1, source_target_pairs={{0,6},{2,4},{4,2},{6,0},{8,14},{10,12},{12,10},{14,8},{16,22},{18,... | collective-permute-start | bytes 245768 | tf_op jit(solution)/shard_map/ppermute | solution.py:501
  54.8 6.3 %collective-permute-done.11.refs_2_ = bf16[160,256]{1,0:T(8,128)(2,1)S(1)} collective-permute-done((bf16[160,256]{1,0:T(8,128)(2,1)S(1)}, bf16[160,256]{1,0:T(8,128)(2,1)S(1)}, u32[]{:S(2)}, u32[]{:S(2)}) %collective-permute-start.11) | collective-permute-done | bytes 81952 | tf_op jit(solution)/shard_map/ppermute | solution.py:501
  61.1 0.0 collective-permute-done.12.refs_3_
  61.1 0.7 %shard_map.112 = (bf16[128,1024]{1,0:T(8,128)(2,1)}, f32[32,128]{1,0:T(8,128)}) custom-call(bf16[160,256]{1,0:T(8,128)(2,1)S(1)} %get-tuple-element.79.refs_0_, bf16[160,256]{1,0:T(8,128)(2,1)S(1)} %collective-permute-done.10.refs_1_, bf16[160,256]{1,0:T(8,128)(2,1)S(1)} %collective-permute-done.11.refs_2_, bf16[160,256]{1,0:T(8,128)(2,1)S(1)} %collective-permute-done.12.refs_3_), custom_call_target="tpu_custom_call" | custom-call | bytes 327680 | tf_op jit(solution)/shard_map/pallas_call | solution.py:34
  61.9 0.0 collective-permute-done.15.refs_1_
  61.9 0.0 collective-permute-done.16.refs_2_
  61.9 0.0 collective-permute-done.17.refs_3_
  61.9 0.9 %shard_map.117 = (bf16[128,1024]{1,0:T(8,128)(2,1)}, bf16[128,1024]{1,0:T(8,128)(2,1)}) custom-call(bf16[256,256]{1,0:T(8,128)(2,1)S(1)} %get-tuple-element.91.refs_0_, bf16[256,256]{1,0:T(8,128)(2,1)S(1)} %collective-permute-done.15.refs_1_, bf16[256,256]{1,0:T(8,128)(2,1)S(1)} %collective-permute-done.16.refs_2_, ...), custom_call_target="tpu_custom_call" | custom-call | bytes 524288 | tf_op jit(solution)/shard_map/pallas_call | solution.py:34
  (6 shorter events, 0.2 us)
Async XLA Ops:
  2.1 8.0 %collective-permute-start = (bf16[272,256]{1,0:T(8,128)(2,1)S(1)}, bf16[272,256]{1,0:T(8,128)(2,1)S(1)}, u32[]{:S(2)}, u32[]{:S(2)}) collective-permute-start(bf16[272,256]{1,0:T(8,128)(2,1)S(1)} %get-tuple-element.52), channel_id=1, source_target_pairs={{0,2},{2,0},{4,6},{6,4},{8,10},{10,8},{12,14},{14,12},{16,18},{18,... | collective-permute-start | bytes 417800 | tf_op jit(solution)/shard_map/ppermute | solution.py:501
  5.1 9.2 %collective-permute-start.1 = (bf16[272,256]{1,0:T(8,128)(2,1)S(1)}, bf16[272,256]{1,0:T(8,128)(2,1)S(1)}, u32[]{:S(2)}, u32[]{:S(2)}) collective-permute-start(bf16[272,256]{1,0:T(8,128)(2,1)S(1)} %get-tuple-element.53), channel_id=1, source_target_pairs={{0,4},{2,6},{4,0},{6,2},{8,12},{10,14},{12,8},{14,10},{16,20},{18,... | collective-permute-start | bytes 417800 | tf_op jit(solution)/shard_map/ppermute | solution.py:501
  6.6 7.6 %collective-permute-start.2 = (bf16[272,256]{1,0:T(8,128)(2,1)S(1)}, bf16[272,256]{1,0:T(8,128)(2,1)S(1)}, u32[]{:S(2)}, u32[]{:S(2)}) collective-permute-start(bf16[272,256]{1,0:T(8,128)(2,1)S(1)} %get-tuple-element.54), channel_id=1, source_target_pairs={{0,6},{2,4},{4,2},{6,0},{8,14},{10,12},{12,10},{14,8},{16,22},{18,... | collective-permute-start | bytes 417800 | tf_op jit(solution)/shard_map/ppermute | solution.py:501
  6.7 9.3 %collective-permute-start.4 = (bf16[256,256]{1,0:T(8,128)(2,1)S(1)}, bf16[256,256]{1,0:T(8,128)(2,1)S(1)}, u32[]{:S(2)}, u32[]{:S(2)}) collective-permute-start(bf16[256,256]{1,0:T(8,128)(2,1)S(1)} %get-tuple-element.59), channel_id=1, source_target_pairs={{0,2},{2,0},{4,6},{6,4},{8,10},{10,8},{12,14},{14,12},{16,18},{18,... | collective-permute-start | bytes 393224 | tf_op jit(solution)/shard_map/ppermute | solution.py:501
  8.6 10.2 %collective-permute-start.5 = (bf16[256,256]{1,0:T(8,128)(2,1)S(1)}, bf16[256,256]{1,0:T(8,128)(2,1)S(1)}, u32[]{:S(2)}, u32[]{:S(2)}) collective-permute-start(bf16[256,256]{1,0:T(8,128)(2,1)S(1)} %get-tuple-element.60), channel_id=1, source_target_pairs={{0,4},{2,6},{4,0},{6,2},{8,12},{10,14},{12,8},{14,10},{16,20},{18,... | collective-permute-start | bytes 393224 | tf_op jit(solution)/shard_map/ppermute | solution.py:501
  10.1 8.7 %collective-permute-start.6 = (bf16[256,256]{1,0:T(8,128)(2,1)S(1)}, bf16[256,256]{1,0:T(8,128)(2,1)S(1)}, u32[]{:S(2)}, u32[]{:S(2)}) collective-permute-start(bf16[256,256]{1,0:T(8,128)(2,1)S(1)} %get-tuple-element.61), channel_id=1, source_target_pairs={{0,6},{2,4},{4,2},{6,0},{8,14},{10,12},{12,10},{14,8},{16,22},{18,... | collective-permute-start | bytes 393224 | tf_op jit(solution)/shard_map/ppermute | solution.py:501
  14.3 13.3 %collective-permute-start.3 = (bf16[768,256]{1,0:T(8,128)(2,1)S(1)}, bf16[768,256]{1,0:T(8,128)(2,1)S(1)}, u32[]{:S(2)}, u32[]{:S(2)}) collective-permute-start(bf16[768,256]{1,0:T(8,128)(2,1)S(1)} %shard_map.104), channel_id=1, source_target_pairs={{0,8},{2,10},{4,12},{6,14},{8,16},{10,18},{12,20},{14,22},{16,24},... | collective-permute-start | bytes 1179656 | tf_op jit(solution)/shard_map/ppermute | solution.py:504
  18.9 27.5 %collective-permute-start.13 = (bf16[816,256]{1,0:T(8,128)(2,1)S(1)}, bf16[816,256]{1,0:T(8,128)(2,1)S(1)}, u32[]{:S(2)}, u32[]{:S(2)}) collective-permute-start(bf16[816,256]{1,0:T(8,128)(2,1)S(1)} %shard_map.113), channel_id=1, source_target_pairs={{0,24},{2,26},{4,28},{6,30},{8,0},{10,2},{12,4},{14,6},{16,8},{18,... | collective-permute-start | bytes 1253384 | tf_op jit(solution)/shard_map/ppermute | solution.py:504
  31.4 3.7 %collective-permute-start.7 = (f32[8,128]{1,0:T(8,128)S(1)}, f32[8,128]{1,0:T(8,128)S(1)}, u32[]{:S(2)}, u32[]{:S(2)}) collective-permute-start(f32[8,128]{1,0:T(8,128)S(1)} %get-tuple-element.78.refs_0_), channel_id=1, source_target_pairs={{0,8},{2,10},{4,12},{6,14},{8,0},{10,2},{12,4},{14,6},{16,24},{18,... | collective-permute-start | bytes 12296 | tf_op jit(solution)/shard_map/ppermute | solution.py:501
  35.1 8.6 %collective-permute-start.8 = (f32[8,128]{1,0:T(8,128)S(1)}, f32[8,128]{1,0:T(8,128)S(1)}, u32[]{:S(2)}, u32[]{:S(2)}) collective-permute-start(f32[8,128]{1,0:T(8,128)S(1)} %shard_map.109.refs_0_), channel_id=1, source_target_pairs={{0,16},{2,18},{4,20},{6,22},{8,24},{10,26},{12,28},{14,30},{16,0},... | collective-permute-start | bytes 12296 | tf_op jit(solution)/shard_map/ppermute | solution.py:501
  42.1 4.3 %collective-permute-start.14 = (f32[2,8,256]{2,1,0:T(8,128)S(1)}, f32[2,8,256]{2,1,0:T(8,128)S(1)}, u32[]{:S(2)}, u32[]{:S(2)}) collective-permute-start(f32[2,8,256]{2,1,0:T(8,128)S(1)} %get-tuple-element.70.refs_1_), channel_id=1, source_target_pairs={{0,24},{2,26},{4,28},{6,30},{8,0},{10,2},{12,4},{14,6},{16,8},{18,... | collective-permute-start | bytes 49160 | tf_op jit(solution)/shard_map/ppermute | solution.py:504
  43.7 1.2 %collective-permute-start.9 = (f32[8,128]{1,0:T(8,128)S(1)}, f32[8,128]{1,0:T(8,128)S(1)}, u32[]{:S(2)}, u32[]{:S(2)}) collective-permute-start(f32[8,128]{1,0:T(8,128)S(1)} %shard_map.110.refs_1_), channel_id=1, source_target_pairs={{0,1},{1,0},{2,3},{3,2},{4,5},{5,4},{6,7},{7,6},{8,9},{9,8},{10,11... | collective-permute-start | bytes 12296 | tf_op jit(solution)/shard_map/ppermute | solution.py:501
  44.9 8.3 %collective-permute-start.10 = (bf16[160,256]{1,0:T(8,128)(2,1)S(1)}, bf16[160,256]{1,0:T(8,128)(2,1)S(1)}, u32[]{:S(2)}, u32[]{:S(2)}) collective-permute-start(bf16[160,256]{1,0:T(8,128)(2,1)S(1)} %get-tuple-element.80), channel_id=1, source_target_pairs={{0,2},{2,0},{4,6},{6,4},{8,10},{10,8},{12,14},{14,12},{16,18},{18,... | collective-permute-start | bytes 245768 | tf_op jit(solution)/shard_map/ppermute | solution.py:501
  48.9 13.0 %collective-permute-start.15 = (bf16[256,256]{1,0:T(8,128)(2,1)S(1)}, bf16[256,256]{1,0:T(8,128)(2,1)S(1)}, u32[]{:S(2)}, u32[]{:S(2)}) collective-permute-start(bf16[256,256]{1,0:T(8,128)(2,1)S(1)} %get-tuple-element.92), channel_id=1, source_target_pairs={{0,2},{2,0},{4,6},{6,4},{8,10},{10,8},{12,14},{14,12},{16,18},{18,... | collective-permute-start | bytes 393224 | tf_op jit(solution)/shard_map/ppermute | solution.py:501
  49.8 12.1 %collective-permute-start.16 = (bf16[256,256]{1,0:T(8,128)(2,1)S(1)}, bf16[256,256]{1,0:T(8,128)(2,1)S(1)}, u32[]{:S(2)}, u32[]{:S(2)}) collective-permute-start(bf16[256,256]{1,0:T(8,128)(2,1)S(1)} %get-tuple-element.93), channel_id=1, source_target_pairs={{0,4},{2,6},{4,0},{6,2},{8,12},{10,14},{12,8},{14,10},{16,20},{18,... | collective-permute-start | bytes 393224 | tf_op jit(solution)/shard_map/ppermute | solution.py:501
  50.9 11.0 %collective-permute-start.17 = (bf16[256,256]{1,0:T(8,128)(2,1)S(1)}, bf16[256,256]{1,0:T(8,128)(2,1)S(1)}, u32[]{:S(2)}, u32[]{:S(2)}) collective-permute-start(bf16[256,256]{1,0:T(8,128)(2,1)S(1)} %get-tuple-element.94), channel_id=1, source_target_pairs={{0,6},{2,4},{4,2},{6,0},{8,14},{10,12},{12,10},{14,8},{16,22},{18,... | collective-permute-start | bytes 393224 | tf_op jit(solution)/shard_map/ppermute | solution.py:501
  52.4 8.7 %collective-permute-start.11 = (bf16[160,256]{1,0:T(8,128)(2,1)S(1)}, bf16[160,256]{1,0:T(8,128)(2,1)S(1)}, u32[]{:S(2)}, u32[]{:S(2)}) collective-permute-start(bf16[160,256]{1,0:T(8,128)(2,1)S(1)} %get-tuple-element.81), channel_id=1, source_target_pairs={{0,4},{2,6},{4,0},{6,2},{8,12},{10,14},{12,8},{14,10},{16,20},{18,... | collective-permute-start | bytes 245768 | tf_op jit(solution)/shard_map/ppermute | solution.py:501
  53.2 7.9 %collective-permute-start.12 = (bf16[160,256]{1,0:T(8,128)(2,1)S(1)}, bf16[160,256]{1,0:T(8,128)(2,1)S(1)}, u32[]{:S(2)}, u32[]{:S(2)}) collective-permute-start(bf16[160,256]{1,0:T(8,128)(2,1)S(1)} %get-tuple-element.82), channel_id=1, source_target_pairs={{0,6},{2,4},{4,2},{6,0},{8,14},{10,12},{12,10},{14,8},{16,22},{18,... | collective-permute-start | bytes 245768 | tf_op jit(solution)/shard_map/ppermute | solution.py:501

commit v4 on v1

--- a/solution.py
+++ b/solution.py
@@ -65,14 +65,15 @@
         return lax.rem(lax.axis_index("seq"), self.group)
 
 
-def pack_kernel(z, q, k, v, d, ids, mask, *refs):
+def pack_kernel(z, q, k, v, d, bias, ids, mask, *refs):
     kv, qd = refs[: z.group], refs[z.group : 2 * z.group]
-    slots, flags, sem = refs[2 * z.group :]
+    table, slots, flags, sem = refs[2 * z.group :]
     index = lax.axis_index("seq")
     me = z.me()
     copies = [
         pltpu.make_async_copy(ids.at[0], slots, sem.at[0]),
         pltpu.make_async_copy(mask, flags, sem.at[1]),
+        pltpu.make_async_copy(bias, table, sem.at[2]),
     ]
     for sources, dst in (((k, v), kv), ((q, d), qd)):
         for g in range(z.group):
@@ -414,21 +415,17 @@
     lax.fori_loop(0, z.pairs, each, 0)
 
 
-def seal_kernel(z, sides, dq, dk, dv, *refs):
-    sums, sends = refs[:sides], refs[sides:]
-    tok = z.tok
-    packs = []
-    for ref in sums:
-        split = thirds(ref[...]).astype(F32)
-        low = jnp.concatenate([split[16:24], jnp.zeros((8, z.buckets), F32)], axis=0)
-        packs.append(jnp.concatenate([split[0:16], low], axis=1).astype(BF16))
-    me = z.me()
+def seal_kernel(z, grads, *refs):
+    sources, sends = refs[:grads], refs[grads:]
     for k in range(z.group):
-        rows = at((me ^ k) * tok, tok)
-        for n, ref in enumerate((dq, dk, dv)):
-            sends[k][n * tok : (n + 1) * tok, :] = ref[rows, :]
-        for n, pack in enumerate(packs):
-            sends[k][3 * tok + n * CODE_ROWS : 3 * tok + (n + 1) * CODE_ROWS, :] = pack
+        rows = at((z.me() ^ k) * z.tok, z.tok)
+        for n, ref in enumerate(sources):
+            sends[k][n * z.tok : (n + 1) * z.tok, :] = ref[rows, :]
+
+
+def join_kernel(*refs):
+    for n, ref in enumerate(refs[:-1]):
+        refs[-1][8 * n : 8 * n + 8, :] = ref[...]
 
 
 def add_kernel(*refs):
@@ -439,7 +436,8 @@
 
 
 def unpack_kernel(z, sides, *refs):
-    got, outs, gb, held, sem = refs[: z.group], refs[z.group : -3], refs[-3], refs[-2], refs[-1]
+    got, sums = refs[: z.group], refs[z.group : 2 * z.group]
+    *outs, gb, held, sem = refs[2 * z.group :]
     me = z.me()
     copies = []
     for k in range(z.group):
@@ -453,10 +451,7 @@
     total = jnp.zeros(held.shape, F32)
     for k in range(z.group):
         for n in range(sides):
-            top = 3 * z.tok + n * CODE_ROWS
-            rows = got[k][top : top + CODE_ROWS, :].astype(F32)
-            sums = rows[0:8, 0 : z.buckets] + rows[8:16, 0 : z.buckets] + rows[0:8, z.buckets :]
-            wide = jnp.concatenate([sums[0 : z.hg]] * (held.shape[0] // z.hg), axis=0)
+            wide = jnp.concatenate([sums[k][8 * n : 8 * n + z.hg, :]] * (held.shape[0] // z.hg), axis=0)
             side = lax.axis_index("head") ^ n
             total = total + jnp.where(owner == side * z.group + (me ^ k), wide, 0.0)
     held[...] = total
@@ -497,17 +492,17 @@
     pack_bytes = group * (z.rows + 2 * tok) * z.cw * 2
     packed = call(
         bind(pack_kernel, z),
-        [((z.rows, z.cw), BF16)] * group + [((2 * tok, z.cw), BF16)] * group,
-        (queries, keys, values, grad_out, bucket_ids, block_mask),
-        spaces=[hbm] * 6,
+        [((z.rows, z.cw), BF16)] * group + [((2 * tok, z.cw), BF16)] * group + [((heads, buckets), F32)],
+        (queries, keys, values, grad_out, bias_table, bucket_ids, block_mask),
+        spaces=[hbm] * 7,
         scratch=[
             pltpu.VMEM((span, z.wide), jnp.int32),
             pltpu.SMEM((1, span), jnp.int32),
-            pltpu.SemaphoreType.DMA((4 * group + 2,)),
+            pltpu.SemaphoreType.DMA((4 * group + 3,)),
         ],
         limit=VMEM_BYTES - pack_bytes - (520 << 10),
     )
-    kv, qd = packed[:group], packed[group:]
+    kv, qd, table = packed[:group], packed[group : 2 * group], packed[2 * group]
     kv_got = [kv[0]] + [swap(kv[k], k) for k in range(1, group)]
     qd_got = [qd[0]] + [swap(qd[k], k) for k in range(1, group)]
     (kv_out,) = call(bind(kv_halo_kernel, z), [((z.halo * 2 * tok, z.cw), BF16)], kv_got)
@@ -527,7 +522,7 @@
         [((group * tok, z.cw), BF16)] * 2
         + [((near * z.pairs, tok, z.wide), F32), ((far * z.pairs, tok, z.wide), F32)]
         + [((group * CODE_ROWS, z.wide), F32)],
-        (*kv_got, bias_table),
+        (*kv_got, table),
         scratch=[pltpu.VMEM((group * span * z.hg * 8, z.wide), F32)],
     )
     qm, dom, wnear, dnear, *sums = call(
@@ -571,7 +566,7 @@
     halo_terms = call(
         bind(tail_kernel, z),
         [rows_of, rows_of, lanes_of, lanes_of],
-        (own_k, own_v, qd_halo, stats_halo, bias_table),
+        (own_k, own_v, qd_halo, stats_halo, table),
         scratch=[pltpu.VMEM((far * z.hg * 8, z.wide), F32)],
         flops=2 * far * z.pairs * unit,
     )
@@ -581,14 +576,14 @@
         (qm, dom, p16, s16, *halo_terms),
         flops=2 * (near + far) * z.pairs * unit,
     )
-    ret = call(
-        bind(seal_kernel, z, sides), [((3 * tok + sides * CODE_ROWS, z.cw), BF16)] * group, (dq, dk, dv, *sums_of)
-    )
-    ret_got = [ret[0]] + [swap(ret[k], k) for k in range(1, group)]
+    ret = call(bind(seal_kernel, z, 3), [((3 * tok, z.cw), BF16)] * group, (dq, dk, dv))
+    back = [ret[0]] + [swap(ret[k], k) for k in range(1, group)]
+    (joined,) = call(join_kernel, [((8 * sides, buckets), F32)], sums_of)
+    spread = [joined] + [swap(joined, k) for k in range(1, group)]
     return call(
         bind(unpack_kernel, z, sides),
         [((tok, width), BF16)] * 3 + [((heads * sides, buckets), F32)],
-        ret_got,
+        (*back, *spread),
         out_space=hbm,
         scratch=[pltpu.VMEM((heads * sides, buckets), F32), pltpu.SemaphoreType.DMA((3 * group + 1,))],
     )

time: 54.5 us -> 58 us (1.064)
  starting transfers between devices: 25.9 us -> 28.6 us
  waiting for transfers between devices: 15.1 us -> 15.8 us
    ppermute x1, starting transfers between devices: 2.47 us -> 4.51 us  [body(): lax.ppermute(stats, 'seq', [(i, (i - group) % blocks) for i in range(bloc...]
    ppermute x12 -> x15, waiting for transfers between devices: 14.2 us -> 14.9 us  [swap(): lax.ppermute(value, axis, [(i, i ^ by) for i in range(lax.axis_size(axis))])]
    ppermute x12 -> x15, starting transfers between devices: 18.8 us -> 19.5 us  [swap(): lax.ppermute(value, axis, [(i, i ^ by) for i in range(lax.axis_size(axis))])]
    pallas_call x14 -> x15, Pallas kernels: 12.5 us -> 12.6 us  [call(): pl.pallas_call(kernel, out_shape=tuple((out_space(s, d) for s, d in outs)...]
  transfers between devices with their start and end apart: 15 -> 18, of which waited for: 6 -> 8; matrix products, arithmetic and copies ran while one was open for 0% -> 0% of each run, Pallas kernels for 19% -> 13%
where the time goes in v4:
time: 58 us; the launch traced here: 57.8 us
  starting transfers between devices  28.6 us (49%)
  waiting for transfers between devices  15.8 us (27%)
  Pallas kernels  12.6 us (22%)
  between operations  0.76 us (1%)
    ppermute x15, starting transfers between devices, swap(): lax.ppermute(value, axis, [(i, i ^ by) for i in range(lax.axis_size(axis))])  19.5 us
    ppermute x15, waiting for transfers between devices, swap(): lax.ppermute(value, axis, [(i, i ^ by) for i in range(lax.axis_size(axis))])  14.9 us
    pallas_call x15, Pallas kernels, call(): pl.pallas_call(kernel, out_shape=tuple((out_space(s, d) for s, d in outs)...  12.6 us
    ppermute x2, starting transfers between devices, shifted(): lax.ppermute(value, 'seq', [(i, i + by) for i in range(blocks) if 0 <= i...  4.64 us
    ppermute x1, starting transfers between devices, body(): lax.ppermute(stats, 'seq', [(i, (i - group) % blocks) for i in range(bloc...  4.51 us
  transfers between devices with their start and end apart: 18, of which 8 were waited for; matrix products, arithmetic and copies ran while one was open for 0% of the time, Pallas kernels for 13%

profile of v4, /device:TPU:0, one launch (start us, length us, event | category | flops | bytes accessed | tf_op | source)
XLA Modules:
  0.0 57.8 jit_solution(5964419796179250110)
XLA Ops:
  0.6 1.5 %shard_map.102 = (bf16[272,256]{1,0:T(8,128)(2,1)S(1)}, bf16[272,256]{1,0:T(8,128)(2,1)S(1)}, bf16[272,256]{1,0:T(8,128)(2,1)S(1)}, bf16[272,256]{1,0:T(8,128)(2...) custom-call(bf16[128,1024]{1,0:T(8,128)(2,1)} %refs_0_.1, ...), custom_call_target="tpu_custom_call" | custom-call | bytes 1060880 | tf_op jit(solution)/shard_map/pallas_call | solution.py:34
  2.1 3.0 %collective-permute-start = (bf16[272,256]{1,0:T(8,128)(2,1)S(1)}, bf16[272,256]{1,0:T(8,128)(2,1)S(1)}, u32[]{:S(2)}, u32[]{:S(2)}) collective-permute-start(bf16[272,256]{1,0:T(8,128)(2,1)S(1)} %get-tuple-element.44), channel_id=1, source_target_pairs={{0,2},{2,0},{4,6},{6,4},{8,10},{10,8},{12,14},{14,12},{16,18},{18,... | collective-permute-start | bytes 417800 | tf_op jit(solution)/shard_map/ppermute | solution.py:482
  5.1 1.5 %collective-permute-start.1 = (bf16[272,256]{1,0:T(8,128)(2,1)S(1)}, bf16[272,256]{1,0:T(8,128)(2,1)S(1)}, u32[]{:S(2)}, u32[]{:S(2)}) collective-permute-start(bf16[272,256]{1,0:T(8,128)(2,1)S(1)} %get-tuple-element.45), channel_id=1, source_target_pairs={{0,4},{2,6},{4,0},{6,2},{8,12},{10,14},{12,8},{14,10},{16,20},{18,... | collective-permute-start | bytes 417800 | tf_op jit(solution)/shard_map/ppermute | solution.py:482
  6.6 0.0 collective-permute-start.2
  6.7 1.9 %collective-permute-start.4 = (bf16[256,256]{1,0:T(8,128)(2,1)S(1)}, bf16[256,256]{1,0:T(8,128)(2,1)S(1)}, u32[]{:S(2)}, u32[]{:S(2)}) collective-permute-start(bf16[256,256]{1,0:T(8,128)(2,1)S(1)} %get-tuple-element.51), channel_id=1, source_target_pairs={{0,2},{2,0},{4,6},{6,4},{8,10},{10,8},{12,14},{14,12},{16,18},{18,... | collective-permute-start | bytes 393224 | tf_op jit(solution)/shard_map/ppermute | solution.py:482
  8.6 1.5 %collective-permute-start.5 = (bf16[256,256]{1,0:T(8,128)(2,1)S(1)}, bf16[256,256]{1,0:T(8,128)(2,1)S(1)}, u32[]{:S(2)}, u32[]{:S(2)}) collective-permute-start(bf16[256,256]{1,0:T(8,128)(2,1)S(1)} %get-tuple-element.52), channel_id=1, source_target_pairs={{0,4},{2,6},{4,0},{6,2},{8,12},{10,14},{12,8},{14,10},{16,20},{18,... | collective-permute-start | bytes 393224 | tf_op jit(solution)/shard_map/ppermute | solution.py:482
  10.1 0.0 collective-permute-done.refs_1_.refs_5_
  10.1 2.5 %collective-permute-start.6 = (bf16[256,256]{1,0:T(8,128)(2,1)S(1)}, bf16[256,256]{1,0:T(8,128)(2,1)S(1)}, u32[]{:S(2)}, u32[]{:S(2)}) collective-permute-start(bf16[256,256]{1,0:T(8,128)(2,1)S(1)} %get-tuple-element.53), channel_id=1, source_target_pairs={{0,6},{2,4},{4,2},{6,0},{8,14},{10,12},{12,10},{14,8},{16,22},{18,... | collective-permute-start | bytes 393224 | tf_op jit(solution)/shard_map/ppermute | solution.py:482
  12.6 1.7 %collective-permute-done.1.refs_2_.refs_6_ = bf16[272,256]{1,0:T(8,128)(2,1)S(1)} collective-permute-done((bf16[272,256]{1,0:T(8,128)(2,1)S(1)}, bf16[272,256]{1,0:T(8,128)(2,1)S(1)}, u32[]{:S(2)}, u32[]{:S(2)}) %collective-permute-start.1) | collective-permute-done | bytes 139296 | tf_op jit(solution)/shard_map/ppermute | solution.py:482
  14.3 0.0 collective-permute-done.2.refs_3_.refs_7_
  14.3 3.3 %collective-permute-start.3 = (bf16[768,256]{1,0:T(8,128)(2,1)S(1)}, bf16[768,256]{1,0:T(8,128)(2,1)S(1)}, u32[]{:S(2)}, u32[]{:S(2)}) collective-permute-start(bf16[768,256]{1,0:T(8,128)(2,1)S(1)} %shard_map.104), channel_id=1, source_target_pairs={{0,8},{2,10},{4,12},{6,14},{8,16},{10,18},{12,20},{14,22},{16,24},... | collective-permute-start | bytes 1179656 | tf_op jit(solution)/shard_map/ppermute | solution.py:485
  17.7 0.0 collective-permute-done.4.refs_1_
  17.7 1.2 %collective-permute-done.5.refs_2_ = bf16[256,256]{1,0:T(8,128)(2,1)S(1)} collective-permute-done((bf16[256,256]{1,0:T(8,128)(2,1)S(1)}, bf16[256,256]{1,0:T(8,128)(2,1)S(1)}, u32[]{:S(2)}, u32[]{:S(2)}) %collective-permute-start.5) | collective-permute-done | bytes 131104 | tf_op jit(solution)/shard_map/ppermute | solution.py:482
  18.9 0.0 collective-permute-done.6.refs_3_
  18.9 1.3 %collective-permute-start.7 = (bf16[816,256]{1,0:T(8,128)(2,1)S(1)}, bf16[816,256]{1,0:T(8,128)(2,1)S(1)}, u32[]{:S(2)}, u32[]{:S(2)}) collective-permute-start(bf16[816,256]{1,0:T(8,128)(2,1)S(1)} %shard_map.109), channel_id=1, source_target_pairs={{8,0},{10,2},{12,4},{14,6},{16,8},{18,10},{20,12},{22,14},{24,16},... | collective-permute-start | bytes 1253384 | tf_op jit(solution)/shard_map/ppermute | solution.py:485
  20.2 1.4 %shard_map.103 = (bf16[512,256]{1,0:T(8,128)(2,1)S(1)}, bf16[512,256]{1,0:T(8,128)(2,1)S(1)}, f32[20,128,256]{2,1,0:T(8,128)S(1)}, f32[12,128,256]{2,1,0:T(8,128)S(1)}, f32[64,256]{1,0:T(8,128)S(1)}) custom-call(bf16[272,256]{1,0:T(8,128)(2,1)S(1)} %get-tuple-element.43.refs_0_.refs_4_, bf16[272,256]{1,0:T(8,128)(2,1)S(1)} %collective-permute-done.refs_1_.refs_5_, ...), custom_call_target="tpu_custom_call" | custom-call | bytes 565248 | tf_op jit(solution)/shard_map/pallas_call | solution.py:34
  21.6 1.6 %shard_map.105 = (bf16[2,1024,128]{2,1,0:T(8,128)(2,1)S(1)}, bf16[2,1024,128]{2,1,0:T(8,128)(2,1)S(1)}, f32[20,128,256]{2,1,0:T(8,128)S(1)}, f32[20,128,256]{2,1...) custom-call(bf16[256,256]{1,0:T(8,128)(2,1)S(1)} %get-tuple-element.50.refs_0_, ...), custom_call_target="tpu_custom_call" | custom-call | flops 335544320 | bytes 3670016 | tf_op jit(solution)/shard_map/pallas_call | solution.py:34
  23.2 0.9 %collective-permute-done.3.refs_0_.refs_1_ = bf16[768,256]{1,0:T(8,128)(2,1)S(1)} collective-permute-done((bf16[768,256]{1,0:T(8,128)(2,1)S(1)}, bf16[768,256]{1,0:T(8,128)(2,1)S(1)}, u32[]{:S(2)}, u32[]{:S(2)}) %collective-permute-start.3) | collective-permute-done | bytes 393248 | tf_op jit(solution)/shard_map/ppermute | solution.py:485
  24.1 1.6 %shard_map.106 = (f32[2,8,256]{2,1,0:T(8,128)S(1)}, f32[20,256]{1,0:T(8,128)S(1)}, f32[12,256]{1,0:T(8,128)S(1)}, f32[12,128,256]{2,1,0:T(8,128)S(1)}, f32[12,12...) custom-call(bf16[768,256]{1,0:T(8,128)(2,1)S(1)} %collective-permute-done.3.refs_0_.refs_1_, ...), custom_call_target="tpu_custom_call" | custom-call | flops 201326592 | bytes 3076096 | tf_op jit(solution)/shard_map/pallas_call | solution.py:34
  25.7 4.5 %collective-permute-start.8 = (f32[2,8,256]{2,1,0:T(8,128)S(1)}, f32[2,8,256]{2,1,0:T(8,128)S(1)}, u32[]{:S(2)}, u32[]{:S(2)}) collective-permute-start(f32[2,8,256]{2,1,0:T(8,128)S(1)} %get-tuple-element.62.refs_1_), channel_id=1, source_target_pairs={{0,24},{2,26},{4,28},{6,30},{8,0},{10,2},{12,4},{14,6},{16,8},{18,... | collective-permute-start | bytes 49160 | tf_op jit(solution)/shard_map/ppermute | solution.py:541
  30.2 2.2 %shard_map.107 = (bf16[2,512,1024]{2,1,0:T(8,128)(2,1)S(1)}, bf16[2,896,1024]{2,1,0:T(8,128)(2,1)S(1)}, f32[8,128]{1,0:T(8,128)S(1)}) custom-call(f32[64,256]{1,0:T(8,128)S(1)} %get-tuple-element.49.refs_0_, f32[2,8,256]{2,1,0:T(8,128)S(1)} %get-tuple-element.62.refs_1_, f32[20,256]{1,0:T(8,128)S(1)} %get-tuple-element.63.refs_2_, ...), custom_call_target="tpu_custom_call" | custom-call | bytes 8503296 | tf_op jit(solution)/shard_map/pallas_call | solution.py:34
  32.3 0.8 %shard_map.108.refs_0_ = bf16[512,256]{1,0:T(8,128)(2,1)S(1)} custom-call(bf16[512,256]{1,0:T(8,128)(2,1)S(1)} %get-tuple-element.48.refs_4_.refs_0_, bf16[768,256]{1,0:T(8,128)(2,1)S(1)} %collective-permute-done.3.refs_0_.refs_1_, bf16[2,896,1024]{2,1,0:T(8,128)(2,1)S(1)} %get-tuple-element.69.refs_2_.refs_3_), custom_call_target="tpu_custom_call" | custom-call | flops 268435456 | bytes 4325376 | tf_op jit(solution)/shard_map/pallas_call | solution.py:34
  33.2 0.0 collective-permute-done.8.refs_3_
  33.2 0.0 collective-permute-done.7.refs_2_
  33.2 1.0 %shard_map.110 = (bf16[2,768,128]{2,1,0:T(8,128)(2,1)S(1)}, bf16[2,768,128]{2,1,0:T(8,128)(2,1)S(1)}, bf16[2,512,768]{2,1,0:T(8,128)(2,1)S(1)}, bf16[2,512,768]{2,1,0:T(8,128)(2,1)S(1)}) custom-call(bf16[512,256]{1,0:T(8,128)(2,1)S(1)} %get-tuple-element.48.refs_4_.refs_0_, bf16[512,256]{1,0:T(8,128)(2,1)S(1)} %get-tuple-element.54.refs_5_.refs_1_, ...), custom_call_target="tpu_custom_call" | custom-call | flops 201326592 | bytes 966656 | tf_op jit(solution)/shard_map/pallas_call | solution.py:34
  34.2 1.5 %shard_map.111 = (bf16[512,256]{1,0:T(8,128)(2,1)S(1)}, bf16[512,256]{1,0:T(8,128)(2,1)S(1)}) custom-call(bf16[2,1024,128]{2,1,0:T(8,128)(2,1)S(1)} %get-tuple-element.56.refs_1_.refs_0_, bf16[2,1024,128]{2,1,0:T(8,128)(2,1)S(1)} %get-tuple-element.57.refs_2_.refs_1_, bf16[2,512,1024]{2,1,0:T(8,128)(2,1)S(1)} %get-tuple-element.70.refs_2_, ...), custom_call_target="tpu_custom_call" | custom-call | flops 536870912 | bytes 10747904 | tf_op jit(solution)/shard_map/pallas_call | solution.py:34
  35.6 0.1 shard_map.112
  35.7 1.5 %collective-permute-start.9 = (bf16[384,256]{1,0:T(8,128)(2,1)S(1)}, bf16[384,256]{1,0:T(8,128)(2,1)S(1)}, u32[]{:S(2)}, u32[]{:S(2)}) collective-permute-start(bf16[384,256]{1,0:T(8,128)(2,1)S(1)} %get-tuple-element.78), channel_id=1, source_target_pairs={{0,2},{2,0},{4,6},{6,4},{8,10},{10,8},{12,14},{14,12},{16,18},{18,... | collective-permute-start | bytes 589832 | tf_op jit(solution)/shard_map/ppermute | solution.py:482
  37.2 0.5 collective-permute-start.10
  37.7 1.6 %collective-permute-start.11 = (bf16[384,256]{1,0:T(8,128)(2,1)S(1)}, bf16[384,256]{1,0:T(8,128)(2,1)S(1)}, u32[]{:S(2)}, u32[]{:S(2)}) collective-permute-start(bf16[384,256]{1,0:T(8,128)(2,1)S(1)} %get-tuple-element.80), channel_id=1, source_target_pairs={{0,6},{2,4},{4,2},{6,0},{8,14},{10,12},{12,10},{14,8},{16,22},{18,... | collective-permute-start | bytes 589832 | tf_op jit(solution)/shard_map/ppermute | solution.py:482
  39.3 0.0 collective-permute-start.12
  39.3 3.6 %collective-permute-done.12.refs_1_ = f32[8,128]{1,0:T(8,128)S(1)} collective-permute-done((f32[8,128]{1,0:T(8,128)S(1)}, f32[8,128]{1,0:T(8,128)S(1)}, u32[]{:S(2)}, u32[]{:S(2)}) %collective-permute-start.12) | collective-permute-done | bytes 4128 | tf_op jit(solution)/shard_map/ppermute | solution.py:482
  42.9 1.1 %collective-permute-start.13 = (f32[8,128]{1,0:T(8,128)S(1)}, f32[8,128]{1,0:T(8,128)S(1)}, u32[]{:S(2)}, u32[]{:S(2)}) collective-permute-start(f32[8,128]{1,0:T(8,128)S(1)} %shard_map.113.refs_0_), channel_id=1, source_target_pairs={{0,16},{2,18},{4,20},{6,22},{8,24},{10,26},{12,28},{14,30},{16,0},... | collective-permute-start | bytes 12296 | tf_op jit(solution)/shard_map/ppermute | solution.py:482
  43.9 3.5 %collective-permute-done.13.refs_1_ = f32[8,128]{1,0:T(8,128)S(1)} collective-permute-done((f32[8,128]{1,0:T(8,128)S(1)}, f32[8,128]{1,0:T(8,128)S(1)}, u32[]{:S(2)}, u32[]{:S(2)}) %collective-permute-start.13) | collective-permute-done | bytes 4128 | tf_op jit(solution)/shard_map/ppermute | solution.py:482
  47.4 0.0 collective-permute-start.14
  47.4 1.2 %collective-permute-done.14.refs_1_ = f32[8,128]{1,0:T(8,128)S(1)} collective-permute-done((f32[8,128]{1,0:T(8,128)S(1)}, f32[8,128]{1,0:T(8,128)S(1)}, u32[]{:S(2)}, u32[]{:S(2)}) %collective-permute-start.14) | collective-permute-done | bytes 4128 | tf_op jit(solution)/shard_map/ppermute | solution.py:482
  48.6 1.4 %collective-permute-start.17 = (f32[16,128]{1,0:T(8,128)S(1)}, f32[16,128]{1,0:T(8,128)S(1)}, u32[]{:S(2)}, u32[]{:S(2)}) collective-permute-start(f32[16,128]{1,0:T(8,128)S(1)} %shard_map.115.refs_4_), channel_id=1, source_target_pairs={{0,6},{2,4},{4,2},{6,0},{8,14},{10,12},{12,10},{14,8},{16,22},{18,... | collective-permute-start | bytes 24584 | tf_op jit(solution)/shard_map/ppermute | solution.py:482
  49.9 1.5 %collective-permute-start.16 = (f32[16,128]{1,0:T(8,128)S(1)}, f32[16,128]{1,0:T(8,128)S(1)}, u32[]{:S(2)}, u32[]{:S(2)}) collective-permute-start(f32[16,128]{1,0:T(8,128)S(1)} %shard_map.115.refs_4_), channel_id=1, source_target_pairs={{0,4},{2,6},{4,0},{6,2},{8,12},{10,14},{12,8},{14,10},{16,20},{18,... | collective-permute-start | bytes 24584 | tf_op jit(solution)/shard_map/ppermute | solution.py:482
  51.5 1.7 %collective-permute-done.17.refs_7_ = f32[16,128]{1,0:T(8,128)S(1)} collective-permute-done((f32[16,128]{1,0:T(8,128)S(1)}, f32[16,128]{1,0:T(8,128)S(1)}, u32[]{:S(2)}, u32[]{:S(2)}) %collective-permute-start.17) | collective-permute-done | bytes 8224 | tf_op jit(solution)/shard_map/ppermute | solution.py:482
  53.1 1.4 %collective-permute-start.15 = (f32[16,128]{1,0:T(8,128)S(1)}, f32[16,128]{1,0:T(8,128)S(1)}, u32[]{:S(2)}, u32[]{:S(2)}) collective-permute-start(f32[16,128]{1,0:T(8,128)S(1)} %shard_map.115.refs_4_), channel_id=1, source_target_pairs={{0,2},{2,0},{4,6},{6,4},{8,10},{10,8},{12,14},{14,12},{16,18},{18,... | collective-permute-start | bytes 24584 | tf_op jit(solution)/shard_map/ppermute | solution.py:482
  54.5 0.0 collective-permute-done.16.refs_6_
  54.5 2.2 %collective-permute-done.15.refs_5_ = f32[16,128]{1,0:T(8,128)S(1)} collective-permute-done((f32[16,128]{1,0:T(8,128)S(1)}, f32[16,128]{1,0:T(8,128)S(1)}, u32[]{:S(2)}, u32[]{:S(2)}) %collective-permute-start.15) | collective-permute-done | bytes 8224 | tf_op jit(solution)/shard_map/ppermute | solution.py:482
  56.8 0.0 collective-permute-done.9.refs_1_
  56.8 0.0 collective-permute-done.10.refs_2_
  56.8 0.0 collective-permute-done.11.refs_3_
  56.8 1.0 %shard_map.116 = (bf16[128,1024]{1,0:T(8,128)(2,1)}, bf16[128,1024]{1,0:T(8,128)(2,1)}, bf16[128,1024]{1,0:T(8,128)(2,1)}, f32[32,128]{1,0:T(8,128)}) custom-call(bf16[384,256]{1,0:T(8,128)(2,1)S(1)} %get-tuple-element.77.refs_0_, bf16[384,256]{1,0:T(8,128)(2,1)S(1)} %collective-permute-done.9.refs_1_, bf16[384,256]{1,0:T(8,128)(2,1)S(1)} %collective-permute-done.10.refs_2_, ...), custom_call_target="tpu_custom_call" | custom-call | bytes 819200 | tf_op jit(solution)/shard_map/pallas_call | solution.py:34
  (5 shorter events, 0.1 us)
Async XLA Ops:
  2.1 8.0 %collective-permute-start = (bf16[272,256]{1,0:T(8,128)(2,1)S(1)}, bf16[272,256]{1,0:T(8,128)(2,1)S(1)}, u32[]{:S(2)}, u32[]{:S(2)}) collective-permute-start(bf16[272,256]{1,0:T(8,128)(2,1)S(1)} %get-tuple-element.44), channel_id=1, source_target_pairs={{0,2},{2,0},{4,6},{6,4},{8,10},{10,8},{12,14},{14,12},{16,18},{18,... | collective-permute-start | bytes 417800 | tf_op jit(solution)/shard_map/ppermute | solution.py:482
  5.1 9.2 %collective-permute-start.1 = (bf16[272,256]{1,0:T(8,128)(2,1)S(1)}, bf16[272,256]{1,0:T(8,128)(2,1)S(1)}, u32[]{:S(2)}, u32[]{:S(2)}) collective-permute-start(bf16[272,256]{1,0:T(8,128)(2,1)S(1)} %get-tuple-element.45), channel_id=1, source_target_pairs={{0,4},{2,6},{4,0},{6,2},{8,12},{10,14},{12,8},{14,10},{16,20},{18,... | collective-permute-start | bytes 417800 | tf_op jit(solution)/shard_map/ppermute | solution.py:482
  6.6 7.6 %collective-permute-start.2 = (bf16[272,256]{1,0:T(8,128)(2,1)S(1)}, bf16[272,256]{1,0:T(8,128)(2,1)S(1)}, u32[]{:S(2)}, u32[]{:S(2)}) collective-permute-start(bf16[272,256]{1,0:T(8,128)(2,1)S(1)} %get-tuple-element.46), channel_id=1, source_target_pairs={{0,6},{2,4},{4,2},{6,0},{8,14},{10,12},{12,10},{14,8},{16,22},{18,... | collective-permute-start | bytes 417800 | tf_op jit(solution)/shard_map/ppermute | solution.py:482
  6.7 11.0 %collective-permute-start.4 = (bf16[256,256]{1,0:T(8,128)(2,1)S(1)}, bf16[256,256]{1,0:T(8,128)(2,1)S(1)}, u32[]{:S(2)}, u32[]{:S(2)}) collective-permute-start(bf16[256,256]{1,0:T(8,128)(2,1)S(1)} %get-tuple-element.51), channel_id=1, source_target_pairs={{0,2},{2,0},{4,6},{6,4},{8,10},{10,8},{12,14},{14,12},{16,18},{18,... | collective-permute-start | bytes 393224 | tf_op jit(solution)/shard_map/ppermute | solution.py:482
  8.6 10.2 %collective-permute-start.5 = (bf16[256,256]{1,0:T(8,128)(2,1)S(1)}, bf16[256,256]{1,0:T(8,128)(2,1)S(1)}, u32[]{:S(2)}, u32[]{:S(2)}) collective-permute-start(bf16[256,256]{1,0:T(8,128)(2,1)S(1)} %get-tuple-element.52), channel_id=1, source_target_pairs={{0,4},{2,6},{4,0},{6,2},{8,12},{10,14},{12,8},{14,10},{16,20},{18,... | collective-permute-start | bytes 393224 | tf_op jit(solution)/shard_map/ppermute | solution.py:482
  10.1 8.7 %collective-permute-start.6 = (bf16[256,256]{1,0:T(8,128)(2,1)S(1)}, bf16[256,256]{1,0:T(8,128)(2,1)S(1)}, u32[]{:S(2)}, u32[]{:S(2)}) collective-permute-start(bf16[256,256]{1,0:T(8,128)(2,1)S(1)} %get-tuple-element.53), channel_id=1, source_target_pairs={{0,6},{2,4},{4,2},{6,0},{8,14},{10,12},{12,10},{14,8},{16,22},{18,... | collective-permute-start | bytes 393224 | tf_op jit(solution)/shard_map/ppermute | solution.py:482
  14.3 9.8 %collective-permute-start.3 = (bf16[768,256]{1,0:T(8,128)(2,1)S(1)}, bf16[768,256]{1,0:T(8,128)(2,1)S(1)}, u32[]{:S(2)}, u32[]{:S(2)}) collective-permute-start(bf16[768,256]{1,0:T(8,128)(2,1)S(1)} %shard_map.104), channel_id=1, source_target_pairs={{0,8},{2,10},{4,12},{6,14},{8,16},{10,18},{12,20},{14,22},{16,24},... | collective-permute-start | bytes 1179656 | tf_op jit(solution)/shard_map/ppermute | solution.py:485
  18.9 14.3 %collective-permute-start.7 = (bf16[816,256]{1,0:T(8,128)(2,1)S(1)}, bf16[816,256]{1,0:T(8,128)(2,1)S(1)}, u32[]{:S(2)}, u32[]{:S(2)}) collective-permute-start(bf16[816,256]{1,0:T(8,128)(2,1)S(1)} %shard_map.109), channel_id=1, source_target_pairs={{8,0},{10,2},{12,4},{14,6},{16,8},{18,10},{20,12},{22,14},{24,16},... | collective-permute-start | bytes 1253384 | tf_op jit(solution)/shard_map/ppermute | solution.py:485
  25.7 7.5 %collective-permute-start.8 = (f32[2,8,256]{2,1,0:T(8,128)S(1)}, f32[2,8,256]{2,1,0:T(8,128)S(1)}, u32[]{:S(2)}, u32[]{:S(2)}) collective-permute-start(f32[2,8,256]{2,1,0:T(8,128)S(1)} %get-tuple-element.62.refs_1_), channel_id=1, source_target_pairs={{0,24},{2,26},{4,28},{6,30},{8,0},{10,2},{12,4},{14,6},{16,8},{18,... | collective-permute-start | bytes 49160 | tf_op jit(solution)/shard_map/ppermute | solution.py:541
  35.7 21.1 %collective-permute-start.9 = (bf16[384,256]{1,0:T(8,128)(2,1)S(1)}, bf16[384,256]{1,0:T(8,128)(2,1)S(1)}, u32[]{:S(2)}, u32[]{:S(2)}) collective-permute-start(bf16[384,256]{1,0:T(8,128)(2,1)S(1)} %get-tuple-element.78), channel_id=1, source_target_pairs={{0,2},{2,0},{4,6},{6,4},{8,10},{10,8},{12,14},{14,12},{16,18},{18,... | collective-permute-start | bytes 589832 | tf_op jit(solution)/shard_map/ppermute | solution.py:482
  37.2 19.6 %collective-permute-start.10 = (bf16[384,256]{1,0:T(8,128)(2,1)S(1)}, bf16[384,256]{1,0:T(8,128)(2,1)S(1)}, u32[]{:S(2)}, u32[]{:S(2)}) collective-permute-start(bf16[384,256]{1,0:T(8,128)(2,1)S(1)} %get-tuple-element.79), channel_id=1, source_target_pairs={{0,4},{2,6},{4,0},{6,2},{8,12},{10,14},{12,8},{14,10},{16,20},{18,... | collective-permute-start | bytes 589832 | tf_op jit(solution)/shard_map/ppermute | solution.py:482
  37.7 19.1 %collective-permute-start.11 = (bf16[384,256]{1,0:T(8,128)(2,1)S(1)}, bf16[384,256]{1,0:T(8,128)(2,1)S(1)}, u32[]{:S(2)}, u32[]{:S(2)}) collective-permute-start(bf16[384,256]{1,0:T(8,128)(2,1)S(1)} %get-tuple-element.80), channel_id=1, source_target_pairs={{0,6},{2,4},{4,2},{6,0},{8,14},{10,12},{12,10},{14,8},{16,22},{18,... | collective-permute-start | bytes 589832 | tf_op jit(solution)/shard_map/ppermute | solution.py:482
  39.3 3.6 %collective-permute-start.12 = (f32[8,128]{1,0:T(8,128)S(1)}, f32[8,128]{1,0:T(8,128)S(1)}, u32[]{:S(2)}, u32[]{:S(2)}) collective-permute-start(f32[8,128]{1,0:T(8,128)S(1)} %get-tuple-element.81.refs_0_), channel_id=1, source_target_pairs={{0,8},{2,10},{4,12},{6,14},{8,0},{10,2},{12,4},{14,6},{16,24},{18,... | collective-permute-start | bytes 12296 | tf_op jit(solution)/shard_map/ppermute | solution.py:482
  42.9 4.5 %collective-permute-start.13 = (f32[8,128]{1,0:T(8,128)S(1)}, f32[8,128]{1,0:T(8,128)S(1)}, u32[]{:S(2)}, u32[]{:S(2)}) collective-permute-start(f32[8,128]{1,0:T(8,128)S(1)} %shard_map.113.refs_0_), channel_id=1, source_target_pairs={{0,16},{2,18},{4,20},{6,22},{8,24},{10,26},{12,28},{14,30},{16,0},... | collective-permute-start | bytes 12296 | tf_op jit(solution)/shard_map/ppermute | solution.py:482
  47.4 1.2 %collective-permute-start.14 = (f32[8,128]{1,0:T(8,128)S(1)}, f32[8,128]{1,0:T(8,128)S(1)}, u32[]{:S(2)}, u32[]{:S(2)}) collective-permute-start(f32[8,128]{1,0:T(8,128)S(1)} %shard_map.114.refs_0_), channel_id=1, source_target_pairs={{0,1},{1,0},{2,3},{3,2},{4,5},{5,4},{6,7},{7,6},{8,9},{9,8},{10,11... | collective-permute-start | bytes 12296 | tf_op jit(solution)/shard_map/ppermute | solution.py:482
  48.6 4.5 %collective-permute-start.17 = (f32[16,128]{1,0:T(8,128)S(1)}, f32[16,128]{1,0:T(8,128)S(1)}, u32[]{:S(2)}, u32[]{:S(2)}) collective-permute-start(f32[16,128]{1,0:T(8,128)S(1)} %shard_map.115.refs_4_), channel_id=1, source_target_pairs={{0,6},{2,4},{4,2},{6,0},{8,14},{10,12},{12,10},{14,8},{16,22},{18,... | collective-permute-start | bytes 24584 | tf_op jit(solution)/shard_map/ppermute | solution.py:482
  49.9 4.6 %collective-permute-start.16 = (f32[16,128]{1,0:T(8,128)S(1)}, f32[16,128]{1,0:T(8,128)S(1)}, u32[]{:S(2)}, u32[]{:S(2)}) collective-permute-start(f32[16,128]{1,0:T(8,128)S(1)} %shard_map.115.refs_4_), channel_id=1, source_target_pairs={{0,4},{2,6},{4,0},{6,2},{8,12},{10,14},{12,8},{14,10},{16,20},{18,... | collective-permute-start | bytes 24584 | tf_op jit(solution)/shard_map/ppermute | solution.py:482
  53.1 3.7 %collective-permute-start.15 = (f32[16,128]{1,0:T(8,128)S(1)}, f32[16,128]{1,0:T(8,128)S(1)}, u32[]{:S(2)}, u32[]{:S(2)}) collective-permute-start(f32[16,128]{1,0:T(8,128)S(1)} %shard_map.115.refs_4_), channel_id=1, source_target_pairs={{0,2},{2,0},{4,6},{6,4},{8,10},{10,8},{12,14},{14,12},{16,18},{18,... | collective-permute-start | bytes 24584 | tf_op jit(solution)/shard_map/ppermute | solution.py:482

commit v5 on v4

--- a/solution.py
+++ b/solution.py
@@ -424,8 +424,9 @@
 
 
 def join_kernel(*refs):
+    rows = refs[0].shape[0]
     for n, ref in enumerate(refs[:-1]):
-        refs[-1][8 * n : 8 * n + 8, :] = ref[...]
+        refs[-1][rows * n : rows * (n + 1), :] = ref[...]
 
 
 def add_kernel(*refs):
@@ -435,9 +436,8 @@
     refs[-1][...] = total
 
 
-def unpack_kernel(z, sides, *refs):
-    got, sums = refs[: z.group], refs[z.group : 2 * z.group]
-    *outs, gb, held, sem = refs[2 * z.group :]
+def unpack_kernel(z, *refs):
+    got, outs, sem = refs[: z.group], refs[z.group : -1], refs[-1]
     me = z.me()
     copies = []
     for k in range(z.group):
@@ -447,18 +447,24 @@
             copies.append(pltpu.make_async_copy(src, out.at[:, cols], sem.at[len(copies)]))
     for copy in copies:
         copy.start()
+    for copy in copies:
+        copy.wait()
+
+
+def spread_kernel(z, sides, mine, other, gb, held, sem):
+    me = z.me()
     owner = lax.broadcasted_iota(jnp.int32, held.shape, 0) // z.hg
     total = jnp.zeros(held.shape, F32)
-    for k in range(z.group):
-        for n in range(sides):
-            wide = jnp.concatenate([sums[k][8 * n : 8 * n + z.hg, :]] * (held.shape[0] // z.hg), axis=0)
-            side = lax.axis_index("head") ^ n
-            total = total + jnp.where(owner == side * z.group + (me ^ k), wide, 0.0)
+    half = z.group * sides // 2
+    for m in range(z.group * sides):
+        ref, row = (mine, 8 * m) if m < half else (other, 8 * (m - half))
+        wide = jnp.concatenate([ref[row : row + z.hg, :]] * (held.shape[0] // z.hg), axis=0)
+        side = lax.axis_index("head") ^ (m % sides)
+        total = total + jnp.where(owner == side * z.group + (me ^ (m // sides)), wide, 0.0)
     held[...] = total
-    last = pltpu.make_async_copy(held, gb, sem.at[len(copies)])
-    last.start()
-    for copy in copies + [last]:
-        copy.wait()
+    copy = pltpu.make_async_copy(held, gb, sem.at[0])
+    copy.start()
+    copy.wait()
 
 
 def bind(kernel, *fixed):
@@ -483,6 +489,10 @@
 
     def shifted(value, by):
         return lax.ppermute(value, "seq", [(i, i + by) for i in range(blocks) if 0 <= i + by < blocks])
+
+    def swapped(parts):
+        got = {k: swap(parts[k], k) for k in (group - 1, *range(1, group - 1))}
+        return [parts[0]] + [got[k] for k in range(1, group)]
 
     def added(*terms):
         (total,) = call(add_kernel, [(terms[0].shape, terms[0].dtype)], terms)
@@ -503,8 +513,8 @@
         limit=VMEM_BYTES - pack_bytes - (520 << 10),
     )
     kv, qd, table = packed[:group], packed[group : 2 * group], packed[2 * group]
-    kv_got = [kv[0]] + [swap(kv[k], k) for k in range(1, group)]
-    qd_got = [qd[0]] + [swap(qd[k], k) for k in range(1, group)]
+    kv_got = swapped(kv)
+    qd_got = swapped(qd)
     (kv_out,) = call(bind(kv_halo_kernel, z), [((z.halo * 2 * tok, z.cw), BF16)], kv_got)
     kv_halo = shifted(kv_out, group)
     (qd_out,) = call(bind(qd_halo_kernel, z), [((z.halo * z.rows, z.cw), BF16)], (*qd_got, *kv_got))
@@ -577,16 +587,32 @@
         flops=2 * (near + far) * z.pairs * unit,
     )
     ret = call(bind(seal_kernel, z, 3), [((3 * tok, z.cw), BF16)] * group, (dq, dk, dv))
-    back = [ret[0]] + [swap(ret[k], k) for k in range(1, group)]
-    (joined,) = call(join_kernel, [((8 * sides, buckets), F32)], sums_of)
-    spread = [joined] + [swap(joined, k) for k in range(1, group)]
-    return call(
-        bind(unpack_kernel, z, sides),
-        [((tok, width), BF16)] * 3 + [((heads * sides, buckets), F32)],
-        (*back, *spread),
+    back = swapped(ret)
+
+    def joined(*parts):
+        rows = sum(p.shape[0] for p in parts)
+        (whole,) = call(join_kernel, [((rows, buckets), F32)], parts)
+        return whole
+
+    mine, by = joined(*sums_of), 1
+    while by * 2 < group:
+        mine, by = joined(mine, swap(mine, by)), by * 2
+    other = swap(mine, by)
+    grads = call(
+        bind(unpack_kernel, z),
+        [((tok, width), BF16)] * 3,
+        back,
         out_space=hbm,
-        scratch=[pltpu.VMEM((heads * sides, buckets), F32), pltpu.SemaphoreType.DMA((3 * group + 1,))],
-    )
+        scratch=[pltpu.SemaphoreType.DMA((3 * group,))],
+    )
+    (grad_bias,) = call(
+        bind(spread_kernel, z, sides),
+        [((heads * sides, buckets), F32)],
+        (mine, other),
+        out_space=hbm,
+        scratch=[pltpu.VMEM((heads * sides, buckets), F32), pltpu.SemaphoreType.DMA((1,))],
+    )
+    return (*grads, grad_bias)
 
 
 def solution(mesh):

time: 58 us -> 57.8 us (level)
  starting transfers between devices: 28.6 us -> 27.1 us
  waiting for transfers between devices: 15.8 us -> 16.6 us
  Pallas kernels: 12.6 us -> 13.2 us
    ppermute x15 -> x14, starting transfers between devices: 19.5 us -> 17.9 us  [swap(): lax.ppermute(value, axis, [(i, i ^ by) for i in range(lax.axis_size(axis))])]
    ppermute x15 -> x14, waiting for transfers between devices: 14.9 us -> 15.7 us  [swap(): lax.ppermute(value, axis, [(i, i ^ by) for i in range(lax.axis_size(axis))])]
    pallas_call x15 -> x17, Pallas kernels: 12.6 us -> 13.2 us  [call(): pl.pallas_call(kernel, out_shape=tuple((out_space(s, d) for s, d in outs)...]
  transfers between devices with their start and end apart: 18 -> 17, of which waited for: 8 -> 8; matrix products, arithmetic and copies ran while one was open for 0% -> 0% of each run, Pallas kernels for 13% -> 14%
where the time goes in v5:
time: 57.8 us; the launch traced here: 57.6 us
  starting transfers between devices  27.1 us (47%)
  waiting for transfers between devices  16.6 us (29%)
  Pallas kernels  13.2 us (23%)
  between operations  0.79 us (1%)
    ppermute x14, starting transfers between devices, swap(): lax.ppermute(value, axis, [(i, i ^ by) for i in range(lax.axis_size(axis))])  17.9 us
    ppermute x14, waiting for transfers between devices, swap(): lax.ppermute(value, axis, [(i, i ^ by) for i in range(lax.axis_size(axis))])  15.7 us
    pallas_call x17, Pallas kernels, call(): pl.pallas_call(kernel, out_shape=tuple((out_space(s, d) for s, d in outs)...  13.2 us
    ppermute x2, starting transfers between devices, shifted(): lax.ppermute(value, 'seq', [(i, i + by) for i in range(blocks) if 0 <= i...  4.64 us
    ppermute x1, starting transfers between devices, body(): lax.ppermute(stats, 'seq', [(i, (i - group) % blocks) for i in range(bloc...  4.51 us
  transfers between devices with their start and end apart: 17, of which 8 were waited for; matrix products, arithmetic and copies ran while one was open for 0% of the time, Pallas kernels for 14%

profile of v5, /device:TPU:0, one launch (start us, length us, event | category | flops | bytes accessed | tf_op | source)
XLA Modules:
  0.0 57.6 jit_solution(12084448927492475340)
XLA Ops:
  0.6 1.5 %shard_map.102 = (bf16[272,256]{1,0:T(8,128)(2,1)S(1)}, bf16[272,256]{1,0:T(8,128)(2,1)S(1)}, bf16[272,256]{1,0:T(8,128)(2,1)S(1)}, bf16[272,256]{1,0:T(8,128)(2...) custom-call(bf16[128,1024]{1,0:T(8,128)(2,1)} %refs_0_.1, ...), custom_call_target="tpu_custom_call" | custom-call | bytes 1060880 | tf_op jit(solution)/shard_map/pallas_call | solution.py:34
  2.1 3.0 %collective-permute-start = (bf16[272,256]{1,0:T(8,128)(2,1)S(1)}, bf16[272,256]{1,0:T(8,128)(2,1)S(1)}, u32[]{:S(2)}, u32[]{:S(2)}) collective-permute-start(bf16[272,256]{1,0:T(8,128)(2,1)S(1)} %get-tuple-element.47), channel_id=1, source_target_pairs={{0,2},{2,0},{4,6},{6,4},{8,10},{10,8},{12,14},{14,12},{16,18},{18,... | collective-permute-start | bytes 417800 | tf_op jit(solution)/shard_map/ppermute | solution.py:488
  5.1 1.5 %collective-permute-start.1 = (bf16[272,256]{1,0:T(8,128)(2,1)S(1)}, bf16[272,256]{1,0:T(8,128)(2,1)S(1)}, u32[]{:S(2)}, u32[]{:S(2)}) collective-permute-start(bf16[272,256]{1,0:T(8,128)(2,1)S(1)} %get-tuple-element.48), channel_id=1, source_target_pairs={{0,4},{2,6},{4,0},{6,2},{8,12},{10,14},{12,8},{14,10},{16,20},{18,... | collective-permute-start | bytes 417800 | tf_op jit(solution)/shard_map/ppermute | solution.py:488
  6.6 0.0 collective-permute-start.2
  6.7 1.9 %collective-permute-start.4 = (bf16[256,256]{1,0:T(8,128)(2,1)S(1)}, bf16[256,256]{1,0:T(8,128)(2,1)S(1)}, u32[]{:S(2)}, u32[]{:S(2)}) collective-permute-start(bf16[256,256]{1,0:T(8,128)(2,1)S(1)} %get-tuple-element.54), channel_id=1, source_target_pairs={{0,2},{2,0},{4,6},{6,4},{8,10},{10,8},{12,14},{14,12},{16,18},{18,... | collective-permute-start | bytes 393224 | tf_op jit(solution)/shard_map/ppermute | solution.py:488
  8.6 1.5 %collective-permute-start.5 = (bf16[256,256]{1,0:T(8,128)(2,1)S(1)}, bf16[256,256]{1,0:T(8,128)(2,1)S(1)}, u32[]{:S(2)}, u32[]{:S(2)}) collective-permute-start(bf16[256,256]{1,0:T(8,128)(2,1)S(1)} %get-tuple-element.55), channel_id=1, source_target_pairs={{0,4},{2,6},{4,0},{6,2},{8,12},{10,14},{12,8},{14,10},{16,20},{18,... | collective-permute-start | bytes 393224 | tf_op jit(solution)/shard_map/ppermute | solution.py:488
  10.1 0.0 collective-permute-done.refs_1_.refs_5_
  10.1 2.5 %collective-permute-start.6 = (bf16[256,256]{1,0:T(8,128)(2,1)S(1)}, bf16[256,256]{1,0:T(8,128)(2,1)S(1)}, u32[]{:S(2)}, u32[]{:S(2)}) collective-permute-start(bf16[256,256]{1,0:T(8,128)(2,1)S(1)} %get-tuple-element.56), channel_id=1, source_target_pairs={{0,6},{2,4},{4,2},{6,0},{8,14},{10,12},{12,10},{14,8},{16,22},{18,... | collective-permute-start | bytes 393224 | tf_op jit(solution)/shard_map/ppermute | solution.py:488
  12.6 1.7 %collective-permute-done.1.refs_2_.refs_6_ = bf16[272,256]{1,0:T(8,128)(2,1)S(1)} collective-permute-done((bf16[272,256]{1,0:T(8,128)(2,1)S(1)}, bf16[272,256]{1,0:T(8,128)(2,1)S(1)}, u32[]{:S(2)}, u32[]{:S(2)}) %collective-permute-start.1) | collective-permute-done | bytes 139296 | tf_op jit(solution)/shard_map/ppermute | solution.py:488
  14.3 0.0 collective-permute-done.2.refs_3_.refs_7_
  14.3 3.3 %collective-permute-start.3 = (bf16[768,256]{1,0:T(8,128)(2,1)S(1)}, bf16[768,256]{1,0:T(8,128)(2,1)S(1)}, u32[]{:S(2)}, u32[]{:S(2)}) collective-permute-start(bf16[768,256]{1,0:T(8,128)(2,1)S(1)} %shard_map.104), channel_id=1, source_target_pairs={{0,8},{2,10},{4,12},{6,14},{8,16},{10,18},{12,20},{14,22},{16,24},... | collective-permute-start | bytes 1179656 | tf_op jit(solution)/shard_map/ppermute | solution.py:491
  17.7 0.0 collective-permute-done.4.refs_1_
  17.7 1.2 %collective-permute-done.5.refs_2_ = bf16[256,256]{1,0:T(8,128)(2,1)S(1)} collective-permute-done((bf16[256,256]{1,0:T(8,128)(2,1)S(1)}, bf16[256,256]{1,0:T(8,128)(2,1)S(1)}, u32[]{:S(2)}, u32[]{:S(2)}) %collective-permute-start.5) | collective-permute-done | bytes 131104 | tf_op jit(solution)/shard_map/ppermute | solution.py:488
  18.9 0.0 collective-permute-done.6.refs_3_
  18.9 1.3 %collective-permute-start.7 = (bf16[816,256]{1,0:T(8,128)(2,1)S(1)}, bf16[816,256]{1,0:T(8,128)(2,1)S(1)}, u32[]{:S(2)}, u32[]{:S(2)}) collective-permute-start(bf16[816,256]{1,0:T(8,128)(2,1)S(1)} %shard_map.109), channel_id=1, source_target_pairs={{8,0},{10,2},{12,4},{14,6},{16,8},{18,10},{20,12},{22,14},{24,16},... | collective-permute-start | bytes 1253384 | tf_op jit(solution)/shard_map/ppermute | solution.py:491
  20.2 1.4 %shard_map.103 = (bf16[512,256]{1,0:T(8,128)(2,1)S(1)}, bf16[512,256]{1,0:T(8,128)(2,1)S(1)}, f32[20,128,256]{2,1,0:T(8,128)S(1)}, f32[12,128,256]{2,1,0:T(8,128)S(1)}, f32[64,256]{1,0:T(8,128)S(1)}) custom-call(bf16[272,256]{1,0:T(8,128)(2,1)S(1)} %get-tuple-element.46.refs_0_.refs_4_, bf16[272,256]{1,0:T(8,128)(2,1)S(1)} %collective-permute-done.refs_1_.refs_5_, ...), custom_call_target="tpu_custom_call" | custom-call | bytes 565248 | tf_op jit(solution)/shard_map/pallas_call | solution.py:34
  21.6 1.6 %shard_map.105 = (bf16[2,1024,128]{2,1,0:T(8,128)(2,1)S(1)}, bf16[2,1024,128]{2,1,0:T(8,128)(2,1)S(1)}, f32[20,128,256]{2,1,0:T(8,128)S(1)}, f32[20,128,256]{2,1...) custom-call(bf16[256,256]{1,0:T(8,128)(2,1)S(1)} %get-tuple-element.53.refs_0_, ...), custom_call_target="tpu_custom_call" | custom-call | flops 335544320 | bytes 3670016 | tf_op jit(solution)/shard_map/pallas_call | solution.py:34
  23.2 0.9 %collective-permute-done.3.refs_0_.refs_1_ = bf16[768,256]{1,0:T(8,128)(2,1)S(1)} collective-permute-done((bf16[768,256]{1,0:T(8,128)(2,1)S(1)}, bf16[768,256]{1,0:T(8,128)(2,1)S(1)}, u32[]{:S(2)}, u32[]{:S(2)}) %collective-permute-start.3) | collective-permute-done | bytes 393248 | tf_op jit(solution)/shard_map/ppermute | solution.py:491
  24.1 1.6 %shard_map.106 = (f32[2,8,256]{2,1,0:T(8,128)S(1)}, f32[20,256]{1,0:T(8,128)S(1)}, f32[12,256]{1,0:T(8,128)S(1)}, f32[12,128,256]{2,1,0:T(8,128)S(1)}, f32[12,12...) custom-call(bf16[768,256]{1,0:T(8,128)(2,1)S(1)} %collective-permute-done.3.refs_0_.refs_1_, ...), custom_call_target="tpu_custom_call" | custom-call | flops 201326592 | bytes 3076096 | tf_op jit(solution)/shard_map/pallas_call | solution.py:34
  25.7 4.5 %collective-permute-start.8 = (f32[2,8,256]{2,1,0:T(8,128)S(1)}, f32[2,8,256]{2,1,0:T(8,128)S(1)}, u32[]{:S(2)}, u32[]{:S(2)}) collective-permute-start(f32[2,8,256]{2,1,0:T(8,128)S(1)} %get-tuple-element.65.refs_1_), channel_id=1, source_target_pairs={{0,24},{2,26},{4,28},{6,30},{8,0},{10,2},{12,4},{14,6},{16,8},{18,... | collective-permute-start | bytes 49160 | tf_op jit(solution)/shard_map/ppermute | solution.py:551
  30.2 2.2 %shard_map.107 = (bf16[2,512,1024]{2,1,0:T(8,128)(2,1)S(1)}, bf16[2,896,1024]{2,1,0:T(8,128)(2,1)S(1)}, f32[8,128]{1,0:T(8,128)S(1)}) custom-call(f32[64,256]{1,0:T(8,128)S(1)} %get-tuple-element.52.refs_0_, f32[2,8,256]{2,1,0:T(8,128)S(1)} %get-tuple-element.65.refs_1_, f32[20,256]{1,0:T(8,128)S(1)} %get-tuple-element.66.refs_2_, ...), custom_call_target="tpu_custom_call" | custom-call | bytes 8503296 | tf_op jit(solution)/shard_map/pallas_call | solution.py:34
  32.3 0.8 %shard_map.108.refs_0_ = bf16[512,256]{1,0:T(8,128)(2,1)S(1)} custom-call(bf16[512,256]{1,0:T(8,128)(2,1)S(1)} %get-tuple-element.51.refs_4_.refs_0_, bf16[768,256]{1,0:T(8,128)(2,1)S(1)} %collective-permute-done.3.refs_0_.refs_1_, bf16[2,896,1024]{2,1,0:T(8,128)(2,1)S(1)} %get-tuple-element.72.refs_2_.refs_3_), custom_call_target="tpu_custom_call" | custom-call | flops 268435456 | bytes 4325376 | tf_op jit(solution)/shard_map/pallas_call | solution.py:34
  33.2 0.0 collective-permute-done.8.refs_3_
  33.2 0.0 collective-permute-done.7.refs_2_
  33.2 1.0 %shard_map.110 = (bf16[2,768,128]{2,1,0:T(8,128)(2,1)S(1)}, bf16[2,768,128]{2,1,0:T(8,128)(2,1)S(1)}, bf16[2,512,768]{2,1,0:T(8,128)(2,1)S(1)}, bf16[2,512,768]{2,1,0:T(8,128)(2,1)S(1)}) custom-call(bf16[512,256]{1,0:T(8,128)(2,1)S(1)} %get-tuple-element.51.refs_4_.refs_0_, bf16[512,256]{1,0:T(8,128)(2,1)S(1)} %get-tuple-element.57.refs_5_.refs_1_, ...), custom_call_target="tpu_custom_call" | custom-call | flops 201326592 | bytes 966656 | tf_op jit(solution)/shard_map/pallas_call | solution.py:34
  34.2 1.5 %shard_map.111 = (bf16[512,256]{1,0:T(8,128)(2,1)S(1)}, bf16[512,256]{1,0:T(8,128)(2,1)S(1)}) custom-call(bf16[2,1024,128]{2,1,0:T(8,128)(2,1)S(1)} %get-tuple-element.59.refs_1_.refs_0_, bf16[2,1024,128]{2,1,0:T(8,128)(2,1)S(1)} %get-tuple-element.60.refs_2_.refs_1_, bf16[2,512,1024]{2,1,0:T(8,128)(2,1)S(1)} %get-tuple-element.73.refs_2_, ...), custom_call_target="tpu_custom_call" | custom-call | flops 536870912 | bytes 10747904 | tf_op jit(solution)/shard_map/pallas_call | solution.py:34
  35.6 0.1 shard_map.112
  35.7 1.5 %collective-permute-start.9 = (bf16[384,256]{1,0:T(8,128)(2,1)S(1)}, bf16[384,256]{1,0:T(8,128)(2,1)S(1)}, u32[]{:S(2)}, u32[]{:S(2)}) collective-permute-start(bf16[384,256]{1,0:T(8,128)(2,1)S(1)} %get-tuple-element.81), channel_id=1, source_target_pairs={{0,2},{2,0},{4,6},{6,4},{8,10},{10,8},{12,14},{14,12},{16,18},{18,... | collective-permute-start | bytes 589832 | tf_op jit(solution)/shard_map/ppermute | solution.py:488
  37.2 0.5 collective-permute-start.10
  37.7 1.6 %collective-permute-start.11 = (bf16[384,256]{1,0:T(8,128)(2,1)S(1)}, bf16[384,256]{1,0:T(8,128)(2,1)S(1)}, u32[]{:S(2)}, u32[]{:S(2)}) collective-permute-start(bf16[384,256]{1,0:T(8,128)(2,1)S(1)} %get-tuple-element.83), channel_id=1, source_target_pairs={{0,6},{2,4},{4,2},{6,0},{8,14},{10,12},{12,10},{14,8},{16,22},{18,... | collective-permute-start | bytes 589832 | tf_op jit(solution)/shard_map/ppermute | solution.py:488
  39.3 0.0 collective-permute-start.12
  39.3 3.6 %collective-permute-done.12.refs_1_ = f32[8,128]{1,0:T(8,128)S(1)} collective-permute-done((f32[8,128]{1,0:T(8,128)S(1)}, f32[8,128]{1,0:T(8,128)S(1)}, u32[]{:S(2)}, u32[]{:S(2)}) %collective-permute-start.12) | collective-permute-done | bytes 4128 | tf_op jit(solution)/shard_map/ppermute | solution.py:488
  42.9 1.1 %collective-permute-start.13 = (f32[8,128]{1,0:T(8,128)S(1)}, f32[8,128]{1,0:T(8,128)S(1)}, u32[]{:S(2)}, u32[]{:S(2)}) collective-permute-start(f32[8,128]{1,0:T(8,128)S(1)} %shard_map.114.refs_0_), channel_id=1, source_target_pairs={{0,16},{2,18},{4,20},{6,22},{8,24},{10,26},{12,28},{14,30},{16,0},... | collective-permute-start | bytes 12296 | tf_op jit(solution)/shard_map/ppermute | solution.py:488
  43.9 3.5 %collective-permute-done.13.refs_1_ = f32[8,128]{1,0:T(8,128)S(1)} collective-permute-done((f32[8,128]{1,0:T(8,128)S(1)}, f32[8,128]{1,0:T(8,128)S(1)}, u32[]{:S(2)}, u32[]{:S(2)}) %collective-permute-start.13) | collective-permute-done | bytes 4128 | tf_op jit(solution)/shard_map/ppermute | solution.py:488
  47.4 0.0 collective-permute-start.14
  47.4 1.2 %collective-permute-done.14.refs_1_ = f32[8,128]{1,0:T(8,128)S(1)} collective-permute-done((f32[8,128]{1,0:T(8,128)S(1)}, f32[8,128]{1,0:T(8,128)S(1)}, u32[]{:S(2)}, u32[]{:S(2)}) %collective-permute-start.14) | collective-permute-done | bytes 4128 | tf_op jit(solution)/shard_map/ppermute | solution.py:488
  48.6 1.4 %collective-permute-start.15 = (f32[16,128]{1,0:T(8,128)S(1)}, f32[16,128]{1,0:T(8,128)S(1)}, u32[]{:S(2)}, u32[]{:S(2)}) collective-permute-start(f32[16,128]{1,0:T(8,128)S(1)} %shard_map.116.refs_0_), channel_id=1, source_target_pairs={{0,2},{2,0},{4,6},{6,4},{8,10},{10,8},{12,14},{14,12},{16,18},{18,... | collective-permute-start | bytes 24584 | tf_op jit(solution)/shard_map/ppermute | solution.py:488
  50.0 2.2 %collective-permute-done.15.refs_1_ = f32[16,128]{1,0:T(8,128)S(1)} collective-permute-done((f32[16,128]{1,0:T(8,128)S(1)}, f32[16,128]{1,0:T(8,128)S(1)}, u32[]{:S(2)}, u32[]{:S(2)}) %collective-permute-start.15) | collective-permute-done | bytes 8224 | tf_op jit(solution)/shard_map/ppermute | solution.py:488
  52.2 1.3 %collective-permute-start.16 = (f32[32,128]{1,0:T(8,128)S(1)}, f32[32,128]{1,0:T(8,128)S(1)}, u32[]{:S(2)}, u32[]{:S(2)}) collective-permute-start(f32[32,128]{1,0:T(8,128)S(1)} %shard_map.117.refs_0_), channel_id=1, source_target_pairs={{0,4},{2,6},{4,0},{6,2},{8,12},{10,14},{12,8},{14,10},{16,20},{18,... | collective-permute-start | bytes 49160 | tf_op jit(solution)/shard_map/ppermute | solution.py:488
  53.6 2.4 %collective-permute-done.16.refs_1_ = f32[32,128]{1,0:T(8,128)S(1)} collective-permute-done((f32[32,128]{1,0:T(8,128)S(1)}, f32[32,128]{1,0:T(8,128)S(1)}, u32[]{:S(2)}, u32[]{:S(2)}) %collective-permute-start.16) | collective-permute-done | bytes 16416 | tf_op jit(solution)/shard_map/ppermute | solution.py:488
  56.0 0.6 %shard_map.118 = f32[32,128]{1,0:T(8,128)} custom-call(f32[32,128]{1,0:T(8,128)S(1)} %shard_map.117.refs_0_, f32[32,128]{1,0:T(8,128)S(1)} %collective-permute-done.16.refs_1_), custom_call_target="tpu_custom_call" | custom-call | bytes 32768 | tf_op jit(solution)/shard_map/pallas_call | solution.py:34
  56.6 0.0 collective-permute-done.9.refs_1_
  56.6 0.0 collective-permute-done.10.refs_2_
  56.6 0.0 collective-permute-done.11.refs_3_
  56.6 1.0 %shard_map.113 = (bf16[128,1024]{1,0:T(8,128)(2,1)}, bf16[128,1024]{1,0:T(8,128)(2,1)}, bf16[128,1024]{1,0:T(8,128)(2,1)}) custom-call(bf16[384,256]{1,0:T(8,128)(2,1)S(1)} %get-tuple-element.80.refs_0_, bf16[384,256]{1,0:T(8,128)(2,1)S(1)} %collective-permute-done.9.refs_1_, bf16[384,256]{1,0:T(8,128)(2,1)S(1)} %collective-permute-done.10.refs_2_, ...), custom_call_target="tpu_custom_call" | custom-call | bytes 786432 | tf_op jit(solution)/shard_map/pallas_call | solution.py:34
  (6 shorter events, 0.1 us)
Async XLA Ops:
  2.1 8.0 %collective-permute-start = (bf16[272,256]{1,0:T(8,128)(2,1)S(1)}, bf16[272,256]{1,0:T(8,128)(2,1)S(1)}, u32[]{:S(2)}, u32[]{:S(2)}) collective-permute-start(bf16[272,256]{1,0:T(8,128)(2,1)S(1)} %get-tuple-element.47), channel_id=1, source_target_pairs={{0,2},{2,0},{4,6},{6,4},{8,10},{10,8},{12,14},{14,12},{16,18},{18,... | collective-permute-start | bytes 417800 | tf_op jit(solution)/shard_map/ppermute | solution.py:488
  5.1 9.2 %collective-permute-start.1 = (bf16[272,256]{1,0:T(8,128)(2,1)S(1)}, bf16[272,256]{1,0:T(8,128)(2,1)S(1)}, u32[]{:S(2)}, u32[]{:S(2)}) collective-permute-start(bf16[272,256]{1,0:T(8,128)(2,1)S(1)} %get-tuple-element.48), channel_id=1, source_target_pairs={{0,4},{2,6},{4,0},{6,2},{8,12},{10,14},{12,8},{14,10},{16,20},{18,... | collective-permute-start | bytes 417800 | tf_op jit(solution)/shard_map/ppermute | solution.py:488
  6.6 7.6 %collective-permute-start.2 = (bf16[272,256]{1,0:T(8,128)(2,1)S(1)}, bf16[272,256]{1,0:T(8,128)(2,1)S(1)}, u32[]{:S(2)}, u32[]{:S(2)}) collective-permute-start(bf16[272,256]{1,0:T(8,128)(2,1)S(1)} %get-tuple-element.49), channel_id=1, source_target_pairs={{0,6},{2,4},{4,2},{6,0},{8,14},{10,12},{12,10},{14,8},{16,22},{18,... | collective-permute-start | bytes 417800 | tf_op jit(solution)/shard_map/ppermute | solution.py:488
  6.7 11.0 %collective-permute-start.4 = (bf16[256,256]{1,0:T(8,128)(2,1)S(1)}, bf16[256,256]{1,0:T(8,128)(2,1)S(1)}, u32[]{:S(2)}, u32[]{:S(2)}) collective-permute-start(bf16[256,256]{1,0:T(8,128)(2,1)S(1)} %get-tuple-element.54), channel_id=1, source_target_pairs={{0,2},{2,0},{4,6},{6,4},{8,10},{10,8},{12,14},{14,12},{16,18},{18,... | collective-permute-start | bytes 393224 | tf_op jit(solution)/shard_map/ppermute | solution.py:488
  8.6 10.2 %collective-permute-start.5 = (bf16[256,256]{1,0:T(8,128)(2,1)S(1)}, bf16[256,256]{1,0:T(8,128)(2,1)S(1)}, u32[]{:S(2)}, u32[]{:S(2)}) collective-permute-start(bf16[256,256]{1,0:T(8,128)(2,1)S(1)} %get-tuple-element.55), channel_id=1, source_target_pairs={{0,4},{2,6},{4,0},{6,2},{8,12},{10,14},{12,8},{14,10},{16,20},{18,... | collective-permute-start | bytes 393224 | tf_op jit(solution)/shard_map/ppermute | solution.py:488
  10.1 8.7 %collective-permute-start.6 = (bf16[256,256]{1,0:T(8,128)(2,1)S(1)}, bf16[256,256]{1,0:T(8,128)(2,1)S(1)}, u32[]{:S(2)}, u32[]{:S(2)}) collective-permute-start(bf16[256,256]{1,0:T(8,128)(2,1)S(1)} %get-tuple-element.56), channel_id=1, source_target_pairs={{0,6},{2,4},{4,2},{6,0},{8,14},{10,12},{12,10},{14,8},{16,22},{18,... | collective-permute-start | bytes 393224 | tf_op jit(solution)/shard_map/ppermute | solution.py:488
  14.3 9.8 %collective-permute-start.3 = (bf16[768,256]{1,0:T(8,128)(2,1)S(1)}, bf16[768,256]{1,0:T(8,128)(2,1)S(1)}, u32[]{:S(2)}, u32[]{:S(2)}) collective-permute-start(bf16[768,256]{1,0:T(8,128)(2,1)S(1)} %shard_map.104), channel_id=1, source_target_pairs={{0,8},{2,10},{4,12},{6,14},{8,16},{10,18},{12,20},{14,22},{16,24},... | collective-permute-start | bytes 1179656 | tf_op jit(solution)/shard_map/ppermute | solution.py:491
  18.9 14.3 %collective-permute-start.7 = (bf16[816,256]{1,0:T(8,128)(2,1)S(1)}, bf16[816,256]{1,0:T(8,128)(2,1)S(1)}, u32[]{:S(2)}, u32[]{:S(2)}) collective-permute-start(bf16[816,256]{1,0:T(8,128)(2,1)S(1)} %shard_map.109), channel_id=1, source_target_pairs={{8,0},{10,2},{12,4},{14,6},{16,8},{18,10},{20,12},{22,14},{24,16},... | collective-permute-start | bytes 1253384 | tf_op jit(solution)/shard_map/ppermute | solution.py:491
  25.7 7.5 %collective-permute-start.8 = (f32[2,8,256]{2,1,0:T(8,128)S(1)}, f32[2,8,256]{2,1,0:T(8,128)S(1)}, u32[]{:S(2)}, u32[]{:S(2)}) collective-permute-start(f32[2,8,256]{2,1,0:T(8,128)S(1)} %get-tuple-element.65.refs_1_), channel_id=1, source_target_pairs={{0,24},{2,26},{4,28},{6,30},{8,0},{10,2},{12,4},{14,6},{16,8},{18,... | collective-permute-start | bytes 49160 | tf_op jit(solution)/shard_map/ppermute | solution.py:551
  35.7 20.9 %collective-permute-start.9 = (bf16[384,256]{1,0:T(8,128)(2,1)S(1)}, bf16[384,256]{1,0:T(8,128)(2,1)S(1)}, u32[]{:S(2)}, u32[]{:S(2)}) collective-permute-start(bf16[384,256]{1,0:T(8,128)(2,1)S(1)} %get-tuple-element.81), channel_id=1, source_target_pairs={{0,2},{2,0},{4,6},{6,4},{8,10},{10,8},{12,14},{14,12},{16,18},{18,... | collective-permute-start | bytes 589832 | tf_op jit(solution)/shard_map/ppermute | solution.py:488
  37.2 19.4 %collective-permute-start.10 = (bf16[384,256]{1,0:T(8,128)(2,1)S(1)}, bf16[384,256]{1,0:T(8,128)(2,1)S(1)}, u32[]{:S(2)}, u32[]{:S(2)}) collective-permute-start(bf16[384,256]{1,0:T(8,128)(2,1)S(1)} %get-tuple-element.82), channel_id=1, source_target_pairs={{0,4},{2,6},{4,0},{6,2},{8,12},{10,14},{12,8},{14,10},{16,20},{18,... | collective-permute-start | bytes 589832 | tf_op jit(solution)/shard_map/ppermute | solution.py:488
  37.7 18.9 %collective-permute-start.11 = (bf16[384,256]{1,0:T(8,128)(2,1)S(1)}, bf16[384,256]{1,0:T(8,128)(2,1)S(1)}, u32[]{:S(2)}, u32[]{:S(2)}) collective-permute-start(bf16[384,256]{1,0:T(8,128)(2,1)S(1)} %get-tuple-element.83), channel_id=1, source_target_pairs={{0,6},{2,4},{4,2},{6,0},{8,14},{10,12},{12,10},{14,8},{16,22},{18,... | collective-permute-start | bytes 589832 | tf_op jit(solution)/shard_map/ppermute | solution.py:488
  39.3 3.6 %collective-permute-start.12 = (f32[8,128]{1,0:T(8,128)S(1)}, f32[8,128]{1,0:T(8,128)S(1)}, u32[]{:S(2)}, u32[]{:S(2)}) collective-permute-start(f32[8,128]{1,0:T(8,128)S(1)} %get-tuple-element.87.refs_0_), channel_id=1, source_target_pairs={{0,8},{2,10},{4,12},{6,14},{8,0},{10,2},{12,4},{14,6},{16,24},{18,... | collective-permute-start | bytes 12296 | tf_op jit(solution)/shard_map/ppermute | solution.py:488
  42.9 4.5 %collective-permute-start.13 = (f32[8,128]{1,0:T(8,128)S(1)}, f32[8,128]{1,0:T(8,128)S(1)}, u32[]{:S(2)}, u32[]{:S(2)}) collective-permute-start(f32[8,128]{1,0:T(8,128)S(1)} %shard_map.114.refs_0_), channel_id=1, source_target_pairs={{0,16},{2,18},{4,20},{6,22},{8,24},{10,26},{12,28},{14,30},{16,0},... | collective-permute-start | bytes 12296 | tf_op jit(solution)/shard_map/ppermute | solution.py:488
  47.4 1.2 %collective-permute-start.14 = (f32[8,128]{1,0:T(8,128)S(1)}, f32[8,128]{1,0:T(8,128)S(1)}, u32[]{:S(2)}, u32[]{:S(2)}) collective-permute-start(f32[8,128]{1,0:T(8,128)S(1)} %shard_map.115.refs_0_), channel_id=1, source_target_pairs={{0,1},{1,0},{2,3},{3,2},{4,5},{5,4},{6,7},{7,6},{8,9},{9,8},{10,11... | collective-permute-start | bytes 12296 | tf_op jit(solution)/shard_map/ppermute | solution.py:488
  48.6 3.7 %collective-permute-start.15 = (f32[16,128]{1,0:T(8,128)S(1)}, f32[16,128]{1,0:T(8,128)S(1)}, u32[]{:S(2)}, u32[]{:S(2)}) collective-permute-start(f32[16,128]{1,0:T(8,128)S(1)} %shard_map.116.refs_0_), channel_id=1, source_target_pairs={{0,2},{2,0},{4,6},{6,4},{8,10},{10,8},{12,14},{14,12},{16,18},{18,... | collective-permute-start | bytes 24584 | tf_op jit(solution)/shard_map/ppermute | solution.py:488
  52.2 3.7 %collective-permute-start.16 = (f32[32,128]{1,0:T(8,128)S(1)}, f32[32,128]{1,0:T(8,128)S(1)}, u32[]{:S(2)}, u32[]{:S(2)}) collective-permute-start(f32[32,128]{1,0:T(8,128)S(1)} %shard_map.117.refs_0_), channel_id=1, source_target_pairs={{0,4},{2,6},{4,0},{6,2},{8,12},{10,14},{12,8},{14,10},{16,20},{18,... | collective-permute-start | bytes 49160 | tf_op jit(solution)/shard_map/ppermute | solution.py:488

commit v6 on v5

--- a/solution.py
+++ b/solution.py
@@ -65,22 +65,26 @@
         return lax.rem(lax.axis_index("seq"), self.group)
 
 
-def pack_kernel(z, q, k, v, d, bias, ids, mask, *refs):
-    kv, qd = refs[: z.group], refs[z.group : 2 * z.group]
-    table, slots, flags, sem = refs[2 * z.group :]
+def chunk_copies(z, sources, dst, sem, first):
+    copies = []
+    for g in range(z.group):
+        cols = at((z.me() ^ g) * z.cw, z.cw)
+        for n, src in enumerate(sources):
+            rows = pl.ds(n * z.tok, z.tok)
+            copies.append(pltpu.make_async_copy(src.at[:, cols], dst[g].at[rows, :], sem.at[first + len(copies)]))
+    return copies
+
+
+def pack_kv_kernel(z, k, v, bias, ids, mask, *refs):
+    kv = refs[: z.group]
+    table, slots, flags, sem = refs[z.group :]
     index = lax.axis_index("seq")
-    me = z.me()
     copies = [
         pltpu.make_async_copy(ids.at[0], slots, sem.at[0]),
         pltpu.make_async_copy(mask, flags, sem.at[1]),
         pltpu.make_async_copy(bias, table, sem.at[2]),
     ]
-    for sources, dst in (((k, v), kv), ((q, d), qd)):
-        for g in range(z.group):
-            cols = at((me ^ g) * z.cw, z.cw)
-            for n, src in enumerate(sources):
-                rows = pl.ds(n * z.tok, z.tok)
-                copies.append(pltpu.make_async_copy(src.at[:, cols], dst[g].at[rows, :], sem.at[len(copies)]))
+    copies += chunk_copies(z, (k, v), kv, sem, len(copies))
     for copy in copies:
         copy.start()
     for copy in copies[:2]:
@@ -94,6 +98,14 @@
     for g in range(z.group):
         kv[g][2 * z.tok :, :] = codes
     for copy in copies[2:]:
+        copy.wait()
+
+
+def pack_qd_kernel(z, q, d, *refs):
+    copies = chunk_copies(z, (q, d), refs[: z.group], refs[z.group], 0)
+    for copy in copies:
+        copy.start()
+    for copy in copies:
         copy.wait()
 
 
@@ -424,9 +436,8 @@
 
 
 def join_kernel(*refs):
-    rows = refs[0].shape[0]
     for n, ref in enumerate(refs[:-1]):
-        refs[-1][rows * n : rows * (n + 1), :] = ref[...]
+        refs[-1][8 * n : 8 * n + 8, :] = ref[...]
 
 
 def add_kernel(*refs):
@@ -451,16 +462,16 @@
         copy.wait()
 
 
-def spread_kernel(z, sides, mine, other, gb, held, sem):
+def spread_kernel(z, sides, *refs):
+    sums, (gb, held, sem) = refs[: z.group], refs[z.group :]
     me = z.me()
     owner = lax.broadcasted_iota(jnp.int32, held.shape, 0) // z.hg
     total = jnp.zeros(held.shape, F32)
-    half = z.group * sides // 2
-    for m in range(z.group * sides):
-        ref, row = (mine, 8 * m) if m < half else (other, 8 * (m - half))
-        wide = jnp.concatenate([ref[row : row + z.hg, :]] * (held.shape[0] // z.hg), axis=0)
-        side = lax.axis_index("head") ^ (m % sides)
-        total = total + jnp.where(owner == side * z.group + (me ^ (m // sides)), wide, 0.0)
+    for k in range(z.group):
+        for n in range(sides):
+            wide = jnp.concatenate([sums[k][8 * n : 8 * n + z.hg, :]] * (held.shape[0] // z.hg), axis=0)
+            side = lax.axis_index("head") ^ n
+            total = total + jnp.where(owner == side * z.group + (me ^ k), wide, 0.0)
     held[...] = total
     copy = pltpu.make_async_copy(held, gb, sem.at[0])
     copy.start()
@@ -491,8 +502,7 @@
         return lax.ppermute(value, "seq", [(i, i + by) for i in range(blocks) if 0 <= i + by < blocks])
 
     def swapped(parts):
-        got = {k: swap(parts[k], k) for k in (group - 1, *range(1, group - 1))}
-        return [parts[0]] + [got[k] for k in range(1, group)]
+        return [parts[0]] + [swap(parts[k], k) for k in range(1, group)]
 
     def added(*terms):
         (total,) = call(add_kernel, [(terms[0].shape, terms[0].dtype)], terms)
@@ -500,19 +510,27 @@
 
     hbm = pltpu.HBM
     pack_bytes = group * (z.rows + 2 * tok) * z.cw * 2
-    packed = call(
-        bind(pack_kernel, z),
-        [((z.rows, z.cw), BF16)] * group + [((2 * tok, z.cw), BF16)] * group + [((heads, buckets), F32)],
-        (queries, keys, values, grad_out, bias_table, bucket_ids, block_mask),
-        spaces=[hbm] * 7,
+    room = VMEM_BYTES - pack_bytes - (520 << 10)
+    *kv, table = call(
+        bind(pack_kv_kernel, z),
+        [((z.rows, z.cw), BF16)] * group + [((heads, buckets), F32)],
+        (keys, values, bias_table, bucket_ids, block_mask),
+        spaces=[hbm] * 5,
         scratch=[
             pltpu.VMEM((span, z.wide), jnp.int32),
             pltpu.SMEM((1, span), jnp.int32),
-            pltpu.SemaphoreType.DMA((4 * group + 3,)),
+            pltpu.SemaphoreType.DMA((2 * group + 3,)),
         ],
-        limit=VMEM_BYTES - pack_bytes - (520 << 10),
-    )
-    kv, qd, table = packed[:group], packed[group : 2 * group], packed[2 * group]
+        limit=room,
+    )
+    qd = call(
+        bind(pack_qd_kernel, z),
+        [((2 * tok, z.cw), BF16)] * group,
+        (queries, grad_out),
+        spaces=[hbm] * 2,
+        scratch=[pltpu.SemaphoreType.DMA((2 * group,))],
+        limit=room - (group - 1) * z.rows * z.cw * 2,
+    )
     kv_got = swapped(kv)
     qd_got = swapped(qd)
     (kv_out,) = call(bind(kv_halo_kernel, z), [((z.halo * 2 * tok, z.cw), BF16)], kv_got)
@@ -589,15 +607,8 @@
     ret = call(bind(seal_kernel, z, 3), [((3 * tok, z.cw), BF16)] * group, (dq, dk, dv))
     back = swapped(ret)
 
-    def joined(*parts):
-        rows = sum(p.shape[0] for p in parts)
-        (whole,) = call(join_kernel, [((rows, buckets), F32)], parts)
-        return whole
-
-    mine, by = joined(*sums_of), 1
-    while by * 2 < group:
-        mine, by = joined(mine, swap(mine, by)), by * 2
-    other = swap(mine, by)
+    (joined,) = call(join_kernel, [((8 * sides, buckets), F32)], sums_of)
+    spread = swapped([joined] * group)
     grads = call(
         bind(unpack_kernel, z),
         [((tok, width), BF16)] * 3,
@@ -608,7 +619,7 @@
     (grad_bias,) = call(
         bind(spread_kernel, z, sides),
         [((heads * sides, buckets), F32)],
-        (mine, other),
+        spread,
         out_space=hbm,
         scratch=[pltpu.VMEM((heads * sides, buckets), F32), pltpu.SemaphoreType.DMA((1,))],
     )

time: 57.8 us -> 58.4 us (1.010)
  waiting for transfers between devices: 16.6 us -> 15.7 us
  Pallas kernels: 13.2 us -> 14.1 us
    ppermute x14 -> x15, waiting for transfers between devices: 15.7 us -> 14.8 us  [swap(): lax.ppermute(value, axis, [(i, i ^ by) for i in range(lax.axis_size(axis))])]
    pallas_call x17, Pallas kernels: 13.2 us -> 14.1 us  [call(): pl.pallas_call(kernel, out_shape=tuple((out_space(s, d) for s, d in outs)...]
    ppermute x14 -> x15, starting transfers between devices: 17.9 us -> 18.3 us  [swap(): lax.ppermute(value, axis, [(i, i ^ by) for i in range(lax.axis_size(axis))])]
  transfers between devices with their start and end apart: 17 -> 18, of which waited for: 8 -> 9; matrix products, arithmetic and copies ran while one was open for 0% -> 0% of each run, Pallas kernels for 14% -> 16%
where the time goes in v6:
time: 58.4 us; the launch traced here: 58.2 us
  starting transfers between devices  27.6 us (47%)
  waiting for transfers between devices  15.7 us (27%)
  Pallas kernels  14.1 us (24%)
  between operations  0.79 us (1%)
    ppermute x15, starting transfers between devices, swap(): lax.ppermute(value, axis, [(i, i ^ by) for i in range(lax.axis_size(axis))])  18.3 us
    ppermute x15, waiting for transfers between devices, swap(): lax.ppermute(value, axis, [(i, i ^ by) for i in range(lax.axis_size(axis))])  14.8 us
    pallas_call x17, Pallas kernels, call(): pl.pallas_call(kernel, out_shape=tuple((out_space(s, d) for s, d in outs)...  14.1 us
    ppermute x2, starting transfers between devices, shifted(): lax.ppermute(value, 'seq', [(i, i + by) for i in range(blocks) if 0 <= i...  4.8 us
    ppermute x1, starting transfers between devices, body(): lax.ppermute(stats, 'seq', [(i, (i - group) % blocks) for i in range(bloc...  4.51 us
  transfers between devices with their start and end apart: 18, of which 9 were waited for; matrix products, arithmetic and copies ran while one was open for 0% of the time, Pallas kernels for 16%

profile of v6, /device:TPU:0, one launch (start us, length us, event | category | flops | bytes accessed | tf_op | source)
XLA Modules:
  0.0 58.2 jit_solution(5693588674350768223)
XLA Ops:
  0.6 1.2 %shard_map.102 = (bf16[272,256]{1,0:T(8,128)(2,1)S(1)}, bf16[272,256]{1,0:T(8,128)(2,1)S(1)}, bf16[272,256]{1,0:T(8,128)(2,1)S(1)}, bf16[272,256]{1,0:T(8,128)(2,1)S(1)}, f32[16,128]{1,0:T(8,128)S(1)}) custom-call(bf16[128,1024]{1,0:T(8,128)(2,1)} %refs_0_.2, bf16[128,1024]{1,0:T(8,128)(2,1)} %refs_1_.2, f32[16,128]{1,0:T(8,128)} %refs_2_.1, ...), custom_call_target="tpu_custom_call" | custom-call | bytes 536592 | tf_op jit(solution)/shard_map/pallas_call | solution.py:34
  1.8 3.0 %collective-permute-start = (bf16[272,256]{1,0:T(8,128)(2,1)S(1)}, bf16[272,256]{1,0:T(8,128)(2,1)S(1)}, u32[]{:S(2)}, u32[]{:S(2)}) collective-permute-start(bf16[272,256]{1,0:T(8,128)(2,1)S(1)} %get-tuple-element.47), channel_id=1, source_target_pairs={{0,2},{2,0},{4,6},{6,4},{8,10},{10,8},{12,14},{14,12},{16,18},{18,... | collective-permute-start | bytes 417800 | tf_op jit(solution)/shard_map/ppermute | solution.py:499
  4.9 1.5 %collective-permute-start.1 = (bf16[272,256]{1,0:T(8,128)(2,1)S(1)}, bf16[272,256]{1,0:T(8,128)(2,1)S(1)}, u32[]{:S(2)}, u32[]{:S(2)}) collective-permute-start(bf16[272,256]{1,0:T(8,128)(2,1)S(1)} %get-tuple-element.48), channel_id=1, source_target_pairs={{0,4},{2,6},{4,0},{6,2},{8,12},{10,14},{12,8},{14,10},{16,20},{18,... | collective-permute-start | bytes 417800 | tf_op jit(solution)/shard_map/ppermute | solution.py:499
  6.4 0.0 collective-permute-start.2
  6.4 1.1 %shard_map.105 = (bf16[256,256]{1,0:T(8,128)(2,1)S(1)}, bf16[256,256]{1,0:T(8,128)(2,1)S(1)}, bf16[256,256]{1,0:T(8,128)(2,1)S(1)}, bf16[256,256]{1,0:T(8,128)(2,1)S(1)}) custom-call(bf16[128,1024]{1,0:T(8,128)(2,1)} %refs_0_.3, bf16[128,1024]{1,0:T(8,128)(2,1)} %refs_1_.3), custom_call_target="tpu_custom_call" | custom-call | bytes 524288 | tf_op jit(solution)/shard_map/pallas_call | solution.py:34
  7.6 2.0 %collective-permute-start.4 = (bf16[256,256]{1,0:T(8,128)(2,1)S(1)}, bf16[256,256]{1,0:T(8,128)(2,1)S(1)}, u32[]{:S(2)}, u32[]{:S(2)}) collective-permute-start(bf16[256,256]{1,0:T(8,128)(2,1)S(1)} %get-tuple-element.54), channel_id=1, source_target_pairs={{0,2},{2,0},{4,6},{6,4},{8,10},{10,8},{12,14},{14,12},{16,18},{18,... | collective-permute-start | bytes 393224 | tf_op jit(solution)/shard_map/ppermute | solution.py:499
  9.6 1.5 %collective-permute-start.5 = (bf16[256,256]{1,0:T(8,128)(2,1)S(1)}, bf16[256,256]{1,0:T(8,128)(2,1)S(1)}, u32[]{:S(2)}, u32[]{:S(2)}) collective-permute-start(bf16[256,256]{1,0:T(8,128)(2,1)S(1)} %get-tuple-element.55), channel_id=1, source_target_pairs={{0,4},{2,6},{4,0},{6,2},{8,12},{10,14},{12,8},{14,10},{16,20},{18,... | collective-permute-start | bytes 393224 | tf_op jit(solution)/shard_map/ppermute | solution.py:499
  11.1 0.0 collective-permute-done.refs_1_.refs_5_
  11.1 1.3 %collective-permute-start.6 = (bf16[256,256]{1,0:T(8,128)(2,1)S(1)}, bf16[256,256]{1,0:T(8,128)(2,1)S(1)}, u32[]{:S(2)}, u32[]{:S(2)}) collective-permute-start(bf16[256,256]{1,0:T(8,128)(2,1)S(1)} %get-tuple-element.56), channel_id=1, source_target_pairs={{0,6},{2,4},{4,2},{6,0},{8,14},{10,12},{12,10},{14,8},{16,22},{18,... | collective-permute-start | bytes 393224 | tf_op jit(solution)/shard_map/ppermute | solution.py:499
  12.4 1.4 %collective-permute-done.1.refs_2_.refs_6_ = bf16[272,256]{1,0:T(8,128)(2,1)S(1)} collective-permute-done((bf16[272,256]{1,0:T(8,128)(2,1)S(1)}, bf16[272,256]{1,0:T(8,128)(2,1)S(1)}, u32[]{:S(2)}, u32[]{:S(2)}) %collective-permute-start.1) | collective-permute-done | bytes 139296 | tf_op jit(solution)/shard_map/ppermute | solution.py:499
  13.8 0.1 collective-permute-done.2.refs_3_.refs_7_
  13.9 3.5 %collective-permute-start.3 = (bf16[768,256]{1,0:T(8,128)(2,1)S(1)}, bf16[768,256]{1,0:T(8,128)(2,1)S(1)}, u32[]{:S(2)}, u32[]{:S(2)}) collective-permute-start(bf16[768,256]{1,0:T(8,128)(2,1)S(1)} %shard_map.104), channel_id=1, source_target_pairs={{0,8},{2,10},{4,12},{6,14},{8,16},{10,18},{12,20},{14,22},{16,24},... | collective-permute-start | bytes 1179656 | tf_op jit(solution)/shard_map/ppermute | solution.py:502
  17.4 0.0 collective-permute-done.4.refs_1_
  17.4 1.2 %collective-permute-done.5.refs_2_ = bf16[256,256]{1,0:T(8,128)(2,1)S(1)} collective-permute-done((bf16[256,256]{1,0:T(8,128)(2,1)S(1)}, bf16[256,256]{1,0:T(8,128)(2,1)S(1)}, u32[]{:S(2)}, u32[]{:S(2)}) %collective-permute-start.5) | collective-permute-done | bytes 131104 | tf_op jit(solution)/shard_map/ppermute | solution.py:499
  18.6 0.0 collective-permute-done.6.refs_3_
  18.7 1.3 %collective-permute-start.7 = (bf16[816,256]{1,0:T(8,128)(2,1)S(1)}, bf16[816,256]{1,0:T(8,128)(2,1)S(1)}, u32[]{:S(2)}, u32[]{:S(2)}) collective-permute-start(bf16[816,256]{1,0:T(8,128)(2,1)S(1)} %shard_map.110), channel_id=1, source_target_pairs={{8,0},{10,2},{12,4},{14,6},{16,8},{18,10},{20,12},{22,14},{24,16},... | collective-permute-start | bytes 1253384 | tf_op jit(solution)/shard_map/ppermute | solution.py:502
  20.0 1.4 %shard_map.103 = (bf16[512,256]{1,0:T(8,128)(2,1)S(1)}, bf16[512,256]{1,0:T(8,128)(2,1)S(1)}, f32[20,128,256]{2,1,0:T(8,128)S(1)}, f32[12,128,256]{2,1,0:T(8,128)S(1)}, f32[64,256]{1,0:T(8,128)S(1)}) custom-call(bf16[272,256]{1,0:T(8,128)(2,1)S(1)} %get-tuple-element.46.refs_0_.refs_4_, bf16[272,256]{1,0:T(8,128)(2,1)S(1)} %collective-permute-done.refs_1_.refs_5_, ...), custom_call_target="tpu_custom_call" | custom-call | bytes 565248 | tf_op jit(solution)/shard_map/pallas_call | solution.py:34
  21.4 1.6 %shard_map.106 = (bf16[2,1024,128]{2,1,0:T(8,128)(2,1)S(1)}, bf16[2,1024,128]{2,1,0:T(8,128)(2,1)S(1)}, f32[20,128,256]{2,1,0:T(8,128)S(1)}, f32[20,128,256]{2,1...) custom-call(bf16[256,256]{1,0:T(8,128)(2,1)S(1)} %get-tuple-element.53.refs_0_, ...), custom_call_target="tpu_custom_call" | custom-call | flops 335544320 | bytes 3670016 | tf_op jit(solution)/shard_map/pallas_call | solution.py:34
  22.9 0.9 %collective-permute-done.3.refs_0_.refs_1_ = bf16[768,256]{1,0:T(8,128)(2,1)S(1)} collective-permute-done((bf16[768,256]{1,0:T(8,128)(2,1)S(1)}, bf16[768,256]{1,0:T(8,128)(2,1)S(1)}, u32[]{:S(2)}, u32[]{:S(2)}) %collective-permute-start.3) | collective-permute-done | bytes 393248 | tf_op jit(solution)/shard_map/ppermute | solution.py:502
  23.8 1.6 %shard_map.107 = (f32[2,8,256]{2,1,0:T(8,128)S(1)}, f32[20,256]{1,0:T(8,128)S(1)}, f32[12,256]{1,0:T(8,128)S(1)}, f32[12,128,256]{2,1,0:T(8,128)S(1)}, f32[12,12...) custom-call(bf16[768,256]{1,0:T(8,128)(2,1)S(1)} %collective-permute-done.3.refs_0_.refs_1_, ...), custom_call_target="tpu_custom_call" | custom-call | flops 201326592 | bytes 3076096 | tf_op jit(solution)/shard_map/pallas_call | solution.py:34
  25.4 4.5 %collective-permute-start.8 = (f32[2,8,256]{2,1,0:T(8,128)S(1)}, f32[2,8,256]{2,1,0:T(8,128)S(1)}, u32[]{:S(2)}, u32[]{:S(2)}) collective-permute-start(f32[2,8,256]{2,1,0:T(8,128)S(1)} %get-tuple-element.65.refs_1_), channel_id=1, source_target_pairs={{0,24},{2,26},{4,28},{6,30},{8,0},{10,2},{12,4},{14,6},{16,8},{18,... | collective-permute-start | bytes 49160 | tf_op jit(solution)/shard_map/ppermute | solution.py:569
  29.9 2.2 %shard_map.108 = (bf16[2,512,1024]{2,1,0:T(8,128)(2,1)S(1)}, bf16[2,896,1024]{2,1,0:T(8,128)(2,1)S(1)}, f32[8,128]{1,0:T(8,128)S(1)}) custom-call(f32[64,256]{1,0:T(8,128)S(1)} %get-tuple-element.52.refs_0_, f32[2,8,256]{2,1,0:T(8,128)S(1)} %get-tuple-element.65.refs_1_, f32[20,256]{1,0:T(8,128)S(1)} %get-tuple-element.66.refs_2_, ...), custom_call_target="tpu_custom_call" | custom-call | bytes 8503296 | tf_op jit(solution)/shard_map/pallas_call | solution.py:34
  32.1 0.8 %shard_map.109.refs_0_ = bf16[512,256]{1,0:T(8,128)(2,1)S(1)} custom-call(bf16[512,256]{1,0:T(8,128)(2,1)S(1)} %get-tuple-element.51.refs_4_.refs_0_, bf16[768,256]{1,0:T(8,128)(2,1)S(1)} %collective-permute-done.3.refs_0_.refs_1_, bf16[2,896,1024]{2,1,0:T(8,128)(2,1)S(1)} %get-tuple-element.72.refs_2_.refs_3_), custom_call_target="tpu_custom_call" | custom-call | flops 268435456 | bytes 4325376 | tf_op jit(solution)/shard_map/pallas_call | solution.py:34
  32.9 0.0 collective-permute-done.8.refs_3_
  32.9 0.0 collective-permute-done.7.refs_2_
  33.0 1.0 %shard_map.111 = (bf16[2,768,128]{2,1,0:T(8,128)(2,1)S(1)}, bf16[2,768,128]{2,1,0:T(8,128)(2,1)S(1)}, bf16[2,512,768]{2,1,0:T(8,128)(2,1)S(1)}, bf16[2,512,768]{2,1,0:T(8,128)(2,1)S(1)}) custom-call(bf16[512,256]{1,0:T(8,128)(2,1)S(1)} %get-tuple-element.51.refs_4_.refs_0_, bf16[512,256]{1,0:T(8,128)(2,1)S(1)} %get-tuple-element.57.refs_5_.refs_1_, ...), custom_call_target="tpu_custom_call" | custom-call | flops 201326592 | bytes 966656 | tf_op jit(solution)/shard_map/pallas_call | solution.py:34
  33.9 1.5 %shard_map.112 = (bf16[512,256]{1,0:T(8,128)(2,1)S(1)}, bf16[512,256]{1,0:T(8,128)(2,1)S(1)}) custom-call(bf16[2,1024,128]{2,1,0:T(8,128)(2,1)S(1)} %get-tuple-element.59.refs_1_.refs_0_, bf16[2,1024,128]{2,1,0:T(8,128)(2,1)S(1)} %get-tuple-element.60.refs_2_.refs_1_, bf16[2,512,1024]{2,1,0:T(8,128)(2,1)S(1)} %get-tuple-element.73.refs_2_, ...), custom_call_target="tpu_custom_call" | custom-call | flops 536870912 | bytes 10747904 | tf_op jit(solution)/shard_map/pallas_call | solution.py:34
  35.4 0.1 shard_map.113
  35.5 1.5 %collective-permute-start.9 = (bf16[384,256]{1,0:T(8,128)(2,1)S(1)}, bf16[384,256]{1,0:T(8,128)(2,1)S(1)}, u32[]{:S(2)}, u32[]{:S(2)}) collective-permute-start(bf16[384,256]{1,0:T(8,128)(2,1)S(1)} %get-tuple-element.81), channel_id=1, source_target_pairs={{0,2},{2,0},{4,6},{6,4},{8,10},{10,8},{12,14},{14,12},{16,18},{18,... | collective-permute-start | bytes 589832 | tf_op jit(solution)/shard_map/ppermute | solution.py:499
  37.0 0.5 collective-permute-start.10
  37.5 1.6 %collective-permute-start.11 = (bf16[384,256]{1,0:T(8,128)(2,1)S(1)}, bf16[384,256]{1,0:T(8,128)(2,1)S(1)}, u32[]{:S(2)}, u32[]{:S(2)}) collective-permute-start(bf16[384,256]{1,0:T(8,128)(2,1)S(1)} %get-tuple-element.83), channel_id=1, source_target_pairs={{0,6},{2,4},{4,2},{6,0},{8,14},{10,12},{12,10},{14,8},{16,22},{18,... | collective-permute-start | bytes 589832 | tf_op jit(solution)/shard_map/ppermute | solution.py:499
  39.0 0.0 collective-permute-start.12
  39.0 3.6 %collective-permute-done.12.refs_1_ = f32[8,128]{1,0:T(8,128)S(1)} collective-permute-done((f32[8,128]{1,0:T(8,128)S(1)}, f32[8,128]{1,0:T(8,128)S(1)}, u32[]{:S(2)}, u32[]{:S(2)}) %collective-permute-start.12) | collective-permute-done | bytes 4128 | tf_op jit(solution)/shard_map/ppermute | solution.py:499
  42.6 1.1 %collective-permute-start.13 = (f32[8,128]{1,0:T(8,128)S(1)}, f32[8,128]{1,0:T(8,128)S(1)}, u32[]{:S(2)}, u32[]{:S(2)}) collective-permute-start(f32[8,128]{1,0:T(8,128)S(1)} %shard_map.115.refs_0_), channel_id=1, source_target_pairs={{0,16},{2,18},{4,20},{6,22},{8,24},{10,26},{12,28},{14,30},{16,0},... | collective-permute-start | bytes 12296 | tf_op jit(solution)/shard_map/ppermute | solution.py:499
  43.7 3.5 %collective-permute-done.13.refs_1_ = f32[8,128]{1,0:T(8,128)S(1)} collective-permute-done((f32[8,128]{1,0:T(8,128)S(1)}, f32[8,128]{1,0:T(8,128)S(1)}, u32[]{:S(2)}, u32[]{:S(2)}) %collective-permute-start.13) | collective-permute-done | bytes 4128 | tf_op jit(solution)/shard_map/ppermute | solution.py:499
  47.1 0.0 collective-permute-start.14
  47.1 1.2 %collective-permute-done.14.refs_1_ = f32[8,128]{1,0:T(8,128)S(1)} collective-permute-done((f32[8,128]{1,0:T(8,128)S(1)}, f32[8,128]{1,0:T(8,128)S(1)}, u32[]{:S(2)}, u32[]{:S(2)}) %collective-permute-start.14) | collective-permute-done | bytes 4128 | tf_op jit(solution)/shard_map/ppermute | solution.py:499
  48.3 1.4 %collective-permute-start.17 = (f32[16,128]{1,0:T(8,128)S(1)}, f32[16,128]{1,0:T(8,128)S(1)}, u32[]{:S(2)}, u32[]{:S(2)}) collective-permute-start(f32[16,128]{1,0:T(8,128)S(1)} %shard_map.117.refs_0_), channel_id=1, source_target_pairs={{0,6},{2,4},{4,2},{6,0},{8,14},{10,12},{12,10},{14,8},{16,22},{18,... | collective-permute-start | bytes 24584 | tf_op jit(solution)/shard_map/ppermute | solution.py:499
  49.7 1.5 %collective-permute-start.16 = (f32[16,128]{1,0:T(8,128)S(1)}, f32[16,128]{1,0:T(8,128)S(1)}, u32[]{:S(2)}, u32[]{:S(2)}) collective-permute-start(f32[16,128]{1,0:T(8,128)S(1)} %shard_map.117.refs_0_), channel_id=1, source_target_pairs={{0,4},{2,6},{4,0},{6,2},{8,12},{10,14},{12,8},{14,10},{16,20},{18,... | collective-permute-start | bytes 24584 | tf_op jit(solution)/shard_map/ppermute | solution.py:499
  51.2 1.7 %collective-permute-done.17.refs_3_ = f32[16,128]{1,0:T(8,128)S(1)} collective-permute-done((f32[16,128]{1,0:T(8,128)S(1)}, f32[16,128]{1,0:T(8,128)S(1)}, u32[]{:S(2)}, u32[]{:S(2)}) %collective-permute-start.17) | collective-permute-done | bytes 8224 | tf_op jit(solution)/shard_map/ppermute | solution.py:499
  52.9 1.4 %collective-permute-start.15 = (f32[16,128]{1,0:T(8,128)S(1)}, f32[16,128]{1,0:T(8,128)S(1)}, u32[]{:S(2)}, u32[]{:S(2)}) collective-permute-start(f32[16,128]{1,0:T(8,128)S(1)} %shard_map.117.refs_0_), channel_id=1, source_target_pairs={{0,2},{2,0},{4,6},{6,4},{8,10},{10,8},{12,14},{14,12},{16,18},{18,... | collective-permute-start | bytes 24584 | tf_op jit(solution)/shard_map/ppermute | solution.py:499
  54.3 0.0 collective-permute-done.16.refs_2_
  54.3 2.2 %collective-permute-done.15.refs_1_ = f32[16,128]{1,0:T(8,128)S(1)} collective-permute-done((f32[16,128]{1,0:T(8,128)S(1)}, f32[16,128]{1,0:T(8,128)S(1)}, u32[]{:S(2)}, u32[]{:S(2)}) %collective-permute-start.15) | collective-permute-done | bytes 8224 | tf_op jit(solution)/shard_map/ppermute | solution.py:499
  56.5 0.6 %shard_map.118 = f32[32,128]{1,0:T(8,128)} custom-call(f32[16,128]{1,0:T(8,128)S(1)} %shard_map.117.refs_0_, f32[16,128]{1,0:T(8,128)S(1)} %collective-permute-done.15.refs_1_, f32[16,128]{1,0:T(8,128)S(1)} %collective-permute-done.16.refs_2_, f32[16,128]{1,0:T(8,128)S(1)} %collective-permute-done.17.refs_3_), custom_call_target="tpu_custom_call" | custom-call | bytes 32768 | tf_op jit(solution)/shard_map/pallas_call | solution.py:34
  57.2 0.0 collective-permute-done.9.refs_1_
  57.2 0.0 collective-permute-done.10.refs_2_
  57.2 0.0 collective-permute-done.11.refs_3_
  57.2 1.0 %shard_map.114 = (bf16[128,1024]{1,0:T(8,128)(2,1)}, bf16[128,1024]{1,0:T(8,128)(2,1)}, bf16[128,1024]{1,0:T(8,128)(2,1)}) custom-call(bf16[384,256]{1,0:T(8,128)(2,1)S(1)} %get-tuple-element.80.refs_0_, bf16[384,256]{1,0:T(8,128)(2,1)S(1)} %collective-permute-done.9.refs_1_, bf16[384,256]{1,0:T(8,128)(2,1)S(1)} %collective-permute-done.10.refs_2_, ...), custom_call_target="tpu_custom_call" | custom-call | bytes 786432 | tf_op jit(solution)/shard_map/pallas_call | solution.py:34
  (5 shorter events, 0.1 us)
Async XLA Ops:
  1.8 9.3 %collective-permute-start = (bf16[272,256]{1,0:T(8,128)(2,1)S(1)}, bf16[272,256]{1,0:T(8,128)(2,1)S(1)}, u32[]{:S(2)}, u32[]{:S(2)}) collective-permute-start(bf16[272,256]{1,0:T(8,128)(2,1)S(1)} %get-tuple-element.47), channel_id=1, source_target_pairs={{0,2},{2,0},{4,6},{6,4},{8,10},{10,8},{12,14},{14,12},{16,18},{18,... | collective-permute-start | bytes 417800 | tf_op jit(solution)/shard_map/ppermute | solution.py:499
  4.9 8.9 %collective-permute-start.1 = (bf16[272,256]{1,0:T(8,128)(2,1)S(1)}, bf16[272,256]{1,0:T(8,128)(2,1)S(1)}, u32[]{:S(2)}, u32[]{:S(2)}) collective-permute-start(bf16[272,256]{1,0:T(8,128)(2,1)S(1)} %get-tuple-element.48), channel_id=1, source_target_pairs={{0,4},{2,6},{4,0},{6,2},{8,12},{10,14},{12,8},{14,10},{16,20},{18,... | collective-permute-start | bytes 417800 | tf_op jit(solution)/shard_map/ppermute | solution.py:499
  6.4 7.5 %collective-permute-start.2 = (bf16[272,256]{1,0:T(8,128)(2,1)S(1)}, bf16[272,256]{1,0:T(8,128)(2,1)S(1)}, u32[]{:S(2)}, u32[]{:S(2)}) collective-permute-start(bf16[272,256]{1,0:T(8,128)(2,1)S(1)} %get-tuple-element.49), channel_id=1, source_target_pairs={{0,6},{2,4},{4,2},{6,0},{8,14},{10,12},{12,10},{14,8},{16,22},{18,... | collective-permute-start | bytes 417800 | tf_op jit(solution)/shard_map/ppermute | solution.py:499
  7.6 9.9 %collective-permute-start.4 = (bf16[256,256]{1,0:T(8,128)(2,1)S(1)}, bf16[256,256]{1,0:T(8,128)(2,1)S(1)}, u32[]{:S(2)}, u32[]{:S(2)}) collective-permute-start(bf16[256,256]{1,0:T(8,128)(2,1)S(1)} %get-tuple-element.54), channel_id=1, source_target_pairs={{0,2},{2,0},{4,6},{6,4},{8,10},{10,8},{12,14},{14,12},{16,18},{18,... | collective-permute-start | bytes 393224 | tf_op jit(solution)/shard_map/ppermute | solution.py:499
  9.6 9.0 %collective-permute-start.5 = (bf16[256,256]{1,0:T(8,128)(2,1)S(1)}, bf16[256,256]{1,0:T(8,128)(2,1)S(1)}, u32[]{:S(2)}, u32[]{:S(2)}) collective-permute-start(bf16[256,256]{1,0:T(8,128)(2,1)S(1)} %get-tuple-element.55), channel_id=1, source_target_pairs={{0,4},{2,6},{4,0},{6,2},{8,12},{10,14},{12,8},{14,10},{16,20},{18,... | collective-permute-start | bytes 393224 | tf_op jit(solution)/shard_map/ppermute | solution.py:499
  11.1 7.5 %collective-permute-start.6 = (bf16[256,256]{1,0:T(8,128)(2,1)S(1)}, bf16[256,256]{1,0:T(8,128)(2,1)S(1)}, u32[]{:S(2)}, u32[]{:S(2)}) collective-permute-start(bf16[256,256]{1,0:T(8,128)(2,1)S(1)} %get-tuple-element.56), channel_id=1, source_target_pairs={{0,6},{2,4},{4,2},{6,0},{8,14},{10,12},{12,10},{14,8},{16,22},{18,... | collective-permute-start | bytes 393224 | tf_op jit(solution)/shard_map/ppermute | solution.py:499
  13.9 9.9 %collective-permute-start.3 = (bf16[768,256]{1,0:T(8,128)(2,1)S(1)}, bf16[768,256]{1,0:T(8,128)(2,1)S(1)}, u32[]{:S(2)}, u32[]{:S(2)}) collective-permute-start(bf16[768,256]{1,0:T(8,128)(2,1)S(1)} %shard_map.104), channel_id=1, source_target_pairs={{0,8},{2,10},{4,12},{6,14},{8,16},{10,18},{12,20},{14,22},{16,24},... | collective-permute-start | bytes 1179656 | tf_op jit(solution)/shard_map/ppermute | solution.py:502
  18.7 14.3 %collective-permute-start.7 = (bf16[816,256]{1,0:T(8,128)(2,1)S(1)}, bf16[816,256]{1,0:T(8,128)(2,1)S(1)}, u32[]{:S(2)}, u32[]{:S(2)}) collective-permute-start(bf16[816,256]{1,0:T(8,128)(2,1)S(1)} %shard_map.110), channel_id=1, source_target_pairs={{8,0},{10,2},{12,4},{14,6},{16,8},{18,10},{20,12},{22,14},{24,16},... | collective-permute-start | bytes 1253384 | tf_op jit(solution)/shard_map/ppermute | solution.py:502
  25.4 7.5 %collective-permute-start.8 = (f32[2,8,256]{2,1,0:T(8,128)S(1)}, f32[2,8,256]{2,1,0:T(8,128)S(1)}, u32[]{:S(2)}, u32[]{:S(2)}) collective-permute-start(f32[2,8,256]{2,1,0:T(8,128)S(1)} %get-tuple-element.65.refs_1_), channel_id=1, source_target_pairs={{0,24},{2,26},{4,28},{6,30},{8,0},{10,2},{12,4},{14,6},{16,8},{18,... | collective-permute-start | bytes 49160 | tf_op jit(solution)/shard_map/ppermute | solution.py:569
  35.5 21.7 %collective-permute-start.9 = (bf16[384,256]{1,0:T(8,128)(2,1)S(1)}, bf16[384,256]{1,0:T(8,128)(2,1)S(1)}, u32[]{:S(2)}, u32[]{:S(2)}) collective-permute-start(bf16[384,256]{1,0:T(8,128)(2,1)S(1)} %get-tuple-element.81), channel_id=1, source_target_pairs={{0,2},{2,0},{4,6},{6,4},{8,10},{10,8},{12,14},{14,12},{16,18},{18,... | collective-permute-start | bytes 589832 | tf_op jit(solution)/shard_map/ppermute | solution.py:499
  37.0 20.2 %collective-permute-start.10 = (bf16[384,256]{1,0:T(8,128)(2,1)S(1)}, bf16[384,256]{1,0:T(8,128)(2,1)S(1)}, u32[]{:S(2)}, u32[]{:S(2)}) collective-permute-start(bf16[384,256]{1,0:T(8,128)(2,1)S(1)} %get-tuple-element.82), channel_id=1, source_target_pairs={{0,4},{2,6},{4,0},{6,2},{8,12},{10,14},{12,8},{14,10},{16,20},{18,... | collective-permute-start | bytes 589832 | tf_op jit(solution)/shard_map/ppermute | solution.py:499
  37.5 19.7 %collective-permute-start.11 = (bf16[384,256]{1,0:T(8,128)(2,1)S(1)}, bf16[384,256]{1,0:T(8,128)(2,1)S(1)}, u32[]{:S(2)}, u32[]{:S(2)}) collective-permute-start(bf16[384,256]{1,0:T(8,128)(2,1)S(1)} %get-tuple-element.83), channel_id=1, source_target_pairs={{0,6},{2,4},{4,2},{6,0},{8,14},{10,12},{12,10},{14,8},{16,22},{18,... | collective-permute-start | bytes 589832 | tf_op jit(solution)/shard_map/ppermute | solution.py:499
  39.0 3.6 %collective-permute-start.12 = (f32[8,128]{1,0:T(8,128)S(1)}, f32[8,128]{1,0:T(8,128)S(1)}, u32[]{:S(2)}, u32[]{:S(2)}) collective-permute-start(f32[8,128]{1,0:T(8,128)S(1)} %get-tuple-element.87.refs_0_), channel_id=1, source_target_pairs={{0,8},{2,10},{4,12},{6,14},{8,0},{10,2},{12,4},{14,6},{16,24},{18,... | collective-permute-start | bytes 12296 | tf_op jit(solution)/shard_map/ppermute | solution.py:499
  42.6 4.5 %collective-permute-start.13 = (f32[8,128]{1,0:T(8,128)S(1)}, f32[8,128]{1,0:T(8,128)S(1)}, u32[]{:S(2)}, u32[]{:S(2)}) collective-permute-start(f32[8,128]{1,0:T(8,128)S(1)} %shard_map.115.refs_0_), channel_id=1, source_target_pairs={{0,16},{2,18},{4,20},{6,22},{8,24},{10,26},{12,28},{14,30},{16,0},... | collective-permute-start | bytes 12296 | tf_op jit(solution)/shard_map/ppermute | solution.py:499
  47.1 1.2 %collective-permute-start.14 = (f32[8,128]{1,0:T(8,128)S(1)}, f32[8,128]{1,0:T(8,128)S(1)}, u32[]{:S(2)}, u32[]{:S(2)}) collective-permute-start(f32[8,128]{1,0:T(8,128)S(1)} %shard_map.116.refs_0_), channel_id=1, source_target_pairs={{0,1},{1,0},{2,3},{3,2},{4,5},{5,4},{6,7},{7,6},{8,9},{9,8},{10,11... | collective-permute-start | bytes 12296 | tf_op jit(solution)/shard_map/ppermute | solution.py:499
  48.3 4.5 %collective-permute-start.17 = (f32[16,128]{1,0:T(8,128)S(1)}, f32[16,128]{1,0:T(8,128)S(1)}, u32[]{:S(2)}, u32[]{:S(2)}) collective-permute-start(f32[16,128]{1,0:T(8,128)S(1)} %shard_map.117.refs_0_), channel_id=1, source_target_pairs={{0,6},{2,4},{4,2},{6,0},{8,14},{10,12},{12,10},{14,8},{16,22},{18,... | collective-permute-start | bytes 24584 | tf_op jit(solution)/shard_map/ppermute | solution.py:499
  49.7 4.6 %collective-permute-start.16 = (f32[16,128]{1,0:T(8,128)S(1)}, f32[16,128]{1,0:T(8,128)S(1)}, u32[]{:S(2)}, u32[]{:S(2)}) collective-permute-start(f32[16,128]{1,0:T(8,128)S(1)} %shard_map.117.refs_0_), channel_id=1, source_target_pairs={{0,4},{2,6},{4,0},{6,2},{8,12},{10,14},{12,8},{14,10},{16,20},{18,... | collective-permute-start | bytes 24584 | tf_op jit(solution)/shard_map/ppermute | solution.py:499
  52.9 3.7 %collective-permute-start.15 = (f32[16,128]{1,0:T(8,128)S(1)}, f32[16,128]{1,0:T(8,128)S(1)}, u32[]{:S(2)}, u32[]{:S(2)}) collective-permute-start(f32[16,128]{1,0:T(8,128)S(1)} %shard_map.117.refs_0_), channel_id=1, source_target_pairs={{0,2},{2,0},{4,6},{6,4},{8,10},{10,8},{12,14},{14,12},{16,18},{18,... | collective-permute-start | bytes 24584 | tf_op jit(solution)/shard_map/ppermute | solution.py:499

commit v7 on v6

--- a/solution.py
+++ b/solution.py
@@ -435,11 +435,6 @@
             sends[k][n * z.tok : (n + 1) * z.tok, :] = ref[rows, :]
 
 
-def join_kernel(*refs):
-    for n, ref in enumerate(refs[:-1]):
-        refs[-1][8 * n : 8 * n + 8, :] = ref[...]
-
-
 def add_kernel(*refs):
     total = refs[0][...]
     for ref in refs[1:-1]:
@@ -462,17 +457,19 @@
         copy.wait()
 
 
-def spread_kernel(z, sides, *refs):
-    sums, (gb, held, sem) = refs[: z.group], refs[z.group :]
-    me = z.me()
-    owner = lax.broadcasted_iota(jnp.int32, held.shape, 0) // z.hg
-    total = jnp.zeros(held.shape, F32)
+def collect_kernel(z, *refs):
+    sums, out = refs[:-1], refs[-1]
+    owner = lax.broadcasted_iota(jnp.int32, out.shape, 0) // z.hg
+    total = jnp.zeros(out.shape, F32)
     for k in range(z.group):
-        for n in range(sides):
-            wide = jnp.concatenate([sums[k][8 * n : 8 * n + z.hg, :]] * (held.shape[0] // z.hg), axis=0)
-            side = lax.axis_index("head") ^ n
-            total = total + jnp.where(owner == side * z.group + (me ^ k), wide, 0.0)
-    held[...] = total
+        wide = jnp.concatenate([sums[k][0 : z.hg, :]] * (out.shape[0] // z.hg), axis=0)
+        total = total + jnp.where(owner == lax.axis_index("head") * z.group + (z.me() ^ k), wide, 0.0)
+    out[...] = total
+
+
+def final_kernel(*refs):
+    parts, (gb, held, sem) = refs[:-3], refs[-3:]
+    held[...] = sum(ref[...] for ref in parts)
     copy = pltpu.make_async_copy(held, gb, sem.at[0])
     copy.start()
     copy.wait()
@@ -582,7 +579,6 @@
         other = swap(gb, by)
         gb = added(gb, other)
         by = by * 2
-    sums_of = [gb] + [swap(gb, k, "head") for k in range(1, sides)]
     (dq,) = call(
         bind(grad_q_kernel, z),
         [((group * tok, z.cw), BF16)],
@@ -607,8 +603,9 @@
     ret = call(bind(seal_kernel, z, 3), [((3 * tok, z.cw), BF16)] * group, (dq, dk, dv))
     back = swapped(ret)
 
-    (joined,) = call(join_kernel, [((8 * sides, buckets), F32)], sums_of)
-    spread = swapped([joined] * group)
+    spread = swapped([gb] * group)
+    (half,) = call(bind(collect_kernel, z), [((heads * sides, buckets), F32)], spread)
+    halves = [half] + [swap(half, k, "head") for k in range(1, sides)]
     grads = call(
         bind(unpack_kernel, z),
         [((tok, width), BF16)] * 3,
@@ -617,9 +614,9 @@
         scratch=[pltpu.SemaphoreType.DMA((3 * group,))],
     )
     (grad_bias,) = call(
-        bind(spread_kernel, z, sides),
+        final_kernel,
         [((heads * sides, buckets), F32)],
-        spread,
+        halves,
         out_space=hbm,
         scratch=[pltpu.VMEM((heads * sides, buckets), F32), pltpu.SemaphoreType.DMA((1,))],
     )

time: 58.4 us -> 58.4 us (level)
  no operation moved by 1% of the time
where the time goes in v7:
time: 58.4 us; the launch traced here: 58.2 us
  starting transfers between devices  27.7 us (47%)
  waiting for transfers between devices  15.6 us (27%)
  Pallas kernels  14.1 us (24%)
  between operations  0.8 us (1%)
    ppermute x15, starting transfers between devices, swap(): lax.ppermute(value, axis, [(i, i ^ by) for i in range(lax.axis_size(axis))])  18.4 us
    ppermute x15, waiting for transfers between devices, swap(): lax.ppermute(value, axis, [(i, i ^ by) for i in range(lax.axis_size(axis))])  14.7 us
    pallas_call x17, Pallas kernels, call(): pl.pallas_call(kernel, out_shape=tuple((out_space(s, d) for s, d in outs)...  14.1 us
    ppermute x2, starting transfers between devices, shifted(): lax.ppermute(value, 'seq', [(i, i + by) for i in range(blocks) if 0 <= i...  4.8 us
    ppermute x1, starting transfers between devices, body(): lax.ppermute(stats, 'seq', [(i, (i - group) % blocks) for i in range(bloc...  4.51 us
  transfers between devices with their start and end apart: 18, of which 9 were waited for; matrix products, arithmetic and copies ran while one was open for 0% of the time, Pallas kernels for 16%

profile of v7, /device:TPU:0, one launch (start us, length us, event | category | flops | bytes accessed | tf_op | source)
XLA Modules:
  0.0 58.2 jit_solution(7274055202613730976)
XLA Ops:
  0.6 1.2 %shard_map.102 = (bf16[272,256]{1,0:T(8,128)(2,1)S(1)}, bf16[272,256]{1,0:T(8,128)(2,1)S(1)}, bf16[272,256]{1,0:T(8,128)(2,1)S(1)}, bf16[272,256]{1,0:T(8,128)(2,1)S(1)}, f32[16,128]{1,0:T(8,128)S(1)}) custom-call(bf16[128,1024]{1,0:T(8,128)(2,1)} %refs_0_.2, bf16[128,1024]{1,0:T(8,128)(2,1)} %refs_1_.2, f32[16,128]{1,0:T(8,128)} %refs_2_.1, ...), custom_call_target="tpu_custom_call" | custom-call | bytes 536592 | tf_op jit(solution)/shard_map/pallas_call | solution.py:34
  1.8 3.0 %collective-permute-start = (bf16[272,256]{1,0:T(8,128)(2,1)S(1)}, bf16[272,256]{1,0:T(8,128)(2,1)S(1)}, u32[]{:S(2)}, u32[]{:S(2)}) collective-permute-start(bf16[272,256]{1,0:T(8,128)(2,1)S(1)} %get-tuple-element.47), channel_id=1, source_target_pairs={{0,2},{2,0},{4,6},{6,4},{8,10},{10,8},{12,14},{14,12},{16,18},{18,... | collective-permute-start | bytes 417800 | tf_op jit(solution)/shard_map/ppermute | solution.py:496
  4.9 1.5 %collective-permute-start.1 = (bf16[272,256]{1,0:T(8,128)(2,1)S(1)}, bf16[272,256]{1,0:T(8,128)(2,1)S(1)}, u32[]{:S(2)}, u32[]{:S(2)}) collective-permute-start(bf16[272,256]{1,0:T(8,128)(2,1)S(1)} %get-tuple-element.48), channel_id=1, source_target_pairs={{0,4},{2,6},{4,0},{6,2},{8,12},{10,14},{12,8},{14,10},{16,20},{18,... | collective-permute-start | bytes 417800 | tf_op jit(solution)/shard_map/ppermute | solution.py:496
  6.4 0.0 collective-permute-start.2
  6.4 1.1 %shard_map.105 = (bf16[256,256]{1,0:T(8,128)(2,1)S(1)}, bf16[256,256]{1,0:T(8,128)(2,1)S(1)}, bf16[256,256]{1,0:T(8,128)(2,1)S(1)}, bf16[256,256]{1,0:T(8,128)(2,1)S(1)}) custom-call(bf16[128,1024]{1,0:T(8,128)(2,1)} %refs_0_.3, bf16[128,1024]{1,0:T(8,128)(2,1)} %refs_1_.3), custom_call_target="tpu_custom_call" | custom-call | bytes 524288 | tf_op jit(solution)/shard_map/pallas_call | solution.py:34
  7.6 2.0 %collective-permute-start.4 = (bf16[256,256]{1,0:T(8,128)(2,1)S(1)}, bf16[256,256]{1,0:T(8,128)(2,1)S(1)}, u32[]{:S(2)}, u32[]{:S(2)}) collective-permute-start(bf16[256,256]{1,0:T(8,128)(2,1)S(1)} %get-tuple-element.54), channel_id=1, source_target_pairs={{0,2},{2,0},{4,6},{6,4},{8,10},{10,8},{12,14},{14,12},{16,18},{18,... | collective-permute-start | bytes 393224 | tf_op jit(solution)/shard_map/ppermute | solution.py:496
  9.6 1.5 %collective-permute-start.5 = (bf16[256,256]{1,0:T(8,128)(2,1)S(1)}, bf16[256,256]{1,0:T(8,128)(2,1)S(1)}, u32[]{:S(2)}, u32[]{:S(2)}) collective-permute-start(bf16[256,256]{1,0:T(8,128)(2,1)S(1)} %get-tuple-element.55), channel_id=1, source_target_pairs={{0,4},{2,6},{4,0},{6,2},{8,12},{10,14},{12,8},{14,10},{16,20},{18,... | collective-permute-start | bytes 393224 | tf_op jit(solution)/shard_map/ppermute | solution.py:496
  11.1 0.0 collective-permute-done.refs_1_.refs_5_
  11.1 1.3 %collective-permute-start.6 = (bf16[256,256]{1,0:T(8,128)(2,1)S(1)}, bf16[256,256]{1,0:T(8,128)(2,1)S(1)}, u32[]{:S(2)}, u32[]{:S(2)}) collective-permute-start(bf16[256,256]{1,0:T(8,128)(2,1)S(1)} %get-tuple-element.56), channel_id=1, source_target_pairs={{0,6},{2,4},{4,2},{6,0},{8,14},{10,12},{12,10},{14,8},{16,22},{18,... | collective-permute-start | bytes 393224 | tf_op jit(solution)/shard_map/ppermute | solution.py:496
  12.4 1.4 %collective-permute-done.1.refs_2_.refs_6_ = bf16[272,256]{1,0:T(8,128)(2,1)S(1)} collective-permute-done((bf16[272,256]{1,0:T(8,128)(2,1)S(1)}, bf16[272,256]{1,0:T(8,128)(2,1)S(1)}, u32[]{:S(2)}, u32[]{:S(2)}) %collective-permute-start.1) | collective-permute-done | bytes 139296 | tf_op jit(solution)/shard_map/ppermute | solution.py:496
  13.8 0.1 collective-permute-done.2.refs_3_.refs_7_
  13.9 3.5 %collective-permute-start.3 = (bf16[768,256]{1,0:T(8,128)(2,1)S(1)}, bf16[768,256]{1,0:T(8,128)(2,1)S(1)}, u32[]{:S(2)}, u32[]{:S(2)}) collective-permute-start(bf16[768,256]{1,0:T(8,128)(2,1)S(1)} %shard_map.104), channel_id=1, source_target_pairs={{0,8},{2,10},{4,12},{6,14},{8,16},{10,18},{12,20},{14,22},{16,24},... | collective-permute-start | bytes 1179656 | tf_op jit(solution)/shard_map/ppermute | solution.py:499
  17.4 0.0 collective-permute-done.4.refs_1_
  17.4 1.2 %collective-permute-done.5.refs_2_ = bf16[256,256]{1,0:T(8,128)(2,1)S(1)} collective-permute-done((bf16[256,256]{1,0:T(8,128)(2,1)S(1)}, bf16[256,256]{1,0:T(8,128)(2,1)S(1)}, u32[]{:S(2)}, u32[]{:S(2)}) %collective-permute-start.5) | collective-permute-done | bytes 131104 | tf_op jit(solution)/shard_map/ppermute | solution.py:496
  18.6 0.0 collective-permute-done.6.refs_3_
  18.7 1.3 %collective-permute-start.7 = (bf16[816,256]{1,0:T(8,128)(2,1)S(1)}, bf16[816,256]{1,0:T(8,128)(2,1)S(1)}, u32[]{:S(2)}, u32[]{:S(2)}) collective-permute-start(bf16[816,256]{1,0:T(8,128)(2,1)S(1)} %shard_map.110), channel_id=1, source_target_pairs={{8,0},{10,2},{12,4},{14,6},{16,8},{18,10},{20,12},{22,14},{24,16},... | collective-permute-start | bytes 1253384 | tf_op jit(solution)/shard_map/ppermute | solution.py:499
  20.0 1.4 %shard_map.103 = (bf16[512,256]{1,0:T(8,128)(2,1)S(1)}, bf16[512,256]{1,0:T(8,128)(2,1)S(1)}, f32[20,128,256]{2,1,0:T(8,128)S(1)}, f32[12,128,256]{2,1,0:T(8,128)S(1)}, f32[64,256]{1,0:T(8,128)S(1)}) custom-call(bf16[272,256]{1,0:T(8,128)(2,1)S(1)} %get-tuple-element.46.refs_0_.refs_4_, bf16[272,256]{1,0:T(8,128)(2,1)S(1)} %collective-permute-done.refs_1_.refs_5_, ...), custom_call_target="tpu_custom_call" | custom-call | bytes 565248 | tf_op jit(solution)/shard_map/pallas_call | solution.py:34
  21.4 1.6 %shard_map.106 = (bf16[2,1024,128]{2,1,0:T(8,128)(2,1)S(1)}, bf16[2,1024,128]{2,1,0:T(8,128)(2,1)S(1)}, f32[20,128,256]{2,1,0:T(8,128)S(1)}, f32[20,128,256]{2,1...) custom-call(bf16[256,256]{1,0:T(8,128)(2,1)S(1)} %get-tuple-element.53.refs_0_, ...), custom_call_target="tpu_custom_call" | custom-call | flops 335544320 | bytes 3670016 | tf_op jit(solution)/shard_map/pallas_call | solution.py:34
  22.9 0.9 %collective-permute-done.3.refs_0_.refs_1_ = bf16[768,256]{1,0:T(8,128)(2,1)S(1)} collective-permute-done((bf16[768,256]{1,0:T(8,128)(2,1)S(1)}, bf16[768,256]{1,0:T(8,128)(2,1)S(1)}, u32[]{:S(2)}, u32[]{:S(2)}) %collective-permute-start.3) | collective-permute-done | bytes 393248 | tf_op jit(solution)/shard_map/ppermute | solution.py:499
  23.8 1.6 %shard_map.107 = (f32[2,8,256]{2,1,0:T(8,128)S(1)}, f32[20,256]{1,0:T(8,128)S(1)}, f32[12,256]{1,0:T(8,128)S(1)}, f32[12,128,256]{2,1,0:T(8,128)S(1)}, f32[12,12...) custom-call(bf16[768,256]{1,0:T(8,128)(2,1)S(1)} %collective-permute-done.3.refs_0_.refs_1_, ...), custom_call_target="tpu_custom_call" | custom-call | flops 201326592 | bytes 3076096 | tf_op jit(solution)/shard_map/pallas_call | solution.py:34
  25.4 4.5 %collective-permute-start.8 = (f32[2,8,256]{2,1,0:T(8,128)S(1)}, f32[2,8,256]{2,1,0:T(8,128)S(1)}, u32[]{:S(2)}, u32[]{:S(2)}) collective-permute-start(f32[2,8,256]{2,1,0:T(8,128)S(1)} %get-tuple-element.65.refs_1_), channel_id=1, source_target_pairs={{0,24},{2,26},{4,28},{6,30},{8,0},{10,2},{12,4},{14,6},{16,8},{18,... | collective-permute-start | bytes 49160 | tf_op jit(solution)/shard_map/ppermute | solution.py:566
  29.9 2.2 %shard_map.108 = (bf16[2,512,1024]{2,1,0:T(8,128)(2,1)S(1)}, bf16[2,896,1024]{2,1,0:T(8,128)(2,1)S(1)}, f32[8,128]{1,0:T(8,128)S(1)}) custom-call(f32[64,256]{1,0:T(8,128)S(1)} %get-tuple-element.52.refs_0_, f32[2,8,256]{2,1,0:T(8,128)S(1)} %get-tuple-element.65.refs_1_, f32[20,256]{1,0:T(8,128)S(1)} %get-tuple-element.66.refs_2_, ...), custom_call_target="tpu_custom_call" | custom-call | bytes 8503296 | tf_op jit(solution)/shard_map/pallas_call | solution.py:34
  32.1 0.8 %shard_map.109.refs_0_ = bf16[512,256]{1,0:T(8,128)(2,1)S(1)} custom-call(bf16[512,256]{1,0:T(8,128)(2,1)S(1)} %get-tuple-element.51.refs_4_.refs_0_, bf16[768,256]{1,0:T(8,128)(2,1)S(1)} %collective-permute-done.3.refs_0_.refs_1_, bf16[2,896,1024]{2,1,0:T(8,128)(2,1)S(1)} %get-tuple-element.72.refs_2_.refs_3_), custom_call_target="tpu_custom_call" | custom-call | flops 268435456 | bytes 4325376 | tf_op jit(solution)/shard_map/pallas_call | solution.py:34
  32.9 0.0 collective-permute-done.8.refs_3_
  32.9 0.0 collective-permute-done.7.refs_2_
  33.0 1.0 %shard_map.111 = (bf16[2,768,128]{2,1,0:T(8,128)(2,1)S(1)}, bf16[2,768,128]{2,1,0:T(8,128)(2,1)S(1)}, bf16[2,512,768]{2,1,0:T(8,128)(2,1)S(1)}, bf16[2,512,768]{2,1,0:T(8,128)(2,1)S(1)}) custom-call(bf16[512,256]{1,0:T(8,128)(2,1)S(1)} %get-tuple-element.51.refs_4_.refs_0_, bf16[512,256]{1,0:T(8,128)(2,1)S(1)} %get-tuple-element.57.refs_5_.refs_1_, ...), custom_call_target="tpu_custom_call" | custom-call | flops 201326592 | bytes 966656 | tf_op jit(solution)/shard_map/pallas_call | solution.py:34
  33.9 1.5 %shard_map.112 = (bf16[512,256]{1,0:T(8,128)(2,1)S(1)}, bf16[512,256]{1,0:T(8,128)(2,1)S(1)}) custom-call(bf16[2,1024,128]{2,1,0:T(8,128)(2,1)S(1)} %get-tuple-element.59.refs_1_.refs_0_, bf16[2,1024,128]{2,1,0:T(8,128)(2,1)S(1)} %get-tuple-element.60.refs_2_.refs_1_, bf16[2,512,1024]{2,1,0:T(8,128)(2,1)S(1)} %get-tuple-element.73.refs_2_, ...), custom_call_target="tpu_custom_call" | custom-call | flops 536870912 | bytes 10747904 | tf_op jit(solution)/shard_map/pallas_call | solution.py:34
  35.4 0.1 shard_map.113
  35.5 1.5 %collective-permute-start.9 = (bf16[384,256]{1,0:T(8,128)(2,1)S(1)}, bf16[384,256]{1,0:T(8,128)(2,1)S(1)}, u32[]{:S(2)}, u32[]{:S(2)}) collective-permute-start(bf16[384,256]{1,0:T(8,128)(2,1)S(1)} %get-tuple-element.81), channel_id=1, source_target_pairs={{0,2},{2,0},{4,6},{6,4},{8,10},{10,8},{12,14},{14,12},{16,18},{18,... | collective-permute-start | bytes 589832 | tf_op jit(solution)/shard_map/ppermute | solution.py:496
  37.0 0.5 collective-permute-start.10
  37.5 1.6 %collective-permute-start.11 = (bf16[384,256]{1,0:T(8,128)(2,1)S(1)}, bf16[384,256]{1,0:T(8,128)(2,1)S(1)}, u32[]{:S(2)}, u32[]{:S(2)}) collective-permute-start(bf16[384,256]{1,0:T(8,128)(2,1)S(1)} %get-tuple-element.83), channel_id=1, source_target_pairs={{0,6},{2,4},{4,2},{6,0},{8,14},{10,12},{12,10},{14,8},{16,22},{18,... | collective-permute-start | bytes 589832 | tf_op jit(solution)/shard_map/ppermute | solution.py:496
  39.0 0.0 collective-permute-start.12
  39.0 3.6 %collective-permute-done.12.refs_1_ = f32[8,128]{1,0:T(8,128)S(1)} collective-permute-done((f32[8,128]{1,0:T(8,128)S(1)}, f32[8,128]{1,0:T(8,128)S(1)}, u32[]{:S(2)}, u32[]{:S(2)}) %collective-permute-start.12) | collective-permute-done | bytes 4128 | tf_op jit(solution)/shard_map/ppermute | solution.py:496
  42.6 1.1 %collective-permute-start.13 = (f32[8,128]{1,0:T(8,128)S(1)}, f32[8,128]{1,0:T(8,128)S(1)}, u32[]{:S(2)}, u32[]{:S(2)}) collective-permute-start(f32[8,128]{1,0:T(8,128)S(1)} %shard_map.115.refs_0_), channel_id=1, source_target_pairs={{0,16},{2,18},{4,20},{6,22},{8,24},{10,26},{12,28},{14,30},{16,0},... | collective-permute-start | bytes 12296 | tf_op jit(solution)/shard_map/ppermute | solution.py:496
  43.7 3.5 %collective-permute-done.13.refs_1_ = f32[8,128]{1,0:T(8,128)S(1)} collective-permute-done((f32[8,128]{1,0:T(8,128)S(1)}, f32[8,128]{1,0:T(8,128)S(1)}, u32[]{:S(2)}, u32[]{:S(2)}) %collective-permute-start.13) | collective-permute-done | bytes 4128 | tf_op jit(solution)/shard_map/ppermute | solution.py:496
  47.1 1.4 %collective-permute-start.16 = (f32[8,128]{1,0:T(8,128)S(1)}, f32[8,128]{1,0:T(8,128)S(1)}, u32[]{:S(2)}, u32[]{:S(2)}) collective-permute-start(f32[8,128]{1,0:T(8,128)S(1)} %shard_map.116.refs_0_), channel_id=1, source_target_pairs={{0,6},{2,4},{4,2},{6,0},{8,14},{10,12},{12,10},{14,8},{16,22},{18,... | collective-permute-start | bytes 12296 | tf_op jit(solution)/shard_map/ppermute | solution.py:496
  48.5 1.5 %collective-permute-start.15 = (f32[8,128]{1,0:T(8,128)S(1)}, f32[8,128]{1,0:T(8,128)S(1)}, u32[]{:S(2)}, u32[]{:S(2)}) collective-permute-start(f32[8,128]{1,0:T(8,128)S(1)} %shard_map.116.refs_0_), channel_id=1, source_target_pairs={{0,4},{2,6},{4,0},{6,2},{8,12},{10,14},{12,8},{14,10},{16,20},{18,... | collective-permute-start | bytes 12296 | tf_op jit(solution)/shard_map/ppermute | solution.py:496
  50.0 1.6 %collective-permute-done.16.refs_3_ = f32[8,128]{1,0:T(8,128)S(1)} collective-permute-done((f32[8,128]{1,0:T(8,128)S(1)}, f32[8,128]{1,0:T(8,128)S(1)}, u32[]{:S(2)}, u32[]{:S(2)}) %collective-permute-start.16) | collective-permute-done | bytes 4128 | tf_op jit(solution)/shard_map/ppermute | solution.py:496
  51.6 1.4 %collective-permute-start.14 = (f32[8,128]{1,0:T(8,128)S(1)}, f32[8,128]{1,0:T(8,128)S(1)}, u32[]{:S(2)}, u32[]{:S(2)}) collective-permute-start(f32[8,128]{1,0:T(8,128)S(1)} %shard_map.116.refs_0_), channel_id=1, source_target_pairs={{0,2},{2,0},{4,6},{6,4},{8,10},{10,8},{12,14},{14,12},{16,18},{18,... | collective-permute-start | bytes 12296 | tf_op jit(solution)/shard_map/ppermute | solution.py:496
  53.1 0.0 collective-permute-done.15.refs_2_
  53.1 2.2 %collective-permute-done.14.refs_1_ = f32[8,128]{1,0:T(8,128)S(1)} collective-permute-done((f32[8,128]{1,0:T(8,128)S(1)}, f32[8,128]{1,0:T(8,128)S(1)}, u32[]{:S(2)}, u32[]{:S(2)}) %collective-permute-start.14) | collective-permute-done | bytes 4128 | tf_op jit(solution)/shard_map/ppermute | solution.py:496
  55.3 0.1 collective-permute-start.17
  55.4 1.2 %collective-permute-done.17.refs_1_ = f32[32,128]{1,0:T(8,128)S(1)} collective-permute-done((f32[32,128]{1,0:T(8,128)S(1)}, f32[32,128]{1,0:T(8,128)S(1)}, u32[]{:S(2)}, u32[]{:S(2)}) %collective-permute-start.17) | collective-permute-done | bytes 16416 | tf_op jit(solution)/shard_map/ppermute | solution.py:496
  56.5 0.6 %shard_map.118 = f32[32,128]{1,0:T(8,128)} custom-call(f32[32,128]{1,0:T(8,128)S(1)} %shard_map.117.refs_0_, f32[32,128]{1,0:T(8,128)S(1)} %collective-permute-done.17.refs_1_), custom_call_target="tpu_custom_call" | custom-call | bytes 32768 | tf_op jit(solution)/shard_map/pallas_call | solution.py:34
  57.1 0.0 collective-permute-done.9.refs_1_
  57.2 0.0 collective-permute-done.10.refs_2_
  57.2 0.0 collective-permute-done.11.refs_3_
  57.2 1.0 %shard_map.114 = (bf16[128,1024]{1,0:T(8,128)(2,1)}, bf16[128,1024]{1,0:T(8,128)(2,1)}, bf16[128,1024]{1,0:T(8,128)(2,1)}) custom-call(bf16[384,256]{1,0:T(8,128)(2,1)S(1)} %get-tuple-element.80.refs_0_, bf16[384,256]{1,0:T(8,128)(2,1)S(1)} %collective-permute-done.9.refs_1_, bf16[384,256]{1,0:T(8,128)(2,1)S(1)} %collective-permute-done.10.refs_2_, ...), custom_call_target="tpu_custom_call" | custom-call | bytes 786432 | tf_op jit(solution)/shard_map/pallas_call | solution.py:34
  (5 shorter events, 0.1 us)
Async XLA Ops:
  1.8 9.3 %collective-permute-start = (bf16[272,256]{1,0:T(8,128)(2,1)S(1)}, bf16[272,256]{1,0:T(8,128)(2,1)S(1)}, u32[]{:S(2)}, u32[]{:S(2)}) collective-permute-start(bf16[272,256]{1,0:T(8,128)(2,1)S(1)} %get-tuple-element.47), channel_id=1, source_target_pairs={{0,2},{2,0},{4,6},{6,4},{8,10},{10,8},{12,14},{14,12},{16,18},{18,... | collective-permute-start | bytes 417800 | tf_op jit(solution)/shard_map/ppermute | solution.py:496
  4.9 8.9 %collective-permute-start.1 = (bf16[272,256]{1,0:T(8,128)(2,1)S(1)}, bf16[272,256]{1,0:T(8,128)(2,1)S(1)}, u32[]{:S(2)}, u32[]{:S(2)}) collective-permute-start(bf16[272,256]{1,0:T(8,128)(2,1)S(1)} %get-tuple-element.48), channel_id=1, source_target_pairs={{0,4},{2,6},{4,0},{6,2},{8,12},{10,14},{12,8},{14,10},{16,20},{18,... | collective-permute-start | bytes 417800 | tf_op jit(solution)/shard_map/ppermute | solution.py:496
  6.4 7.5 %collective-permute-start.2 = (bf16[272,256]{1,0:T(8,128)(2,1)S(1)}, bf16[272,256]{1,0:T(8,128)(2,1)S(1)}, u32[]{:S(2)}, u32[]{:S(2)}) collective-permute-start(bf16[272,256]{1,0:T(8,128)(2,1)S(1)} %get-tuple-element.49), channel_id=1, source_target_pairs={{0,6},{2,4},{4,2},{6,0},{8,14},{10,12},{12,10},{14,8},{16,22},{18,... | collective-permute-start | bytes 417800 | tf_op jit(solution)/shard_map/ppermute | solution.py:496
  7.6 9.9 %collective-permute-start.4 = (bf16[256,256]{1,0:T(8,128)(2,1)S(1)}, bf16[256,256]{1,0:T(8,128)(2,1)S(1)}, u32[]{:S(2)}, u32[]{:S(2)}) collective-permute-start(bf16[256,256]{1,0:T(8,128)(2,1)S(1)} %get-tuple-element.54), channel_id=1, source_target_pairs={{0,2},{2,0},{4,6},{6,4},{8,10},{10,8},{12,14},{14,12},{16,18},{18,... | collective-permute-start | bytes 393224 | tf_op jit(solution)/shard_map/ppermute | solution.py:496
  9.6 9.0 %collective-permute-start.5 = (bf16[256,256]{1,0:T(8,128)(2,1)S(1)}, bf16[256,256]{1,0:T(8,128)(2,1)S(1)}, u32[]{:S(2)}, u32[]{:S(2)}) collective-permute-start(bf16[256,256]{1,0:T(8,128)(2,1)S(1)} %get-tuple-element.55), channel_id=1, source_target_pairs={{0,4},{2,6},{4,0},{6,2},{8,12},{10,14},{12,8},{14,10},{16,20},{18,... | collective-permute-start | bytes 393224 | tf_op jit(solution)/shard_map/ppermute | solution.py:496
  11.1 7.5 %collective-permute-start.6 = (bf16[256,256]{1,0:T(8,128)(2,1)S(1)}, bf16[256,256]{1,0:T(8,128)(2,1)S(1)}, u32[]{:S(2)}, u32[]{:S(2)}) collective-permute-start(bf16[256,256]{1,0:T(8,128)(2,1)S(1)} %get-tuple-element.56), channel_id=1, source_target_pairs={{0,6},{2,4},{4,2},{6,0},{8,14},{10,12},{12,10},{14,8},{16,22},{18,... | collective-permute-start | bytes 393224 | tf_op jit(solution)/shard_map/ppermute | solution.py:496
  13.9 9.9 %collective-permute-start.3 = (bf16[768,256]{1,0:T(8,128)(2,1)S(1)}, bf16[768,256]{1,0:T(8,128)(2,1)S(1)}, u32[]{:S(2)}, u32[]{:S(2)}) collective-permute-start(bf16[768,256]{1,0:T(8,128)(2,1)S(1)} %shard_map.104), channel_id=1, source_target_pairs={{0,8},{2,10},{4,12},{6,14},{8,16},{10,18},{12,20},{14,22},{16,24},... | collective-permute-start | bytes 1179656 | tf_op jit(solution)/shard_map/ppermute | solution.py:499
  18.7 14.3 %collective-permute-start.7 = (bf16[816,256]{1,0:T(8,128)(2,1)S(1)}, bf16[816,256]{1,0:T(8,128)(2,1)S(1)}, u32[]{:S(2)}, u32[]{:S(2)}) collective-permute-start(bf16[816,256]{1,0:T(8,128)(2,1)S(1)} %shard_map.110), channel_id=1, source_target_pairs={{8,0},{10,2},{12,4},{14,6},{16,8},{18,10},{20,12},{22,14},{24,16},... | collective-permute-start | bytes 1253384 | tf_op jit(solution)/shard_map/ppermute | solution.py:499
  25.4 7.5 %collective-permute-start.8 = (f32[2,8,256]{2,1,0:T(8,128)S(1)}, f32[2,8,256]{2,1,0:T(8,128)S(1)}, u32[]{:S(2)}, u32[]{:S(2)}) collective-permute-start(f32[2,8,256]{2,1,0:T(8,128)S(1)} %get-tuple-element.65.refs_1_), channel_id=1, source_target_pairs={{0,24},{2,26},{4,28},{6,30},{8,0},{10,2},{12,4},{14,6},{16,8},{18,... | collective-permute-start | bytes 49160 | tf_op jit(solution)/shard_map/ppermute | solution.py:566
  35.5 21.7 %collective-permute-start.9 = (bf16[384,256]{1,0:T(8,128)(2,1)S(1)}, bf16[384,256]{1,0:T(8,128)(2,1)S(1)}, u32[]{:S(2)}, u32[]{:S(2)}) collective-permute-start(bf16[384,256]{1,0:T(8,128)(2,1)S(1)} %get-tuple-element.81), channel_id=1, source_target_pairs={{0,2},{2,0},{4,6},{6,4},{8,10},{10,8},{12,14},{14,12},{16,18},{18,... | collective-permute-start | bytes 589832 | tf_op jit(solution)/shard_map/ppermute | solution.py:496
  37.0 20.2 %collective-permute-start.10 = (bf16[384,256]{1,0:T(8,128)(2,1)S(1)}, bf16[384,256]{1,0:T(8,128)(2,1)S(1)}, u32[]{:S(2)}, u32[]{:S(2)}) collective-permute-start(bf16[384,256]{1,0:T(8,128)(2,1)S(1)} %get-tuple-element.82), channel_id=1, source_target_pairs={{0,4},{2,6},{4,0},{6,2},{8,12},{10,14},{12,8},{14,10},{16,20},{18,... | collective-permute-start | bytes 589832 | tf_op jit(solution)/shard_map/ppermute | solution.py:496
  37.5 19.7 %collective-permute-start.11 = (bf16[384,256]{1,0:T(8,128)(2,1)S(1)}, bf16[384,256]{1,0:T(8,128)(2,1)S(1)}, u32[]{:S(2)}, u32[]{:S(2)}) collective-permute-start(bf16[384,256]{1,0:T(8,128)(2,1)S(1)} %get-tuple-element.83), channel_id=1, source_target_pairs={{0,6},{2,4},{4,2},{6,0},{8,14},{10,12},{12,10},{14,8},{16,22},{18,... | collective-permute-start | bytes 589832 | tf_op jit(solution)/shard_map/ppermute | solution.py:496
  39.0 3.6 %collective-permute-start.12 = (f32[8,128]{1,0:T(8,128)S(1)}, f32[8,128]{1,0:T(8,128)S(1)}, u32[]{:S(2)}, u32[]{:S(2)}) collective-permute-start(f32[8,128]{1,0:T(8,128)S(1)} %get-tuple-element.87.refs_0_), channel_id=1, source_target_pairs={{0,8},{2,10},{4,12},{6,14},{8,0},{10,2},{12,4},{14,6},{16,24},{18,... | collective-permute-start | bytes 12296 | tf_op jit(solution)/shard_map/ppermute | solution.py:496
  42.6 4.5 %collective-permute-start.13 = (f32[8,128]{1,0:T(8,128)S(1)}, f32[8,128]{1,0:T(8,128)S(1)}, u32[]{:S(2)}, u32[]{:S(2)}) collective-permute-start(f32[8,128]{1,0:T(8,128)S(1)} %shard_map.115.refs_0_), channel_id=1, source_target_pairs={{0,16},{2,18},{4,20},{6,22},{8,24},{10,26},{12,28},{14,30},{16,0},... | collective-permute-start | bytes 12296 | tf_op jit(solution)/shard_map/ppermute | solution.py:496
  47.1 4.5 %collective-permute-start.16 = (f32[8,128]{1,0:T(8,128)S(1)}, f32[8,128]{1,0:T(8,128)S(1)}, u32[]{:S(2)}, u32[]{:S(2)}) collective-permute-start(f32[8,128]{1,0:T(8,128)S(1)} %shard_map.116.refs_0_), channel_id=1, source_target_pairs={{0,6},{2,4},{4,2},{6,0},{8,14},{10,12},{12,10},{14,8},{16,22},{18,... | collective-permute-start | bytes 12296 | tf_op jit(solution)/shard_map/ppermute | solution.py:496
  48.5 4.6 %collective-permute-start.15 = (f32[8,128]{1,0:T(8,128)S(1)}, f32[8,128]{1,0:T(8,128)S(1)}, u32[]{:S(2)}, u32[]{:S(2)}) collective-permute-start(f32[8,128]{1,0:T(8,128)S(1)} %shard_map.116.refs_0_), channel_id=1, source_target_pairs={{0,4},{2,6},{4,0},{6,2},{8,12},{10,14},{12,8},{14,10},{16,20},{18,... | collective-permute-start | bytes 12296 | tf_op jit(solution)/shard_map/ppermute | solution.py:496
  51.6 3.6 %collective-permute-start.14 = (f32[8,128]{1,0:T(8,128)S(1)}, f32[8,128]{1,0:T(8,128)S(1)}, u32[]{:S(2)}, u32[]{:S(2)}) collective-permute-start(f32[8,128]{1,0:T(8,128)S(1)} %shard_map.116.refs_0_), channel_id=1, source_target_pairs={{0,2},{2,0},{4,6},{6,4},{8,10},{10,8},{12,14},{14,12},{16,18},{18,... | collective-permute-start | bytes 12296 | tf_op jit(solution)/shard_map/ppermute | solution.py:496
  55.3 1.2 %collective-permute-start.17 = (f32[32,128]{1,0:T(8,128)S(1)}, f32[32,128]{1,0:T(8,128)S(1)}, u32[]{:S(2)}, u32[]{:S(2)}) collective-permute-start(f32[32,128]{1,0:T(8,128)S(1)} %shard_map.117.refs_0_), channel_id=1, source_target_pairs={{0,1},{1,0},{2,3},{3,2},{4,5},{5,4},{6,7},{7,6},{8,9},{9,8},{10,11... | collective-permute-start | bytes 49160 | tf_op jit(solution)/shard_map/ppermute | solution.py:496
